TPU v7x, 256 devices: a whole 4x4x8 slice. The times are simulated.
256 devices in a mesh: seq: 64 (over z, x, core), mp: 4 (over y).
Axes of the slice: x: 4, y: 4, z: 8, core: 2. Of those that a mesh axis runs over, the one named last changes fastest.
Arguments:
- branch_in: bfloat16 [32768, 4096], P('seq', 'mp'), may hold values from -48 to 48
- branch_gate: bfloat16 [32768, 4096], P('seq', 'mp'), may hold values from -6 to 6
- conv_taps: float32 [4, 4096], P(None, 'mp'), may hold values from -3 to 3
- conv_shift: float32 [4096], P('mp'), may hold values from -3 to 3
- inflow_weight: bfloat16 [16, 256, 256], P('mp'), may hold values from -0.375 to 0.375
- inflow_bias: float32 [4096], P('mp'), may hold values from -4 to 4
- decay_weight: bfloat16 [16, 256, 256], P('mp'), may hold values from -0.375 to 0.375
- decay_bias: float32 [4096], P('mp'), may hold values from -12 to -1.5
- decay_param: float32 [4096], P('mp'), may hold values from 3 to 4
- stream: bfloat16 [32768, 4096], P('seq', 'mp'), may hold values from -48 to 48
- norm_gain: float32 [4096], P('mp'), may hold values from 0.5 to 1.5
- memory_weight: bfloat16 [4096, 512], P('mp'), may hold values from -1 to 1
- queries: bfloat16 [32768, 4096], P('seq', 'mp'), may hold values from -128 to 128
Outputs:
- recurrent_out: bfloat16 [32768, 4096], P('seq', 'mp')
- attended: bfloat16 [32768, 4096], P('seq', 'mp')
All inputs are finite; a program needn't handle non-finite values.
Results may differ from a plain program's by a relative error of at most 0.0071.
Values may be sent and summed in bfloat16 or wider, within the bound.
No kernel may reach another device: no remote copies, remote signals or barrier semaphores. Data moves between devices by JAX's collectives and lax.ppermute only.
A program may use at most 128 MiB of HBM per device.

v0:
```python
import jax
import jax.numpy as jnp
from jax import lax
from jax.sharding import Mesh
from jax.sharding import PartitionSpec as P

D = 4096
HD = 256
CONV = 4
WINDOW = 2048
BLK = 256
SEQ = ("seq_0", "seq_1", "seq_2")


decay_power = 8.0
norm_epsilon = 1e-06
masked_score = -1e30


def from_behind(value, axis, steps):
    count = lax.axis_size(axis)
    leading, last = (max(0, -steps), min(count, count - steps))
    return lax.ppermute(value, axis, [(source, source + steps) for source in range(leading, last)])


def filled_with(x, identity):
    return jax.tree.map(
        lambda part, zero: jnp.zeros_like(part) + jnp.asarray(zero, part.dtype), x, identity
    )


def gathered_once(x, axis):
    leaves = jax.tree.leaves(x)
    turns = sorted(range(len(leaves)), key=lambda k: -leaves[k].size)
    width = (1, *leaves[turns[0]].shape)[-1]
    lines = [
        jnp.pad(leaves[k].reshape(-1), (0, -leaves[k].size % width)).reshape(-1, width)
        for k in turns
    ]
    both, at, found = (lax.all_gather(jnp.concatenate(lines), axis), 0, {})
    for k, line in zip(turns, lines):
        piece = both[:, at : at + len(line)].reshape(len(both), -1)
        found[k] = piece[:, : leaves[k].size].reshape(-1, *leaves[k].shape)
        at += len(line)
    numbers = iter(range(len(leaves)))
    return jax.tree.map(lambda _: found[next(numbers)], x)


def entering(x, axes, combine, identity):
    before = start = filled_with(x, identity)
    subtotal = x
    for axis in reversed(axes):
        count, position = (lax.axis_size(axis), lax.axis_index(axis))
        pieces = gathered_once(subtotal, axis)
        inside, subtotal = (start, start)
        for k in range(count):
            passed = k < position
            subtotal = combine(subtotal, jax.tree.map(lambda part: part[k], pieces))
            inside = jax.tree.map(lambda new, old: jnp.where(passed, new, old), subtotal, inside)
        before = combine(inside, before)
    return before


def packed_total(arrays, axis):
    ravelled, at, outs = (jnp.concatenate([a.reshape(-1) for a in arrays]), 0, [])
    subtotal = lax.psum(ravelled, axis)
    for a in arrays:
        outs.append(subtotal[at : at + a.size].reshape(a.shape))
        at += a.size
    return tuple(outs)


def compose(earlier, later):
    return (earlier[0] * later[0], later[0] * earlier[1] + later[1])


def attend_block(query_block, window_block, query_start, key_start, head_count):
    token_rows = query_block.shape[0]
    key_count = window_block.shape[0]
    grouped = query_block.reshape(token_rows, head_count, HD)
    key_rows = window_block[:, :HD]
    value_rows = window_block[:, HD:]
    scores = jnp.einsum(
        "qhd,kd->hqk", grouped, key_rows, preferred_element_type=jnp.float32
    ) * HD ** (-0.5)
    query_pos = query_start + jnp.arange(token_rows, dtype=jnp.int32)
    key_pos = key_start + jnp.arange(key_count, dtype=jnp.int32)
    distance = query_pos[:, None] - key_pos[None, :]
    allowed = (distance >= 0) & (distance < WINDOW) & (key_pos[None, :] >= 0)
    scores = jnp.where(allowed[None], scores, masked_score)
    row_peak = jnp.max(scores, axis=2, keepdims=True)
    weights = jnp.exp(scores - row_peak)
    softmax_probs = (weights / jnp.sum(weights, axis=2, keepdims=True)).astype(jnp.bfloat16)
    output = jnp.einsum(
        "hqk,kd->qhd", softmax_probs, value_rows, preferred_element_type=jnp.float32
    )
    return output.reshape(token_rows, head_count * HD).astype(jnp.bfloat16)


def shards(
    branch_in,
    branch_gate,
    conv_taps,
    conv_shift,
    inflow_weight,
    inflow_bias,
    decay_weight,
    decay_bias,
    decay_param,
    stream,
    norm_gain,
    memory_weight,
    queries,
):
    token_rows = branch_in.shape[0]
    channels = branch_in.shape[1]
    position = lax.axis_index(SEQ)
    edge_rows = from_behind(branch_in[token_rows - (CONV - 1) :], SEQ, 1)
    extended = jnp.concatenate([edge_rows, branch_in], axis=0).astype(jnp.float32)
    totals = conv_shift[None, :] + conv_taps[0][None, :] * extended[CONV - 1 :]
    for offset in range(1, CONV):
        totals = (
            totals
            + conv_taps[offset][None, :]
            * extended[CONV - 1 - offset : CONV - 1 - offset + token_rows]
        )
    mixed_conv = totals.astype(jnp.bfloat16)
    groups = inflow_weight.shape[0]
    grouped = mixed_conv.reshape(token_rows, groups, BLK)
    inflow = jax.nn.sigmoid(
        jnp.einsum(
            "tnb,nbc->tnc", grouped, inflow_weight, preferred_element_type=jnp.float32
        ).reshape(token_rows, channels)
        + inflow_bias[None, :]
    )
    recurrence = jax.nn.sigmoid(
        jnp.einsum(
            "tnb,nbc->tnc", grouped, decay_weight, preferred_element_type=jnp.float32
        ).reshape(token_rows, channels)
        + decay_bias[None, :]
    )
    log_decay = -decay_power * recurrence * jax.nn.softplus(-decay_param)[None, :]
    factor = jnp.exp(log_decay)
    pushed = jnp.sqrt(-jnp.expm1(2.0 * log_decay)) * inflow * mixed_conv.astype(jnp.float32)
    running_factor, running_state = lax.associative_scan(compose, (factor, pushed), axis=0)
    final_couple = (running_factor[token_rows - 1], running_state[token_rows - 1])
    start_state = jnp.zeros((channels,), jnp.float32)
    incoming = entering(
        final_couple, SEQ, compose, (jnp.ones((channels,), jnp.float32), start_state)
    )[1]
    states = running_state + running_factor * incoming[None, :]
    recurrent_out = (
        states * jax.nn.gelu(branch_gate.astype(jnp.float32), approximate=True)
    ).astype(jnp.bfloat16)
    stream_float = stream.astype(jnp.float32)
    partial_squares = jnp.sum(jnp.square(stream_float), axis=1)
    scaled = (stream_float * norm_gain[None, :]).astype(jnp.bfloat16)
    partial_memory = jnp.dot(scaled, memory_weight, preferred_element_type=jnp.float32)
    summed_memory, summed_squares = packed_total((partial_memory, partial_squares), "mp")
    memory = (summed_memory / jnp.sqrt(summed_squares / D + norm_epsilon)[:, None]).astype(
        jnp.bfloat16
    )
    shards_back = WINDOW // token_rows
    held = memory
    held_count = 1
    while held_count < shards_back + 1:
        wanted = min(held_count, shards_back + 1 - held_count)
        arrived = from_behind(held[held.shape[0] - wanted * token_rows :], SEQ, held_count)
        held = jnp.concatenate([arrived, held], axis=0)
        held_count = held_count + wanted
    query_start = position * token_rows
    attended = attend_block(
        queries, held, query_start, query_start - shards_back * token_rows, queries.shape[1] // HD
    )
    return (recurrent_out, attended)


def solution(mesh):
    finer = Mesh(mesh.devices.reshape(8, 4, 2, mesh.shape["mp"]), ("seq_0", "seq_1", "seq_2", "mp"))
    in_specs = (
        P(SEQ, "mp"),
        P(SEQ, "mp"),
        P(None, "mp"),
        P("mp"),
        P("mp", None, None),
        P("mp"),
        P("mp", None, None),
        P("mp"),
        P("mp"),
        P(SEQ, "mp"),
        P("mp"),
        P("mp", None),
        P(SEQ, "mp"),
    )
    out_specs = (P(SEQ, "mp"), P(SEQ, "mp"))
    return jax.shard_map(
        shards, mesh=finer, in_specs=in_specs, out_specs=out_specs, check_vma=False
    )
```

profile of v0, /device:TPU:50, one launch (start us, length us, event | category | flops | bytes accessed | tf_op | source)
XLA Modules:
  0.0 242.1 jit_solution(14254350156096811092)
XLA Ops:
  8.0 1.9 collective-permute-start
  9.9 1.5 fusion.9
  11.5 1.9 convolution_bitcast_fusion
  13.7 1.0 pad_maximum_fusion.1
  14.9 3.1 %fusion.7 = pred[512,2560]{0,1:T(8,128)(4,1)} fusion(s32[2560]{0:T(1024)S(1)} %iota_add_fusion, s32[512]{0:T(512)S(1)} %iota_add_fusion.1, pred[2560]{0:T(1024)(128)(4,1)S(1)} %broadcast_compare_fusion), kind=kLoop, calls=%fused_computation.12 | loop fusion | flops 6553600 | bytes 1325568 | tf_op jit(solution)/shard_map/and | solution.py:89
  18.3 1.0 fusion.18
  19.4 1.8 fusion.33
  21.2 2.9 %copy.30 = f32[512,1024]{1,0:T(8,128)} copy(f32[512,1024]{0,1:T(8,128)} %bitcast.140) | data formatting | bytes 4194304 | tf_op jit(solution)/shard_map/reshape | solution.py:133
  24.1 2.9 %fusion.35 = f32[4,512,256]{1,2,0:T(8,128)} fusion(bf16[4,256,256]{2,1,0:T(8,128)(2,1)} %param.19, bf16[64,4,8,256]{3,2,1,0:T(8,128)(2,1)S(1)} %bitcast.138), kind=kOutput, calls=%fused_computation.52 | convolution fusion | flops 268435456 | bytes 3670016 | tf_op jit(solution)/shard_map/tnb,nbc->tnc/dot_general | solution.py:137
  27.0 2.9 %copy.27 = f32[512,1024]{1,0:T(8,128)} copy(f32[512,1024]{0,1:T(8,128)} %bitcast.139) | data formatting | bytes 4194304 | tf_op jit(solution)/shard_map/reshape | solution.py:139
  29.9 5.7 %convert_multiply_fusion.5 = (f32[512,1024]{1,0:T(8,128)S(1)}, f32[512,1024]{1,0:T(8,128)}) fusion(f32[512,1024]{1,0:T(8,128)} %copy.30, f32[1024]{0:T(1024)S(1)} %copy-done.19, f32[1024]{0:T(1024)S(1)} %fusion.56, f32[512,1024]{1,0:T(8,128)} %copy.27, f32[1024]{0:T(1024)S(1)} %copy-done.20, f32[515,1024]{1,0:T(8,128)S(1)} %maximum_convert_fusion, ...), kind=kLoop, calls=%fused_computation.38 | loop fusion | flops 12058624 | bytes 16809984 | tf_op jit(solution)/shard_map/mul | solution.py:144
  35.6 1.3 copy-done.3
  37.0 5.5 %slice.536 = f32[255,1024]{1,0:T(8,128)} slice(f32[512,1024]{1,0:T(8,128)} %copy-done.3), slice={[2:512:2], [0:1024:1]} | slice | bytes 2088960 | tf_op jit(solution)/shard_map/slice | solution.py:145
  42.5 5.6 %slice.474 = f32[256,1024]{1,0:T(8,128)} slice(f32[512,1024]{1,0:T(8,128)} %copy-done.3), slice={[1:512:2], [0:1024:1]} | slice | bytes 2097152 | tf_op jit(solution)/shard_map/slice | solution.py:145
  48.0 5.4 %slice.473 = f32[256,1024]{1,0:T(8,128)} slice(f32[512,1024]{1,0:T(8,128)} %copy-done.3), slice={[0:511:2], [0:1024:1]} | slice | bytes 2097152 | tf_op jit(solution)/shard_map/slice | solution.py:145
  53.4 2.8 %slice.476 = f32[256,1024]{1,0:T(8,128)} slice(f32[512,1024]{1,0:T(8,128)S(1)} %copy-done.2), slice={[0:511:2], [0:1024:1]} | slice | bytes 2097152 | tf_op jit(solution)/shard_map/slice | solution.py:145
  56.3 2.8 %slice.472 = f32[256,1024]{1,0:T(8,128)} slice(f32[512,1024]{1,0:T(8,128)S(1)} %copy-done.2), slice={[1:512:2], [0:1024:1]} | slice | bytes 2097152 | tf_op jit(solution)/shard_map/slice | solution.py:145
  59.1 2.9 %slice.471 = f32[255,1024]{1,0:T(8,128)} slice(f32[512,1024]{1,0:T(8,128)S(1)} %copy-done.2), slice={[2:512:2], [0:1024:1]} | slice | bytes 2088960 | tf_op jit(solution)/shard_map/slice | solution.py:145
  62.0 2.7 %multiply_add_fusion = (f32[256,1024]{1,0:T(8,128)S(1)}, f32[256,1024]{1,0:T(8,128)S(1)}) fusion(f32[256,1024]{1,0:T(8,128)} %slice.474, f32[256,1024]{1,0:T(8,128)} %slice.472, f32[256,1024]{1,0:T(8,128)} %slice.473, f32[256,1024]{1,0:T(8,128)} %slice.476), kind=kLoop, calls=%fused_computation.62 | loop fusion | flops 786432 | bytes 6291456 | tf_op jit(solution)/shard_map/add | solution.py:74
  64.8 1.5 slice.534
  67.4 1.5 slice.477
  73.0 0.9 add.475
  73.9 0.9 add.464
  74.8 1.1 fusion.45
  77.1 2.1 pad.125
  79.2 4.6 %pad.143 = f32[256,1024]{1,0:T(8,128)} pad(f32[128,1024]{1,0:T(8,128)} %add.475, f32[]{:T(128)} %constant.30.clone.1), padding=1_0_1x0_0_0 | pad | bytes 1572868 | tf_op jit(solution)/shard_map/pad | solution.py:145
  83.9 2.4 add.476
  86.3 1.1 add.466
  88.5 1.7 fusion.37
  90.6 1.4 pad_maximum_fusion.2
  92.0 4.9 %pad.126 = f32[512,1024]{1,0:T(8,128)} pad(f32[256,1024]{1,0:T(8,128)S(1)} %pad_maximum_fusion.2, f32[]{:T(128)} %constant.30.clone.1), padding=0_1_1x0_0_0 | pad | bytes 3145732 | tf_op jit(solution)/shard_map/pad | solution.py:145
  96.8 8.6 %pad.127 = f32[512,1024]{1,0:T(8,128)} pad(f32[256,1024]{1,0:T(8,128)} %add.466, f32[]{:T(128)} %constant.30.clone.1), padding=1_0_1x0_0_0 | pad | bytes 3145732 | tf_op jit(solution)/shard_map/pad | solution.py:145
  105.4 4.9 %pad.145 = f32[512,1024]{1,0:T(8,128)} pad(f32[256,1024]{1,0:T(8,128)S(1)} %copy-done.6, f32[]{:T(128)} %constant.30.clone.1), padding=1_0_1x0_0_0 | pad | bytes 3145732 | tf_op jit(solution)/shard_map/pad | solution.py:145
  111.9 3.2 %all-gather.3 = f32[2,2,1024]{2,1,0:T(2,128)S(1)} all-gather(f32[1,2,1024]{2,1,0:T(2,128)S(1)} %maximum_bitcast_fusion), channel_id=2, replica_groups=mesh['seq_0'=8,'seq_1'=4,'seq_2'=2,'mp'=4] {'seq_2'}, dimensions={0}, use_global_device_ids=true | all-gather | bytes 24576 | tf_op jit(solution)/shard_map/all_gather | solution.py:40
  115.1 12.2 %all-gather.4 = f32[4,2,1024]{2,1,0:T(2,128)S(1)} all-gather(f32[1,2,1024]{2,1,0:T(2,128)S(1)} %maximum_bitcast_fusion.1), channel_id=3, replica_groups=mesh['seq_0'=8,'seq_1'=4,'seq_2'=2,'mp'=4] {'seq_1'}, dimensions={0}, use_global_device_ids=true | all-gather | bytes 40960 | tf_op jit(solution)/shard_map/all_gather | solution.py:40
  127.4 1.2 slice-done
  128.6 1.1 slice.585
  130.6 1.5 divide_convert_fusion.4
  132.0 1.9 collective-permute-start.2
  134.0 26.4 %all-gather.5 = f32[8,2,1024]{2,1,0:T(2,128)S(1)} all-gather(f32[1,2,1024]{2,1,0:T(2,128)S(1)} %maximum_bitcast_fusion.2), channel_id=4, replica_groups=mesh['seq_0'=8,'seq_1'=4,'seq_2'=2,'mp'=4] {'seq_0'}, dimensions={0}, use_global_device_ids=true | all-gather | bytes 73728 | tf_op jit(solution)/shard_map/all_gather | solution.py:40
  160.5 2.4 collective-permute-start.3
  163.0 5.0 %collective-permute-start.1 = (bf16[512,512]{1,0:T(8,128)(2,1)S(1)}, bf16[512,512]{1,0:T(8,128)(2,1)S(1)}, u32[]{:S(2)}, u32[]{:S(2)}) collective-permute-start(bf16[512,512]{1,0:T(8,128)(2,1)S(1)} %divide_convert_fusion.4), channel_id=1, source_target_pairs={{0,16},{4,20},{8,24},{12,28},{16,32},{20,36},{24,40},{28,44},{32,4... | collective-permute-start | bytes 1572872 | tf_op jit(solution)/shard_map/ppermute | solution.py:23
  168.1 4.4 %fusion.16 = bf16[512,1024]{1,0:T(8,128)(2,1)} fusion(bf16[512,1024]{1,0:T(8,128)(2,1)S(1)} %copy-done.14, f32[512,1024]{1,0:T(8,128)S(1)} %pad.144, f32[512,1024]{1,0:T(8,128)} %pad.145, f32[512,1024]{1,0:T(8,128)S(1)} %copy-done.5, f32[512,1024]{1,0:T(8,128)} %pad.127, f32[1024]{0:T(1024)S(1)} %add_add_fusion), kind=kLoop, calls=%fused_computation.28 | loop fusion | flops 7864320 | bytes 10489856 | tf_op jit(solution)/shard_map/convert_element_type | solution.py:154
  172.5 37.0 %collective-permute-done.1 = bf16[512,512]{1,0:T(8,128)(2,1)S(1)} collective-permute-done((bf16[512,512]{1,0:T(8,128)(2,1)S(1)}, bf16[512,512]{1,0:T(8,128)(2,1)S(1)}, u32[]{:S(2)}, u32[]{:S(2)}) %collective-permute-start.1) | collective-permute-done | bytes 524320 | tf_op jit(solution)/shard_map/ppermute | solution.py:23
  209.5 1.6 pad_maximum_fusion
  211.1 12.5 %fusion.69 = (f32[4,512]{1,0:T(4,128)S(1)}, f32[4,512,2560]{1,2,0:T(8,128)}) fusion(pred[512,2560]{0,1:T(8,128)(4,1)S(1)} %copy-done.12, bf16[2560,512]{1,0:T(8,128)(2,1)} %pad_maximum_fusion, bf16[64,4,8,256]{3,2,1,0:T(8,128)(2,1)S(1)} %bitcast.165), kind=kOutput, calls=%fused_computation.179 | convolution fusion | flops 2705328640 | bytes 24649728 | tf_op jit(solution)/shard_map/sub | solution.py:92
  223.6 10.3 %fusion.24 = bf16[256,4,512]{2,0,1:T(8,128)(2,1)S(1)} fusion(f32[4,512,2560]{1,2,0:T(8,128)} %get-tuple-element.69, f32[4,512]{1,0:T(4,128)S(1)} %get-tuple-element.68, bf16[2560,512]{1,0:T(8,128)(2,1)} %pad_maximum_fusion), kind=kOutput, calls=%fused_computation.41 | convolution fusion | flops 2695364608 | bytes 23339008 | tf_op jit(solution)/shard_map/hqk,kd->qhd/dot_general | solution.py:94
  233.9 1.3 copy.34
  (190 shorter events, 11.5 us)
Async XLA Ops:
  7.2 4.3 %copy-start = (bf16[1024,512]{1,0:T(8,128)(2,1)S(1)}, bf16[1024,512]{1,0:T(8,128)(2,1)}, u32[]{:S(2)}) copy-start(bf16[1024,512]{1,0:T(8,128)(2,1)} %param.24) | copy-start | bytes 3145732
  7.2 120.2 %all-reduce.38.cloned.1.call-start = ((), (), s32[]{:S(2)}) async-start(), calls=%async_computation | async-start | bytes 2105344 | tf_op jit(solution)/shard_map/psum | solution.py:66
  8.0 9.9 %collective-permute-start = (bf16[3,1024]{1,0:T(4,128)(2,1)S(1)}, bf16[3,1024]{1,0:T(4,128)(2,1)S(1)}, u32[]{:S(2)}, u32[]{:S(2)}) collective-permute-start(bf16[3,1024]{1,0:T(4,128)(2,1)S(1)} %slice.462), channel_id=1, source_target_pairs={{0,4},{4,8},{8,12},{12,16},{16,20},{20,24},{24,28},{28,32},{32,36}... | collective-permute-start | bytes 18440 | tf_op jit(solution)/shard_map/ppermute | solution.py:23
  13.7 1.2 copy-start.16
  13.7 4.2 %copy-start.18 = (f32[1024]{0:T(1024)S(1)}, f32[1024]{0:T(1024)}, u32[]{:S(2)}) copy-start(f32[1024]{0:T(1024)} %param.21) | copy-start | bytes 12292
  14.7 3.2 %copy-start.13 = (bf16[512,1024]{1,0:T(8,128)(2,1)S(1)}, bf16[512,1024]{1,0:T(8,128)(2,1)}, u32[]{:S(2)}) copy-start(bf16[512,1024]{1,0:T(8,128)(2,1)} %param.13) | copy-start | bytes 3145732
  14.9 3.5 %copy-start.17 = (f32[1024]{0:T(1024)S(1)}, f32[1024]{0:T(1024)}, u32[]{:S(2)}) copy-start(f32[1024]{0:T(1024)} %param.16) | copy-start | bytes 12292
  18.3 1.0 copy-start.15
  27.0 2.9 %copy-start.19 = (f32[1024]{0:T(1024)S(1)}, f32[1024]{0:T(1024)}, u32[]{:S(2)}) copy-start(f32[1024]{0:T(1024)} %param.18) | copy-start | bytes 12292
  27.0 2.9 %copy-start.20 = (f32[1024]{0:T(1024)S(1)}, f32[1024]{0:T(1024)}, u32[]{:S(2)}) copy-start(f32[1024]{0:T(1024)} %param.20) | copy-start | bytes 12292
  35.6 1.3 copy-start.3
  42.5 10.9 %copy-start.2 = (f32[512,1024]{1,0:T(8,128)S(1)}, f32[512,1024]{1,0:T(8,128)}, u32[]{:S(2)}) copy-start(f32[512,1024]{1,0:T(8,128)} %get-tuple-element.9) | copy-start | bytes 6291460
  72.9 1.9 copy-start.9
  73.0 1.9 copy-start.10
  75.9 1.0 copy-start.11
  86.3 1.6 copy-start.4
  86.3 1.9 copy-start.7
  86.3 2.2 copy-start.8
  96.8 8.6 %copy-start.6 = (f32[256,1024]{1,0:T(8,128)S(1)}, f32[256,1024]{1,0:T(8,128)}, u32[]{:S(2)}) copy-start(f32[256,1024]{1,0:T(8,128)} %add.476) | copy-start | bytes 3145732
  127.4 1.2 slice-start
  129.7 38.3 %copy-start.5 = (f32[512,1024]{1,0:T(8,128)S(1)}, f32[512,1024]{1,0:T(8,128)}, u32[]{:S(2)}) copy-start(f32[512,1024]{1,0:T(8,128)} %pad.126) | copy-start | bytes 6291460
  129.7 38.3 %copy-start.14 = (bf16[512,1024]{1,0:T(8,128)(2,1)S(1)}, bf16[512,1024]{1,0:T(8,128)(2,1)}, u32[]{:S(2)}) copy-start(bf16[512,1024]{1,0:T(8,128)(2,1)} %param.14) | copy-start | bytes 3145732
  132.0 28.4 %collective-permute-start.2 = (bf16[512,512]{1,0:T(8,128)(2,1)S(1)}, bf16[512,512]{1,0:T(8,128)(2,1)S(1)}, u32[]{:S(2)}, u32[]{:S(2)}) collective-permute-start(bf16[512,512]{1,0:T(8,128)(2,1)S(1)} %divide_convert_fusion.4), channel_id=1, source_target_pairs={{0,4},{4,8},{8,12},{12,16},{16,20},{20,24},{24,28},{28,32},{32,36}... | collective-permute-start | bytes 1572872 | tf_op jit(solution)/shard_map/ppermute | solution.py:23
  160.5 49.0 %collective-permute-start.3 = (bf16[1024,512]{1,0:T(8,128)(2,1)S(1)}, bf16[1024,512]{1,0:T(8,128)(2,1)S(1)}, u32[]{:S(2)}, u32[]{:S(2)}) collective-permute-start(bf16[1024,512]{1,0:T(8,128)(2,1)S(1)} %pad_maximum_fusion.4), channel_id=1, source_target_pairs={{0,8},{4,12},{8,16},{12,20},{16,24},{20,28},{24,32},{28,36},{32,40... | collective-permute-start | bytes 3145736 | tf_op jit(solution)/shard_map/ppermute | solution.py:23
  163.0 46.5 %collective-permute-start.1 = (bf16[512,512]{1,0:T(8,128)(2,1)S(1)}, bf16[512,512]{1,0:T(8,128)(2,1)S(1)}, u32[]{:S(2)}, u32[]{:S(2)}) collective-permute-start(bf16[512,512]{1,0:T(8,128)(2,1)S(1)} %divide_convert_fusion.4), channel_id=1, source_target_pairs={{0,16},{4,20},{8,24},{12,28},{16,32},{20,36},{24,40},{28,44},{32,4... | collective-permute-start | bytes 1572872 | tf_op jit(solution)/shard_map/ppermute | solution.py:23
  172.5 38.6 %copy-start.12 = (pred[512,2560]{0,1:T(8,128)(4,1)S(1)}, pred[512,2560]{0,1:T(8,128)(4,1)}, u32[]{:S(2)}) copy-start(pred[512,2560]{0,1:T(8,128)(4,1)} %fusion.7) | copy-start | bytes 3932164
  172.5 38.6 %copy-start.21 = (bf16[512,1024]{1,0:T(8,128)(2,1)S(1)}, bf16[512,1024]{1,0:T(8,128)(2,1)}, u32[]{:S(2)}) copy-start(bf16[512,1024]{1,0:T(8,128)(2,1)} %param.25) | copy-start | bytes 3145732
  223.6 11.7 %copy-start.1 = (bf16[1024,512]{1,0:T(8,128)(2,1)S(1)}, bf16[1024,512]{1,0:T(8,128)(2,1)}, u32[]{:S(2)}) copy-start(bf16[1024,512]{1,0:T(8,128)(2,1)} %param.24) | copy-start | bytes 3145732
Sparse Core Ops, SparseCore 0:
  14.9 53.6 all-reduce.37
where the time goes:
time: 243 us; the launch traced here: 242 us
  local copies, waits for them, and re-layouts  71.4 us (29%)
  blocking collectives  41.8 us (17%)
  waiting for transfers between devices  37.1 us (15%)
  other arithmetic  36 us (15%)
  matrix products  29.4 us (12%)
  between operations  15.1 us (6%)
  starting transfers between devices  11.3 us (5%)
    all_gather x3, blocking collectives, gathered_once(): both, at, found = (lax.all_gather(jnp.concatenate(lines), axis), 0, {})  41.8 us
    ppermute x4, waiting for transfers between devices, from_behind(): lax.ppermute(value, axis, [(source, source + steps) for source in range(l...  37 us
    slice x60, local copies, waits for them, and re-layouts, shards(): lax.associative_scan(compose, (factor, pushed), axis=0)  31.1 us
    pad x32, local copies, waits for them, and re-layouts, shards(): lax.associative_scan(compose, (factor, pushed), axis=0)  26.4 us
    sub x1, matrix products, attend_block(): weights = jnp.exp(scores - row_peak)  12.5 us
    ppermute x4, starting transfers between devices, from_behind(): lax.ppermute(value, axis, [(source, source + steps) for source in range(l...  11.3 us
    dot_general x1, matrix products, attend_block(): jnp.einsum('hqk,kd->qhd', softmax_probs, value_rows, preferred_element_ty...  10.3 us
    add x17, other arithmetic, shards(): lax.associative_scan(compose, (factor, pushed), axis=0)  7 us
  transfers between devices with their start and end apart: 5, of which 1 were waited for; matrix products, arithmetic and copies ran while one was open for 42% of the time, Pallas kernels for 0%

commit v1 on v0

v1 whole, which is shorter than its diff:
```python
import functools

import jax
import jax.numpy as jnp
from jax import lax
from jax.experimental import pallas as pl
from jax.experimental.pallas import tpu as pltpu
from jax.sharding import Mesh
from jax.sharding import PartitionSpec as P

D = 4096
HD = 256
CONV = 4
WINDOW = 2048
BLK = 256
SEQ = ("seq_0", "seq_1", "seq_2")
CORE = "seq_2"
TOK = 512
QUARTER = 128
PARTS = 4
SEGMENTS = 8
STEPS = TOK // SEGMENTS
QROWS = 256
LANES = 128

decay_power = 8.0
norm_epsilon = 1e-06
masked_score = -1e30
F32 = jnp.float32
BF16 = jnp.bfloat16
SMEM = pl.BlockSpec(memory_space=pltpu.SMEM)


def whole(shape):
    return pl.BlockSpec(shape, lambda *_: (0,) * len(shape))


def shifted(value, steps):
    count = lax.axis_size(SEQ)
    return lax.ppermute(value, SEQ, [(k, k + steps) for k in range(count - steps)])


def turned(value, steps):
    return lax.ppermute(value, "mp", [(k, (k + steps) % PARTS) for k in range(PARTS)])


def swapped(value):
    return lax.ppermute(value, CORE, [(0, 1), (1, 0)])


def project_kernel(place, stream, gain, weight, *parts):
    for k, part in enumerate(parts):
        start = pl.multiple_of(lax.rem(place[0] + k, PARTS) * QUARTER, QUARTER)
        x = stream[pl.ds(start, QUARTER), :].astype(F32)
        squares = jnp.sum(x * x, axis=1, keepdims=True)
        scaled = (x * gain[...]).astype(BF16)
        part[0:QUARTER, :] = jnp.dot(scaled, weight[...], preferred_element_type=F32)
        part[QUARTER:, :] = jnp.zeros((8, 2 * HD), F32)
        part[QUARTER:, 0:QUARTER] = jnp.broadcast_to(squares, (QUARTER, QUARTER)).T[0:8]


def project(place, stream, gain, weight):
    shape = (QUARTER + 8, 2 * HD)
    return pl.pallas_call(
        project_kernel,
        name="project",
        out_shape=[jax.ShapeDtypeStruct(shape, F32)] * PARTS,
        in_specs=[SMEM, whole(stream.shape), whole(gain.shape), whole(weight.shape)],
        out_specs=[whole(shape)] * PARTS,
        compiler_params=pltpu.CompilerParams(vmem_limit_bytes=24 << 20),
        cost_estimate=pl.CostEstimate(flops=1 << 29, bytes_accessed=3 << 20, transcendentals=0),
    )(place, stream, gain, weight)


def norm_kernel(a, b, c, d, out):
    total = (a[...] + b[...]) + (c[...] + d[...])
    row = jnp.broadcast_to(total[QUARTER : QUARTER + 1, 0:QUARTER], (QUARTER, QUARTER))
    column = row.T[:, 0:1]
    root = jnp.sqrt(column / D + norm_epsilon)
    out[...] = (total[0:QUARTER] / root).astype(BF16)


def normed(parts):
    shape = (QUARTER, 2 * HD)
    return pl.pallas_call(
        norm_kernel,
        name="normed",
        out_shape=jax.ShapeDtypeStruct(shape, BF16),
        in_specs=[whole(parts[0].shape)] * PARTS,
        out_specs=whole(shape),
        cost_estimate=pl.CostEstimate(flops=1 << 20, bytes_accessed=5 << 18, transcendentals=0),
    )(*parts)


def join_kernel(place, *refs):
    out = refs[PARTS]
    for k in range(PARTS):
        start = pl.multiple_of(lax.rem(place[0] + PARTS - k, PARTS) * QUARTER, QUARTER)
        out[pl.ds(start, QUARTER), :] = refs[k][...]


def joined(place, pieces):
    shape = (TOK, 2 * HD)
    return pl.pallas_call(
        join_kernel,
        name="joined",
        out_shape=jax.ShapeDtypeStruct(shape, BF16),
        in_specs=[SMEM] + [whole(pieces[0].shape)] * PARTS,
        out_specs=whole(shape),
        cost_estimate=pl.CostEstimate(flops=0, bytes_accessed=1 << 20, transcendentals=0),
    )(place, *pieces)


def negative_expm1(y, grown):
    series = jnp.full_like(y, 1.0)
    for k in (8, 7, 6, 5, 4, 3, 2):
        series = 1.0 + series * (y * (1.0 / k))
    return jnp.where(y > -0.5, -y * series, 1.0 - grown)


def recur_kernel(
    branch, edge, gate, taps, shift, in_w, in_b, de_w, de_b, param, u_out, w_out, end_out,
    extended, factors, pushes,
):
    extended[8 : 8 + TOK, :] = branch[...].astype(F32)
    extended[8 - (CONV - 1) : 8, :] = edge[...].astype(F32)
    totals = shift[...] + taps[0:1, :] * extended[8 : 8 + TOK, :]
    for k in range(1, CONV):
        totals = totals + taps[k : k + 1, :] * extended[8 - k : 8 - k + TOK, :]
    mixed = totals.astype(BF16)
    inflow = jax.nn.sigmoid(
        jnp.dot(mixed, in_w[0], preferred_element_type=F32) + in_b[...]
    )
    recurrence = jax.nn.sigmoid(
        jnp.dot(mixed, de_w[0], preferred_element_type=F32) + de_b[...]
    )
    v = -param[...]
    soft = jnp.maximum(v, 0.0) + jnp.log1p(jnp.exp(-jnp.abs(v)))
    log_decay = recurrence * (-decay_power * soft)
    factor = jnp.exp(log_decay)
    push = (
        jnp.sqrt(negative_expm1(2.0 * log_decay, factor * factor))
        * inflow
        * mixed.astype(F32)
    )
    for lane in range(BLK // LANES):
        there = slice(lane * LANES, (lane + 1) * LANES)
        factors[lane] = factor[:, there]
        pushes[lane] = push[:, there]

    lanes = range(BLK // LANES)
    product = [jnp.ones((SEGMENTS, LANES), F32) for _ in lanes]
    state = [jnp.zeros((SEGMENTS, LANES), F32) for _ in lanes]
    for t in range(STEPS):
        rows = pl.ds(t, SEGMENTS, stride=STEPS)
        for lane in lanes:
            f = factors[lane, rows, :]
            state[lane] = f * state[lane] + pushes[lane, rows, :]
            product[lane] = product[lane] * f
            pushes[lane, rows, :] = state[lane]
            factors[lane, rows, :] = product[lane]
    for lane in lanes:
        there = slice(lane * LANES, (lane + 1) * LANES)
        before_f = jnp.ones((1, LANES), F32)
        before_s = jnp.zeros((1, LANES), F32)
        for r in range(SEGMENTS):
            rows = slice(r * STEPS, (r + 1) * STEPS)
            g = gate[rows, there].astype(F32)
            g = 0.5 * g * (1.0 + jnp.tanh(0.7978845608028654 * (g + 0.044715 * (g * g * g))))
            local_f = factors[lane, rows, :]
            u_out[rows, there] = (pushes[lane, rows, :] + local_f * before_s) * g
            w_out[rows, there] = (local_f * before_f) * g
            before_s = product[lane][r : r + 1] * before_s + state[lane][r : r + 1]
            before_f = product[lane][r : r + 1] * before_f
        end_out[0:1, there] = before_f
        end_out[1:2, there] = before_s


def recur(branch, edge, gate, taps, shift, in_w, in_b, de_w, de_b, param):
    channels = branch.shape[1]
    groups = channels // BLK
    lane = lambda rows: pl.BlockSpec((rows, BLK), lambda n: (0, n))
    square = pl.BlockSpec((1, BLK, BLK), lambda n: (n, 0, 0))
    return pl.pallas_call(
        recur_kernel,
        name="recur",
        grid=(groups,),
        out_shape=[
            jax.ShapeDtypeStruct((TOK, channels), F32),
            jax.ShapeDtypeStruct((TOK, channels), F32),
            jax.ShapeDtypeStruct((2, channels), F32),
        ],
        in_specs=[
            lane(TOK), lane(CONV - 1), lane(TOK), lane(CONV), lane(1),
            square, lane(1), square, lane(1), lane(1),
        ],
        out_specs=[lane(TOK), lane(TOK), lane(2)],
        scratch_shapes=[
            pltpu.VMEM((TOK + 8, BLK), F32),
            pltpu.VMEM((BLK // LANES, TOK, LANES), F32),
            pltpu.VMEM((BLK // LANES, TOK, LANES), F32),
        ],
        compiler_params=pltpu.CompilerParams(vmem_limit_bytes=24 << 20),
        cost_estimate=pl.CostEstimate(
            flops=1 << 30, bytes_accessed=8 << 20, transcendentals=1 << 22
        ),
    )(branch, edge, gate, taps, shift, in_w, in_b, de_w, de_b, param)


def attend_kernel(
    info, q_ref, own, back2, back4, swap0, swap1, swap2, u, w, state, out, recurrent_out, chosen
):
    core, position = (info[0], info[1])
    recurrent_out[...] = (u[...] + w[...] * state[...]).astype(BF16)

    @pl.when(pl.program_id(0) == 0)
    def _():
        @pl.when(core == 0)
        def _():
            chosen[...] = swap2[...]

        @pl.when(core != 0)
        def _():
            chosen[...] = swap0[...]

    def bias(behind):
        return jnp.where(position >= behind, 0.0, masked_score).astype(F32)

    first = bias(1 + 2 * core)
    second = bias(3 - 2 * core)
    rows = lax.broadcasted_iota(jnp.int32, (QROWS, QROWS), 0)
    columns = lax.broadcasted_iota(jnp.int32, (QROWS, QROWS), 1)
    causal = rows >= columns
    halves = (slice(0, QROWS), slice(QROWS, TOK))
    full = slice(0, TOK)
    for half in range(2):
        q = q_ref[halves[half], :] * jnp.asarray(HD**-0.5, BF16)
        blocks = [
            (back2, full, bias(2), None),
            (swap1, full, first, None),
            (chosen, full, second, None),
            (back4, halves[half], bias(4), ~causal),
        ]
        if half == 0:
            blocks.append((back4, halves[1], bias(4), None))
        else:
            blocks.append((own, halves[0], None, None))
        blocks.append((own, halves[half], None, causal))
        scores = []
        for ref, keys, extra, mask in blocks:
            s = lax.dot_general(
                q, ref[keys, 0:HD], (((1,), (1,)), ((), ())), preferred_element_type=F32
            )
            if extra is not None:
                s = s + extra
            if mask is not None:
                s = jnp.where(mask, s, masked_score)
            scores.append(s)
        tiles = [s[:, k : k + 128] for s in scores for k in range(0, s.shape[1], 128)]
        peak = jnp.max(functools.reduce(jnp.maximum, tiles), axis=1, keepdims=True)
        weights = [jnp.exp(s - peak) for s in scores]
        tiles = [p[:, k : k + 128] for p in weights for k in range(0, p.shape[1], 128)]
        norm = jnp.sum(functools.reduce(jnp.add, tiles), axis=1, keepdims=True)
        total = jnp.zeros((QROWS, HD), F32)
        for p, (ref, keys, _, _) in zip(weights, blocks):
            total = total + jnp.dot(
                p.astype(BF16), ref[keys, HD:], preferred_element_type=F32
            )
        out[halves[half], :] = (total / norm).astype(BF16)


def attend(info, queries, shards_of_memory, u, w, state):
    heads = queries.shape[1] // HD
    head = pl.BlockSpec((TOK, HD), lambda h: (0, h))
    one = pl.BlockSpec((1, HD), lambda h: (0, h))
    memory = whole((TOK, 2 * HD))
    return pl.pallas_call(
        attend_kernel,
        name="attend",
        grid=(heads,),
        out_shape=[jax.ShapeDtypeStruct(queries.shape, BF16)] * 2,
        in_specs=[SMEM, head] + [memory] * 6 + [head, head, one],
        out_specs=[head, head],
        scratch_shapes=[pltpu.VMEM((TOK, 2 * HD), BF16)],
        compiler_params=pltpu.CompilerParams(vmem_limit_bytes=40 << 20),
        cost_estimate=pl.CostEstimate(
            flops=5 << 30, bytes_accessed=10 << 20, transcendentals=5 << 20
        ),
    )(info, queries, *shards_of_memory, u, w, state)


def compose(earlier, later):
    return jnp.stack([earlier[0] * later[0], later[0] * earlier[1] + later[1]])


def entering(couple, core):
    other = swapped(couple)
    first = core == 0
    inclusive = compose(jnp.where(first, couple, other), jnp.where(first, other, couple))
    empty = jnp.stack([jnp.ones_like(couple[0]), jnp.zeros_like(couple[0])])
    before = jnp.where(first, empty, other)
    steps = 2
    while steps < lax.axis_size(SEQ):
        arrived = shifted(inclusive, steps)
        before = compose(arrived, before)
        inclusive = compose(arrived, inclusive)
        steps *= 2
    return before[1:2]


def shards(
    branch_in,
    branch_gate,
    conv_taps,
    conv_shift,
    inflow_weight,
    inflow_bias,
    decay_weight,
    decay_bias,
    decay_param,
    stream,
    norm_gain,
    memory_weight,
    queries,
):
    position = lax.axis_index(SEQ)
    core = lax.axis_index(CORE)
    place = lax.axis_index("mp").reshape(1)
    info = jnp.stack([core, position]).astype(jnp.int32)
    line = lambda v: v.reshape(1, -1)

    edge = shifted(branch_in[TOK - (CONV - 1) :], 1)
    parts = project(place, stream, line(norm_gain), memory_weight)
    edge, *parts = lax.optimization_barrier((edge, *parts))
    arrived = [turned(parts[k], k) for k in range(1, PARTS)]
    u, w, couple = recur(
        branch_in, edge, branch_gate, conv_taps, line(conv_shift),
        inflow_weight, line(inflow_bias), decay_weight, line(decay_bias), line(decay_param),
    )
    quarter = normed([parts[0]] + arrived)
    quarter, couple = lax.optimization_barrier((quarter, couple))
    pieces = [quarter] + [turned(quarter, k) for k in range(1, PARTS)]
    memory = joined(place, pieces)
    back2 = shifted(memory, 2)
    back4 = shifted(memory, 4)
    swap0, swap1, swap2 = (swapped(memory), swapped(back2), swapped(back4))
    incoming = entering(couple, core)
    window = (memory, back2, back4, swap0, swap1, swap2)
    attended, recurrent_out = attend(info, queries, window, u, w, incoming)
    return (recurrent_out, attended)


def solution(mesh):
    finer = Mesh(mesh.devices.reshape(8, 4, 2, mesh.shape["mp"]), (*SEQ, "mp"))
    in_specs = (
        P(SEQ, "mp"),
        P(SEQ, "mp"),
        P(None, "mp"),
        P("mp"),
        P("mp", None, None),
        P("mp"),
        P("mp", None, None),
        P("mp"),
        P("mp"),
        P(SEQ, "mp"),
        P("mp"),
        P("mp", None),
        P(SEQ, "mp"),
    )
    out_specs = (P(SEQ, "mp"), P(SEQ, "mp"))
    return jax.shard_map(
        shards, mesh=finer, in_specs=in_specs, out_specs=out_specs, check_vma=False
    )
```

time: 243 us -> 115 us (0.47)
  the two profiles are of different devices: /device:TPU:50 before, /device:TPU:6 now
where the time goes in v1:
time: 115 us; the launch traced here: 114 us
  starting transfers between devices  49.3 us (43%)
  Pallas kernels  28.2 us (25%)
  waiting for transfers between devices  19.9 us (17%)
  local copies, waits for them, and re-layouts  15.7 us (14%)
    ppermute x8, starting transfers between devices, shifted(): lax.ppermute(value, SEQ, [(k, k + steps) for k in range(count - steps)])  38.9 us
    ppermute x8, waiting for transfers between devices, shifted(): lax.ppermute(value, SEQ, [(k, k + steps) for k in range(count - steps)])  15.9 us
    unnamed x52, local copies, waits for them, and re-layouts  15 us
    pallas_call x1, Pallas kernels, attend(): pl.pallas_call(attend_kernel, name='attend', grid=(heads,), out_shape=[ja...  12.2 us
    pallas_call x1, Pallas kernels, recur(): pl.pallas_call(recur_kernel, name='recur', grid=(groups,), out_shape=[jax...  11.3 us
    ppermute x6, starting transfers between devices, turned(): lax.ppermute(value, 'mp', [(k, (k + steps) % PARTS) for k in range(PARTS)])  8.65 us
    ppermute x6, waiting for transfers between devices, turned(): lax.ppermute(value, 'mp', [(k, (k + steps) % PARTS) for k in range(PARTS)])  3.24 us
  transfers between devices with their start and end apart: 18, of which 6 were waited for; matrix products, arithmetic and copies ran while one was open for 0% of the time, Pallas kernels for 12%

profile of v1, /device:TPU:6, one launch (start us, length us, event | category | flops | bytes accessed | tf_op | source)
XLA Modules:
  0.0 114.5 jit_solution(15598916956176471172)
XLA Ops:
  0.7 0.7 slice.58
  1.4 1.9 %collective-permute-start = (bf16[3,1024]{1,0:T(4,128)(2,1)S(1)}, bf16[3,1024]{1,0:T(4,128)(2,1)S(1)}, u32[]{:S(2)}, u32[]{:S(2)}) collective-permute-start(bf16[3,1024]{1,0:T(4,128)(2,1)S(1)} %slice.58), channel_id=1, source_target_pairs={{0,4},{4,8},{8,12},{12,16},{16,20},{20,24},{24,28},{28,32},{32,36}... | collective-permute-start | bytes 18440 | tf_op jit(solution)/shard_map/ppermute | solution.py:40
  3.3 0.0 copy-start
  3.3 1.2 %copy-done = bf16[512,1024]{1,0:T(8,128)(2,1)S(1)} copy-done((bf16[512,1024]{1,0:T(8,128)(2,1)S(1)}, bf16[512,1024]{1,0:T(8,128)(2,1)}, u32[]{:S(2)}) %copy-start) | copy-done | bytes 1048600
  4.6 1.2 %copy-done.1 = bf16[1024,512]{1,0:T(8,128)(2,1)S(1)} copy-done((bf16[1024,512]{1,0:T(8,128)(2,1)S(1)}, bf16[1024,512]{1,0:T(8,128)(2,1)}, u32[]{:S(2)}) %copy-start.1) | copy-done | bytes 1048600
  5.8 0.7 copy-done.4
  6.5 0.7 project.1
  7.2 0.0 copy-start.3
  7.2 0.7 copy-done.3
  7.9 1.6 %collective-permute-start.1 = (f32[136,512]{1,0:T(8,128)S(1)}, f32[136,512]{1,0:T(8,128)S(1)}, u32[]{:S(2)}, u32[]{:S(2)}) collective-permute-start(f32[136,512]{1,0:T(8,128)S(1)} %get-tuple-element.23), channel_id=1, source_target_pairs={{0,1},{1,2},{2,3},{3,0},{4,5},{5,6},{6,7},{7,4},{8,9},{9,10},{10,1... | collective-permute-start | bytes 835592 | tf_op jit(solution)/shard_map/ppermute | solution.py:44
  9.5 2.9 %collective-permute-start.2 = (f32[136,512]{1,0:T(8,128)S(1)}, f32[136,512]{1,0:T(8,128)S(1)}, u32[]{:S(2)}, u32[]{:S(2)}) collective-permute-start(f32[136,512]{1,0:T(8,128)S(1)} %get-tuple-element.24), channel_id=1, source_target_pairs={{0,2},{1,3},{2,0},{3,1},{4,6},{5,7},{6,4},{7,5},{8,10},{9,11},{10,... | collective-permute-start | bytes 835592 | tf_op jit(solution)/shard_map/ppermute | solution.py:44
  12.4 1.3 %collective-permute-start.3 = (f32[136,512]{1,0:T(8,128)S(1)}, f32[136,512]{1,0:T(8,128)S(1)}, u32[]{:S(2)}, u32[]{:S(2)}) collective-permute-start(f32[136,512]{1,0:T(8,128)S(1)} %get-tuple-element.25), channel_id=1, source_target_pairs={{0,3},{1,0},{2,1},{3,2},{4,7},{5,4},{6,5},{7,6},{8,11},{9,8},{10,9... | collective-permute-start | bytes 835592 | tf_op jit(solution)/shard_map/ppermute | solution.py:44
  13.8 0.0 copy-start.8
  13.8 1.0 copy-done.8
  14.8 1.0 copy-done.9
  15.9 11.3 %recur.1 = (f32[512,1024]{1,0:T(8,128)S(1)}, f32[512,1024]{1,0:T(8,128)S(1)}, f32[2,1024]{1,0:T(2,128)S(1)}) custom-call(bf16[512,1024]{1,0:T(8,128)(2,1)S(1)} %copy-done.5, bf16[3,1024]{1,0:T(4,128)(2,1)S(1)} %collective-permute-done.edge, bf16[512,1024]{1,0:T(8,128)(2,1)S(1)} %copy-done.6, f32[4,1024]{1,0:T(4,128)S(1)} %copy-done.10, ...), custom_call_target="tpu_custom_call" | custom-call | flops 1073741824 | bytes 8388608 | tf_op jit(solution)/shard_map/recur/pallas_call | solution.py:184
  27.2 1.3 %copy-done.15 = f32[512,1024]{1,0:T(8,128)} copy-done((f32[512,1024]{1,0:T(8,128)}, f32[512,1024]{1,0:T(8,128)S(1)}, u32[]{:S(2)}) %copy-start.15) | copy-done | bytes 2097176
  28.6 1.3 %copy-done.17 = f32[512,1024]{1,0:T(8,128)} copy-done((f32[512,1024]{1,0:T(8,128)}, f32[512,1024]{1,0:T(8,128)S(1)}, u32[]{:S(2)}) %copy-start.17) | copy-done | bytes 2097176
  29.9 0.7 copy-done.19
  30.6 0.1 copy-done.20
  30.7 0.7 copy-done.21
  31.4 2.1 %normed.1.refs_0_ = bf16[128,512]{1,0:T(8,128)(2,1)} custom-call(f32[136,512]{1,0:T(8,128)} %copy-done.3, f32[136,512]{1,0:T(8,128)} %copy-done.19, f32[136,512]{1,0:T(8,128)} %copy-done.20, f32[136,512]{1,0:T(8,128)} %copy-done.21), custom_call_target="tpu_custom_call" | custom-call | flops 1048576 | bytes 1310720 | tf_op jit(solution)/shard_map/normed/pallas_call | solution.py:85
  33.5 1.1 collective-permute-start.12
  34.6 0.8 collective-permute-done.12
  35.5 3.5 %collective-permute-start.13 = (f32[2,1024]{1,0:T(2,128)S(1)}, f32[2,1024]{1,0:T(2,128)S(1)}, u32[]{:S(2)}, u32[]{:S(2)}) collective-permute-start(f32[2,1024]{1,0:T(2,128)S(1)} %pad_maximum_fusion), channel_id=1, source_target_pairs={{0,8},{4,12},{8,16},{12,20},{16,24},{20,28},{24,32},{28,36},{32,40... | collective-permute-start | bytes 24584 | tf_op jit(solution)/shard_map/ppermute | solution.py:40
  39.0 0.2 collective-permute-start.6
  39.3 2.6 %collective-permute-start.5 = (bf16[128,512]{1,0:T(8,128)(2,1)}, bf16[128,512]{1,0:T(8,128)(2,1)S(1)}, u32[]{:S(2)}, u32[]{:S(2)}) collective-permute-start(bf16[128,512]{1,0:T(8,128)(2,1)} %normed.1.refs_0_), channel_id=1, source_target_pairs={{0,2},{1,3},{2,0},{3,1},{4,6},{5,7},{6,4},{7,5},{8,10},{9,11},{10,... | collective-permute-start | bytes 393224 | tf_op jit(solution)/shard_map/ppermute | solution.py:44
  41.9 3.9 %collective-permute-start.14 = (f32[2,1024]{1,0:T(2,128)S(1)}, f32[2,1024]{1,0:T(2,128)S(1)}, u32[]{:S(2)}, u32[]{:S(2)}) collective-permute-start(f32[2,1024]{1,0:T(2,128)S(1)} %pad_maximum_fusion.1), channel_id=1, source_target_pairs={{0,16},{4,20},{8,24},{12,28},{16,32},{20,36},{24,40},{28,44},{32,4... | collective-permute-start | bytes 24584 | tf_op jit(solution)/shard_map/ppermute | solution.py:40
  45.8 1.3 %collective-permute-done.5.refs_2_ = bf16[128,512]{1,0:T(8,128)(2,1)S(1)} collective-permute-done((bf16[128,512]{1,0:T(8,128)(2,1)}, bf16[128,512]{1,0:T(8,128)(2,1)S(1)}, u32[]{:S(2)}, u32[]{:S(2)}) %collective-permute-start.5) | collective-permute-done | bytes 131104 | tf_op jit(solution)/shard_map/ppermute | solution.py:44
  47.1 2.0 %collective-permute-done.4.refs_1_ = bf16[128,512]{1,0:T(8,128)(2,1)S(1)} collective-permute-done((bf16[128,512]{1,0:T(8,128)(2,1)}, bf16[128,512]{1,0:T(8,128)(2,1)S(1)}, u32[]{:S(2)}, u32[]{:S(2)}) %collective-permute-start.4) | collective-permute-done | bytes 131104 | tf_op jit(solution)/shard_map/ppermute | solution.py:44
  49.1 0.7 copy-done.24
  49.7 1.9 %joined.1.own = bf16[512,512]{1,0:T(8,128)(2,1)} custom-call(s32[1]{0:T(128)} %bitcast.2.place, bf16[128,512]{1,0:T(8,128)(2,1)} %normed.1.refs_0_, bf16[128,512]{1,0:T(8,128)(2,1)} %copy-done.24, bf16[128,512]{1,0:T(8,128)(2,1)} %copy-done.23, bf16[128,512]{1,0:T(8,128)(2,1)} %copy-done.22), custom_call_target="tpu_custom_call" | custom-call | bytes 1048576 | tf_op jit(solution)/shard_map/joined/pallas_call | solution.py:104
  51.7 4.0 %collective-permute-start.8 = (bf16[512,512]{1,0:T(8,128)(2,1)}, bf16[512,512]{1,0:T(8,128)(2,1)S(1)}, u32[]{:S(2)}, u32[]{:S(2)}) collective-permute-start(bf16[512,512]{1,0:T(8,128)(2,1)} %joined.1.own), channel_id=1, source_target_pairs={{0,16},{4,20},{8,24},{12,28},{16,32},{20,36},{24,40},{28,44},{32,4... | collective-permute-start | bytes 1572872 | tf_op jit(solution)/shard_map/ppermute | solution.py:40
  55.7 4.3 %collective-permute-start.7 = (bf16[512,512]{1,0:T(8,128)(2,1)}, bf16[512,512]{1,0:T(8,128)(2,1)S(1)}, u32[]{:S(2)}, u32[]{:S(2)}) collective-permute-start(bf16[512,512]{1,0:T(8,128)(2,1)} %joined.1.own), channel_id=1, source_target_pairs={{0,8},{4,12},{8,16},{12,20},{16,24},{20,28},{24,32},{28,36},{32,40... | collective-permute-start | bytes 1572872 | tf_op jit(solution)/shard_map/ppermute | solution.py:40
  60.1 3.8 %collective-permute-start.15 = (f32[2,1024]{1,0:T(2,128)S(1)}, f32[2,1024]{1,0:T(2,128)S(1)}, u32[]{:S(2)}, u32[]{:S(2)}) collective-permute-start(f32[2,1024]{1,0:T(2,128)S(1)} %pad_maximum_fusion.2), channel_id=1, source_target_pairs={{0,32},{4,36},{8,40},{12,44},{16,48},{20,52},{24,56},{28,60},{32,6... | collective-permute-start | bytes 24584 | tf_op jit(solution)/shard_map/ppermute | solution.py:40
  63.9 14.1 %collective-permute-done.15 = f32[2,1024]{1,0:T(2,128)S(1)} collective-permute-done((f32[2,1024]{1,0:T(2,128)S(1)}, f32[2,1024]{1,0:T(2,128)S(1)}, u32[]{:S(2)}, u32[]{:S(2)}) %collective-permute-start.15) | collective-permute-done | bytes 8224 | tf_op jit(solution)/shard_map/ppermute | solution.py:40
  78.1 5.7 %collective-permute-start.16 = (f32[2,1024]{1,0:T(2,128)S(1)}, f32[2,1024]{1,0:T(2,128)S(1)}, u32[]{:S(2)}, u32[]{:S(2)}) collective-permute-start(f32[2,1024]{1,0:T(2,128)S(1)} %pad_maximum_fusion.3), channel_id=1, source_target_pairs={{0,64},{4,68},{8,72},{12,76},{16,80},{20,84},{24,88},{28,92},{32,9... | collective-permute-start | bytes 24584 | tf_op jit(solution)/shard_map/ppermute | solution.py:40
  83.8 0.1 collective-permute-start.9
  83.9 0.5 collective-permute-start.11
  84.4 0.1 collective-permute-start.10
  84.5 0.6 collective-permute-done.16
  85.2 11.6 %collective-permute-start.17 = (f32[2,1024]{1,0:T(2,128)S(1)}, f32[2,1024]{1,0:T(2,128)S(1)}, u32[]{:S(2)}, u32[]{:S(2)}) collective-permute-start(f32[2,1024]{1,0:T(2,128)S(1)} %pad_maximum_fusion.4), channel_id=1, source_target_pairs={{0,128},{4,132},{8,136},{12,140},{16,144},{20,148},{24,152},{28,15... | collective-permute-start | bytes 24584 | tf_op jit(solution)/shard_map/ppermute | solution.py:40
  96.8 0.1 pad_add_fusion.info
  96.9 1.1 collective-permute-done.17
  98.1 1.0 copy-done.2
  99.1 1.6 %copy-done.16 = f32[512,1024]{1,0:T(8,128)S(1)} copy-done((f32[512,1024]{1,0:T(8,128)S(1)}, f32[512,1024]{1,0:T(8,128)}, u32[]{:S(2)}) %copy-start.16) | copy-done | bytes 2097176
  100.7 1.6 %copy-done.18 = f32[512,1024]{1,0:T(8,128)S(1)} copy-done((f32[512,1024]{1,0:T(8,128)S(1)}, f32[512,1024]{1,0:T(8,128)}, u32[]{:S(2)}) %copy-start.18) | copy-done | bytes 2097176
  102.3 12.2 %attend.1 = (bf16[512,1024]{1,0:T(8,128)(2,1)}, bf16[512,1024]{1,0:T(8,128)(2,1)}) custom-call(s32[2]{0:T(128)S(1)} %pad_add_fusion.info, bf16[512,1024]{1,0:T(8,128)(2,1)S(1)} %copy-done.7, bf16[512,512]{1,0:T(8,128)(2,1)S(1)} %copy-done.2, bf16[512,512]{1,0:T(8,128)(2,1)S(1)} %collective-permute-done.7.back2, ...), custom_call_target="tpu_custom_call" | custom-call | flops 5368709120 | bytes 10485760 | tf_op jit(solution)/shard_map/attend/pallas_call | solution.py:277
  (59 shorter events, 0.3 us)
Async XLA Ops:
  0.6 13.1 %copy-start.12 = (f32[1024]{0:T(1024)S(1)}, f32[1024]{0:T(1024)}, u32[]{:S(2)}) copy-start(f32[1024]{0:T(1024)} %param.18) | copy-start | bytes 12292
  0.6 13.1 %copy-start.11 = (f32[1024]{0:T(1024)S(1)}, f32[1024]{0:T(1024)}, u32[]{:S(2)}) copy-start(f32[1024]{0:T(1024)} %param.16) | copy-start | bytes 12292
  0.7 13.1 %copy-start.10 = (f32[4,1024]{1,0:T(4,128)S(1)}, f32[4,1024]{1,0:T(4,128)}, u32[]{:S(2)}) copy-start(f32[4,1024]{1,0:T(4,128)} %taps.1) | copy-start | bytes 49156
  1.4 6.5 %collective-permute-start = (bf16[3,1024]{1,0:T(4,128)(2,1)S(1)}, bf16[3,1024]{1,0:T(4,128)(2,1)S(1)}, u32[]{:S(2)}, u32[]{:S(2)}) collective-permute-start(bf16[3,1024]{1,0:T(4,128)(2,1)S(1)} %slice.58), channel_id=1, source_target_pairs={{0,4},{4,8},{8,12},{12,16},{16,20},{20,24},{24,28},{28,32},{32,36}... | collective-permute-start | bytes 18440 | tf_op jit(solution)/shard_map/ppermute | solution.py:40
  3.3 1.2 %copy-start = (bf16[512,1024]{1,0:T(8,128)(2,1)S(1)}, bf16[512,1024]{1,0:T(8,128)(2,1)}, u32[]{:S(2)}) copy-start(bf16[512,1024]{1,0:T(8,128)(2,1)} %stream.1) | copy-start | bytes 3145732
  4.6 1.2 %copy-start.1 = (bf16[1024,512]{1,0:T(8,128)(2,1)S(1)}, bf16[1024,512]{1,0:T(8,128)(2,1)}, u32[]{:S(2)}) copy-start(bf16[1024,512]{1,0:T(8,128)(2,1)} %weight.1) | copy-start | bytes 3145732
  5.8 0.7 copy-start.4
  6.5 7.3 %copy-start.5 = (bf16[512,1024]{1,0:T(8,128)(2,1)S(1)}, bf16[512,1024]{1,0:T(8,128)(2,1)}, u32[]{:S(2)}) copy-start(bf16[512,1024]{1,0:T(8,128)(2,1)} %branch.1) | copy-start | bytes 3145732
  6.5 7.3 %copy-start.6 = (bf16[512,1024]{1,0:T(8,128)(2,1)S(1)}, bf16[512,1024]{1,0:T(8,128)(2,1)}, u32[]{:S(2)}) copy-start(bf16[512,1024]{1,0:T(8,128)(2,1)} %gate.1) | copy-start | bytes 3145732
  6.5 7.3 %copy-start.13 = (f32[1024]{0:T(1024)S(1)}, f32[1024]{0:T(1024)}, u32[]{:S(2)}) copy-start(f32[1024]{0:T(1024)} %param.20) | copy-start | bytes 12292
  6.5 7.3 %copy-start.14 = (f32[1024]{0:T(1024)S(1)}, f32[1024]{0:T(1024)}, u32[]{:S(2)}) copy-start(f32[1024]{0:T(1024)} %param.21) | copy-start | bytes 12292
  7.2 0.7 copy-start.3
  7.9 22.0 %collective-permute-start.1 = (f32[136,512]{1,0:T(8,128)S(1)}, f32[136,512]{1,0:T(8,128)S(1)}, u32[]{:S(2)}, u32[]{:S(2)}) collective-permute-start(f32[136,512]{1,0:T(8,128)S(1)} %get-tuple-element.23), channel_id=1, source_target_pairs={{0,1},{1,2},{2,3},{3,0},{4,5},{5,6},{6,7},{7,4},{8,9},{9,10},{10,1... | collective-permute-start | bytes 835592 | tf_op jit(solution)/shard_map/ppermute | solution.py:44
  9.5 20.4 %collective-permute-start.2 = (f32[136,512]{1,0:T(8,128)S(1)}, f32[136,512]{1,0:T(8,128)S(1)}, u32[]{:S(2)}, u32[]{:S(2)}) collective-permute-start(f32[136,512]{1,0:T(8,128)S(1)} %get-tuple-element.24), channel_id=1, source_target_pairs={{0,2},{1,3},{2,0},{3,1},{4,6},{5,7},{6,4},{7,5},{8,10},{9,11},{10,... | collective-permute-start | bytes 835592 | tf_op jit(solution)/shard_map/ppermute | solution.py:44
  12.4 17.5 %collective-permute-start.3 = (f32[136,512]{1,0:T(8,128)S(1)}, f32[136,512]{1,0:T(8,128)S(1)}, u32[]{:S(2)}, u32[]{:S(2)}) collective-permute-start(f32[136,512]{1,0:T(8,128)S(1)} %get-tuple-element.25), channel_id=1, source_target_pairs={{0,3},{1,0},{2,1},{3,2},{4,7},{5,4},{6,5},{7,6},{8,11},{9,8},{10,9... | collective-permute-start | bytes 835592 | tf_op jit(solution)/shard_map/ppermute | solution.py:44
  13.8 1.0 copy-start.8
  14.8 1.0 copy-start.9
  15.9 19.5 %copy-start.25 = (f32[2,1024]{1,0:T(2,128)S(1)}, f32[2,1024]{1,0:T(2,128)}, u32[]{:S(2)}) copy-start(f32[2,1024]{1,0:T(2,128)} %constant.24.clone.1) | copy-start | bytes 24580
  27.2 1.3 %copy-start.15 = (f32[512,1024]{1,0:T(8,128)}, f32[512,1024]{1,0:T(8,128)S(1)}, u32[]{:S(2)}) copy-start(f32[512,1024]{1,0:T(8,128)S(1)} %get-tuple-element.29.u) | copy-start | bytes 6291460
  28.6 1.3 %copy-start.17 = (f32[512,1024]{1,0:T(8,128)}, f32[512,1024]{1,0:T(8,128)S(1)}, u32[]{:S(2)}) copy-start(f32[512,1024]{1,0:T(8,128)S(1)} %get-tuple-element.30.w) | copy-start | bytes 6291460
  29.9 68.2 %copy-start.7 = (bf16[512,1024]{1,0:T(8,128)(2,1)S(1)}, bf16[512,1024]{1,0:T(8,128)(2,1)}, u32[]{:S(2)}) copy-start(bf16[512,1024]{1,0:T(8,128)(2,1)} %q_ref.1) | copy-start | bytes 3145732
  29.9 0.7 copy-start.19
  29.9 0.8 copy-start.20
  30.7 0.7 copy-start.21
  33.5 1.9 %collective-permute-start.12 = (f32[2,1024]{1,0:T(2,128)S(1)}, f32[2,1024]{1,0:T(2,128)S(1)}, u32[]{:S(2)}, u32[]{:S(2)}) collective-permute-start(f32[2,1024]{1,0:T(2,128)S(1)} %get-tuple-element.31), channel_id=1, source_target_pairs={{0,4},{4,0},{1,5},{5,1},{2,6},{6,2},{3,7},{7,3},{8,12},{12,8},{9,1... | collective-permute-start | bytes 24584 | tf_op jit(solution)/shard_map/ppermute | solution.py:48
  35.5 6.4 %collective-permute-start.13 = (f32[2,1024]{1,0:T(2,128)S(1)}, f32[2,1024]{1,0:T(2,128)S(1)}, u32[]{:S(2)}, u32[]{:S(2)}) collective-permute-start(f32[2,1024]{1,0:T(2,128)S(1)} %pad_maximum_fusion), channel_id=1, source_target_pairs={{0,8},{4,12},{8,16},{12,20},{16,24},{20,28},{24,32},{28,36},{32,40... | collective-permute-start | bytes 24584 | tf_op jit(solution)/shard_map/ppermute | solution.py:40
  39.0 6.8 %collective-permute-start.6 = (bf16[128,512]{1,0:T(8,128)(2,1)}, bf16[128,512]{1,0:T(8,128)(2,1)S(1)}, u32[]{:S(2)}, u32[]{:S(2)}) collective-permute-start(bf16[128,512]{1,0:T(8,128)(2,1)} %normed.1.refs_0_), channel_id=1, source_target_pairs={{0,3},{1,0},{2,1},{3,2},{4,7},{5,4},{6,5},{7,6},{8,11},{9,8},{10,9... | collective-permute-start | bytes 393224 | tf_op jit(solution)/shard_map/ppermute | solution.py:44
  39.3 7.8 %collective-permute-start.5 = (bf16[128,512]{1,0:T(8,128)(2,1)}, bf16[128,512]{1,0:T(8,128)(2,1)S(1)}, u32[]{:S(2)}, u32[]{:S(2)}) collective-permute-start(bf16[128,512]{1,0:T(8,128)(2,1)} %normed.1.refs_0_), channel_id=1, source_target_pairs={{0,2},{1,3},{2,0},{3,1},{4,6},{5,7},{6,4},{7,5},{8,10},{9,11},{10,... | collective-permute-start | bytes 393224 | tf_op jit(solution)/shard_map/ppermute | solution.py:44
  41.9 7.2 %collective-permute-start.4 = (bf16[128,512]{1,0:T(8,128)(2,1)}, bf16[128,512]{1,0:T(8,128)(2,1)S(1)}, u32[]{:S(2)}, u32[]{:S(2)}) collective-permute-start(bf16[128,512]{1,0:T(8,128)(2,1)} %normed.1.refs_0_), channel_id=1, source_target_pairs={{0,1},{1,2},{2,3},{3,0},{4,5},{5,6},{6,7},{7,4},{8,9},{9,10},{10,1... | collective-permute-start | bytes 393224 | tf_op jit(solution)/shard_map/ppermute | solution.py:44
  41.9 18.1 %collective-permute-start.14 = (f32[2,1024]{1,0:T(2,128)S(1)}, f32[2,1024]{1,0:T(2,128)S(1)}, u32[]{:S(2)}, u32[]{:S(2)}) collective-permute-start(f32[2,1024]{1,0:T(2,128)S(1)} %pad_maximum_fusion.1), channel_id=1, source_target_pairs={{0,16},{4,20},{8,24},{12,28},{16,32},{20,36},{24,40},{28,44},{32,4... | collective-permute-start | bytes 24584 | tf_op jit(solution)/shard_map/ppermute | solution.py:40
  45.8 3.2 %copy-start.22 = (bf16[128,512]{1,0:T(8,128)(2,1)}, bf16[128,512]{1,0:T(8,128)(2,1)S(1)}, u32[]{:S(2)}) copy-start(bf16[128,512]{1,0:T(8,128)(2,1)S(1)} %collective-permute-done.6.refs_3_) | copy-start | bytes 393220
  47.1 2.0 %copy-start.23 = (bf16[128,512]{1,0:T(8,128)(2,1)}, bf16[128,512]{1,0:T(8,128)(2,1)S(1)}, u32[]{:S(2)}) copy-start(bf16[128,512]{1,0:T(8,128)(2,1)S(1)} %collective-permute-done.5.refs_2_) | copy-start | bytes 393220
  49.1 0.7 copy-start.24
  51.7 32.3 %collective-permute-start.8 = (bf16[512,512]{1,0:T(8,128)(2,1)}, bf16[512,512]{1,0:T(8,128)(2,1)S(1)}, u32[]{:S(2)}, u32[]{:S(2)}) collective-permute-start(bf16[512,512]{1,0:T(8,128)(2,1)} %joined.1.own), channel_id=1, source_target_pairs={{0,16},{4,20},{8,24},{12,28},{16,32},{20,36},{24,40},{28,44},{32,4... | collective-permute-start | bytes 1572872 | tf_op jit(solution)/shard_map/ppermute | solution.py:40
  55.7 28.7 %collective-permute-start.7 = (bf16[512,512]{1,0:T(8,128)(2,1)}, bf16[512,512]{1,0:T(8,128)(2,1)S(1)}, u32[]{:S(2)}, u32[]{:S(2)}) collective-permute-start(bf16[512,512]{1,0:T(8,128)(2,1)} %joined.1.own), channel_id=1, source_target_pairs={{0,8},{4,12},{8,16},{12,20},{16,24},{20,28},{24,32},{28,36},{32,40... | collective-permute-start | bytes 1572872 | tf_op jit(solution)/shard_map/ppermute | solution.py:40
  60.1 18.0 %collective-permute-start.15 = (f32[2,1024]{1,0:T(2,128)S(1)}, f32[2,1024]{1,0:T(2,128)S(1)}, u32[]{:S(2)}, u32[]{:S(2)}) collective-permute-start(f32[2,1024]{1,0:T(2,128)S(1)} %pad_maximum_fusion.2), channel_id=1, source_target_pairs={{0,32},{4,36},{8,40},{12,44},{16,48},{20,52},{24,56},{28,60},{32,6... | collective-permute-start | bytes 24584 | tf_op jit(solution)/shard_map/ppermute | solution.py:40
  78.1 7.1 %collective-permute-start.16 = (f32[2,1024]{1,0:T(2,128)S(1)}, f32[2,1024]{1,0:T(2,128)S(1)}, u32[]{:S(2)}, u32[]{:S(2)}) collective-permute-start(f32[2,1024]{1,0:T(2,128)S(1)} %pad_maximum_fusion.3), channel_id=1, source_target_pairs={{0,64},{4,68},{8,72},{12,76},{16,80},{20,84},{24,88},{28,92},{32,9... | collective-permute-start | bytes 24584 | tf_op jit(solution)/shard_map/ppermute | solution.py:40
  83.8 14.2 %collective-permute-start.9 = (bf16[512,512]{1,0:T(8,128)(2,1)}, bf16[512,512]{1,0:T(8,128)(2,1)S(1)}, u32[]{:S(2)}, u32[]{:S(2)}) collective-permute-start(bf16[512,512]{1,0:T(8,128)(2,1)} %joined.1.own), channel_id=1, source_target_pairs={{0,4},{4,0},{1,5},{5,1},{2,6},{6,2},{3,7},{7,3},{8,12},{12,8},{9,1... | collective-permute-start | bytes 1572872 | tf_op jit(solution)/shard_map/ppermute | solution.py:48
  83.9 14.1 %collective-permute-start.11 = (bf16[512,512]{1,0:T(8,128)(2,1)S(1)}, bf16[512,512]{1,0:T(8,128)(2,1)S(1)}, u32[]{:S(2)}, u32[]{:S(2)}) collective-permute-start(bf16[512,512]{1,0:T(8,128)(2,1)S(1)} %collective-permute-done.8.back4), channel_id=1, source_target_pairs={{0,4},{4,0},{1,5},{5,1},{2,6},{6,2},{3,7},{7,3},{8,12},{12,8},{9,1... | collective-permute-start | bytes 1572872 | tf_op jit(solution)/shard_map/ppermute | solution.py:48
  84.4 13.6 %collective-permute-start.10 = (bf16[512,512]{1,0:T(8,128)(2,1)S(1)}, bf16[512,512]{1,0:T(8,128)(2,1)S(1)}, u32[]{:S(2)}, u32[]{:S(2)}) collective-permute-start(bf16[512,512]{1,0:T(8,128)(2,1)S(1)} %collective-permute-done.7.back2), channel_id=1, source_target_pairs={{0,4},{4,0},{1,5},{5,1},{2,6},{6,2},{3,7},{7,3},{8,12},{12,8},{9,1... | collective-permute-start | bytes 1572872 | tf_op jit(solution)/shard_map/ppermute | solution.py:48
  85.2 12.8 %collective-permute-start.17 = (f32[2,1024]{1,0:T(2,128)S(1)}, f32[2,1024]{1,0:T(2,128)S(1)}, u32[]{:S(2)}, u32[]{:S(2)}) collective-permute-start(f32[2,1024]{1,0:T(2,128)S(1)} %pad_maximum_fusion.4), channel_id=1, source_target_pairs={{0,128},{4,132},{8,136},{12,140},{16,144},{20,148},{24,152},{28,15... | collective-permute-start | bytes 24584 | tf_op jit(solution)/shard_map/ppermute | solution.py:40
  98.1 1.0 copy-start.2
  99.1 1.6 %copy-start.16 = (f32[512,1024]{1,0:T(8,128)S(1)}, f32[512,1024]{1,0:T(8,128)}, u32[]{:S(2)}) copy-start(f32[512,1024]{1,0:T(8,128)} %copy-done.15) | copy-start | bytes 6291460
  100.7 1.6 %copy-start.18 = (f32[512,1024]{1,0:T(8,128)S(1)}, f32[512,1024]{1,0:T(8,128)}, u32[]{:S(2)}) copy-start(f32[512,1024]{1,0:T(8,128)} %copy-done.17) | copy-start | bytes 6291460

commit v2 on v1

v2 whole, which is shorter than its diff:
```python
import functools

import jax
import jax.numpy as jnp
from jax import lax
from jax.experimental import pallas as pl
from jax.experimental.pallas import tpu as pltpu
from jax.sharding import Mesh
from jax.sharding import PartitionSpec as P

D = 4096
HD = 256
CONV = 4
WINDOW = 2048
BLK = 256
SEQ = ("seq_0", "seq_1", "seq_2")
CORE = "seq_2"
TOK = 512
QUARTER = 128
PARTS = 4
SEGMENTS = 8
STEPS = TOK // SEGMENTS
QROWS = 256
LANES = 128
EXTRA = 16
ROOM = 60 << 20
SHARDS = 5

decay_power = 8.0
norm_epsilon = 1e-06
masked_score = -1e30
F32 = jnp.float32
BF16 = jnp.bfloat16
SMEM = pl.BlockSpec(memory_space=pltpu.SMEM)


def whole(shape):
    return pl.BlockSpec(shape, lambda *_: (0,) * len(shape))


def shifted(value, steps):
    count = lax.axis_size(SEQ)
    return lax.ppermute(value, SEQ, [(k, k + steps) for k in range(count - steps)])


def turned(value, steps):
    return lax.ppermute(value, "mp", [(k, (k + steps) % PARTS) for k in range(PARTS)])


def swapped(value):
    return lax.ppermute(value, CORE, [(0, 1), (1, 0)])


def project_kernel(place, stream, gain, weight, *parts):
    row = lax.broadcasted_iota(jnp.int32, (EXTRA, QUARTER), 0)
    for k, part in enumerate(parts):
        start = pl.multiple_of(lax.rem(place[0] + k, PARTS) * QUARTER, QUARTER)
        x = stream[pl.ds(start, QUARTER), :].astype(F32)
        squares = jnp.sum(x * x, axis=1, keepdims=True)
        scaled = (x * gain[...]).astype(BF16)
        product = jnp.dot(scaled, weight[...], preferred_element_type=F32)
        part[0:QUARTER, :] = product.astype(part.dtype)
        part[QUARTER:, :] = jnp.zeros((EXTRA, 2 * HD), part.dtype)
        line = jnp.broadcast_to(squares, (QUARTER, QUARTER)).T[0:EXTRA]
        high = line.astype(BF16).astype(F32)
        line = jnp.where(row == 0, high, jnp.where(row == 1, line - high, 0.0))
        part[QUARTER:, 0:QUARTER] = line.astype(part.dtype)


def project(place, stream, gain, weight):
    shape = (QUARTER + EXTRA, 2 * HD)
    return pl.pallas_call(
        project_kernel,
        name="project",
        out_shape=[jax.ShapeDtypeStruct(shape, F32 if k == 0 else BF16) for k in range(PARTS)],
        in_specs=[SMEM, whole(stream.shape), whole(gain.shape), whole(weight.shape)],
        out_specs=[whole(shape)] * PARTS,
        compiler_params=pltpu.CompilerParams(vmem_limit_bytes=ROOM),
        cost_estimate=pl.CostEstimate(flops=1 << 29, bytes_accessed=3 << 20, transcendentals=0),
    )(place, stream, gain, weight)


def norm_kernel(a, b, c, d, out):
    total = (a[...] + b[...].astype(F32)) + (c[...].astype(F32) + d[...].astype(F32))
    line = total[QUARTER : QUARTER + 1, 0:QUARTER] + total[QUARTER + 1 : QUARTER + 2, 0:QUARTER]
    column = jnp.broadcast_to(line, (QUARTER, QUARTER)).T[:, 0:1]
    root = jnp.sqrt(column / D + norm_epsilon)
    out[...] = (total[0:QUARTER] / root).astype(BF16)


def normed(parts):
    shape = (QUARTER, 2 * HD)
    return pl.pallas_call(
        norm_kernel,
        name="normed",
        out_shape=jax.ShapeDtypeStruct(shape, BF16),
        in_specs=[whole(parts[0].shape)] * PARTS,
        out_specs=whole(shape),
        compiler_params=pltpu.CompilerParams(vmem_limit_bytes=8 << 20),
        cost_estimate=pl.CostEstimate(flops=1 << 20, bytes_accessed=5 << 17, transcendentals=0),
    )(*parts)


def negative_expm1(y, grown):
    series = jnp.full_like(y, 1.0)
    for k in (8, 7, 6, 5, 4, 3, 2):
        series = 1.0 + series * (y * (1.0 / k))
    return jnp.where(y > -0.5, -y * series, 1.0 - grown)


def recur_kernel(
    branch, edge, gate, taps, shift, in_w, in_b, de_w, de_b, param, *rest
):
    u_out, w_out, end_out, extended, factors, pushes = rest[-6:]
    extended[8 : 8 + TOK, :] = branch[...].astype(F32)
    extended[8 - (CONV - 1) : 8, :] = edge[...].astype(F32)
    totals = shift[...] + taps[0:1, :] * extended[8 : 8 + TOK, :]
    for k in range(1, CONV):
        totals = totals + taps[k : k + 1, :] * extended[8 - k : 8 - k + TOK, :]
    mixed = totals.astype(BF16)
    inflow = jax.nn.sigmoid(
        jnp.dot(mixed, in_w[0], preferred_element_type=F32) + in_b[...]
    )
    recurrence = jax.nn.sigmoid(
        jnp.dot(mixed, de_w[0], preferred_element_type=F32) + de_b[...]
    )
    v = -param[...]
    soft = jnp.maximum(v, 0.0) + jnp.log1p(jnp.exp(-jnp.abs(v)))
    log_decay = recurrence * (-decay_power * soft)
    factor = jnp.exp(log_decay)
    push = (
        jnp.sqrt(negative_expm1(2.0 * log_decay, factor * factor))
        * inflow
        * mixed.astype(F32)
    )
    for lane in range(BLK // LANES):
        there = slice(lane * LANES, (lane + 1) * LANES)
        factors[lane] = factor[:, there]
        pushes[lane] = push[:, there]

    lanes = range(BLK // LANES)
    product = [jnp.ones((SEGMENTS, LANES), F32) for _ in lanes]
    state = [jnp.zeros((SEGMENTS, LANES), F32) for _ in lanes]
    for t in range(STEPS):
        rows = pl.ds(t, SEGMENTS, stride=STEPS)
        for lane in lanes:
            f = factors[lane, rows, :]
            state[lane] = f * state[lane] + pushes[lane, rows, :]
            product[lane] = product[lane] * f
            pushes[lane, rows, :] = state[lane]
            factors[lane, rows, :] = product[lane]
    for lane in lanes:
        there = slice(lane * LANES, (lane + 1) * LANES)
        before_f = jnp.ones((1, LANES), F32)
        before_s = jnp.zeros((1, LANES), F32)
        for r in range(SEGMENTS):
            rows = slice(r * STEPS, (r + 1) * STEPS)
            g = gate[rows, there].astype(F32)
            g = 0.5 * g * (1.0 + jnp.tanh(0.7978845608028654 * (g + 0.044715 * (g * g * g))))
            local_f = factors[lane, rows, :]
            u_out[rows, there] = (pushes[lane, rows, :] + local_f * before_s) * g
            w_out[rows, there] = (local_f * before_f) * g
            before_s = product[lane][r : r + 1] * before_s + state[lane][r : r + 1]
            before_f = product[lane][r : r + 1] * before_f
        end_out[0:1, there] = before_f
        end_out[1:2, there] = before_s


def recur(group, count, branch, edge, gate, taps, shift, in_w, in_b, de_w, de_b, param, filled):
    channels = branch.shape[1]
    lane = lambda rows: pl.BlockSpec((rows, BLK), lambda n: (0, n + group))
    square = pl.BlockSpec((1, BLK, BLK), lambda n: (n + group, 0, 0))
    kept = pl.BlockSpec(memory_space=pl.ANY)
    inputs = (branch, edge, gate, taps, shift, in_w, in_b, de_w, de_b, param)
    return pl.pallas_call(
        recur_kernel,
        name="recur",
        grid=(count,),
        out_shape=[
            jax.ShapeDtypeStruct((TOK, channels), F32),
            jax.ShapeDtypeStruct((TOK, channels), F32),
            jax.ShapeDtypeStruct((2, channels), F32),
        ],
        in_specs=[
            lane(TOK), lane(CONV - 1), lane(TOK), lane(CONV), lane(1),
            square, lane(1), square, lane(1), lane(1),
        ] + [kept] * len(filled),
        out_specs=[lane(TOK), lane(TOK), lane(2)],
        scratch_shapes=[
            pltpu.VMEM((TOK + 8, BLK), F32),
            pltpu.VMEM((BLK // LANES, TOK, LANES), F32),
            pltpu.VMEM((BLK // LANES, TOK, LANES), F32),
        ],
        input_output_aliases={len(inputs) + k: k for k in range(len(filled))},
        compiler_params=pltpu.CompilerParams(vmem_limit_bytes=ROOM),
        cost_estimate=pl.CostEstimate(
            flops=count << 28, bytes_accessed=count << 21, transcendentals=count << 20
        ),
    )(*inputs, *filled)


def attend_kernel(info, q_ref, *refs):
    own, other = (refs[0:PARTS], refs[PARTS : 2 * PARTS])
    out, kv = refs[-2:]
    core, position, place = (info[0], info[1], info[2])

    @pl.when(pl.program_id(0) == 0)
    def _():
        for k in range(PARTS):
            row = lax.rem(place + PARTS - k, PARTS) * QUARTER
            for behind in range(SHARDS):
                there = pl.ds(
                    pl.multiple_of((SHARDS - 1 - behind) * TOK + row, QUARTER), QUARTER
                )
                if behind % 2 == 0:
                    kv[there, :] = own[k][behind // 2 * QUARTER : (behind // 2 + 1) * QUARTER, :]
                else:
                    begin = pl.multiple_of(((behind + 1) // 2 - core) * QUARTER, QUARTER)
                    kv[there, :] = other[k][pl.ds(begin, QUARTER), :]

    def bias(behind):
        return jnp.where(position >= behind, 0.0, masked_score).astype(F32)

    rows = lax.broadcasted_iota(jnp.int32, (QROWS, QROWS), 0)
    columns = lax.broadcasted_iota(jnp.int32, (QROWS, QROWS), 1)
    causal = rows >= columns
    last = (SHARDS - 1) * TOK
    for half in range(2):
        low = half * QROWS
        q = q_ref[low : low + QROWS, :] * jnp.asarray(HD**-0.5, BF16)
        blocks = [(k * TOK, TOK, bias(SHARDS - 1 - k), None) for k in range(1, SHARDS - 1)]
        if half == 0:
            blocks.append((QROWS, QROWS, bias(SHARDS - 1), None))
        else:
            blocks.append((last, QROWS, None, None))
        blocks.append((low, QROWS, bias(SHARDS - 1), ~causal))
        blocks.append((last + low, QROWS, None, causal))
        scores = []
        for begin, size, extra, mask in blocks:
            s = lax.dot_general(
                q,
                kv[begin : begin + size, 0:HD],
                (((1,), (1,)), ((), ())),
                preferred_element_type=F32,
            )
            if extra is not None:
                s = s + extra
            if mask is not None:
                s = jnp.where(mask, s, masked_score)
            scores.append(s)
        tiles = [s[:, k : k + 128] for s in scores for k in range(0, s.shape[1], 128)]
        peak = jnp.max(functools.reduce(jnp.maximum, tiles), axis=1, keepdims=True)
        weights = [jnp.exp(s - peak) for s in scores]
        tiles = [p[:, k : k + 128] for p in weights for k in range(0, p.shape[1], 128)]
        norm = jnp.sum(functools.reduce(jnp.add, tiles), axis=1, keepdims=True)
        total = jnp.zeros((QROWS, HD), F32)
        for p, (begin, size, _, _) in zip(weights, blocks):
            total = total + jnp.dot(
                p.astype(BF16), kv[begin : begin + size, HD:], preferred_element_type=F32
            )
        out[low : low + QROWS, :] = (total / norm).astype(BF16)


def attend(head, count, info, queries, own, other, filled):
    block = pl.BlockSpec((TOK, HD), lambda h: (0, h + head))
    kept = pl.BlockSpec(memory_space=pl.ANY)
    inputs = (info, queries, *own, *other)
    return pl.pallas_call(
        attend_kernel,
        name="attend",
        grid=(count,),
        out_shape=jax.ShapeDtypeStruct(queries.shape, BF16),
        in_specs=[SMEM, block] + [whole(own[0].shape)] * (2 * PARTS) + [kept] * len(filled),
        out_specs=block,
        scratch_shapes=[pltpu.VMEM((SHARDS * TOK, 2 * HD), BF16)],
        input_output_aliases={len(inputs) + k: k for k in range(len(filled))},
        compiler_params=pltpu.CompilerParams(vmem_limit_bytes=32 << 20),
        cost_estimate=pl.CostEstimate(
            flops=count << 30, bytes_accessed=4 << 20, transcendentals=count << 20
        ),
    )(*inputs, *filled)


def compose(earlier, later):
    return jnp.stack([earlier[0] * later[0], later[0] * earlier[1] + later[1]])


def near_prefix(couple, core):
    other = swapped(couple)
    first = core == 0
    inclusive = compose(jnp.where(first, couple, other), jnp.where(first, other, couple))
    empty = jnp.stack([jnp.ones_like(couple[0]), jnp.zeros_like(couple[0])])
    return jnp.where(first, empty, other), inclusive


def doubled(before, inclusive, arrived):
    return compose(arrived, before), compose(arrived, inclusive)


def shards(
    branch_in,
    branch_gate,
    conv_taps,
    conv_shift,
    inflow_weight,
    inflow_bias,
    decay_weight,
    decay_bias,
    decay_param,
    stream,
    norm_gain,
    memory_weight,
    queries,
):
    position = lax.axis_index(SEQ)
    core = lax.axis_index(CORE)
    turn = lax.axis_index("mp")
    place = turn.reshape(1)
    info = jnp.stack([core, position, turn]).astype(jnp.int32)
    line = lambda v: v.reshape(1, -1)

    edge = shifted(branch_in[TOK - (CONV - 1) :], 1)
    parts = project(place, stream, line(norm_gain), memory_weight)
    edge, *parts = lax.optimization_barrier((edge, *parts))
    arrived = [turned(parts[k], k) for k in range(1, PARTS)]
    rest = (
        branch_gate, conv_taps, line(conv_shift), inflow_weight, line(inflow_bias),
        decay_weight, line(decay_bias), line(decay_param),
    )
    groups = branch_in.shape[1] // BLK
    early = groups // 4
    filled = recur(0, early, branch_in, edge, *rest, ())
    own_part, *filled = lax.optimization_barrier((parts[0], *filled))
    quarter = normed([own_part] + arrived)
    trio = jnp.concatenate([quarter, shifted(quarter, 2), shifted(quarter, 4)])
    trio, edge = lax.optimization_barrier((trio, edge))
    own = [trio] + [turned(trio, k) for k in range(1, PARTS)]
    u, w, couple = recur(early, groups - early, branch_in, edge, *rest, filled)
    couple, *own = lax.optimization_barrier((couple, *own))
    before, inclusive = near_prefix(couple, core)
    before, inclusive = doubled(before, inclusive, shifted(inclusive, 2))
    other = [swapped(piece) for piece in own]
    before, inclusive = doubled(before, inclusive, shifted(inclusive, 4))
    heads = queries.shape[1] // HD
    half = heads // 2
    arrived = shifted(inclusive, 8)
    attended = attend(0, half, info, queries, own, other, ())
    arrived, attended = lax.optimization_barrier((arrived, attended))
    before, inclusive = doubled(before, inclusive, arrived)
    arrived = [shifted(inclusive, 16 * k) for k in range(1, 4)]
    attended = attend(half, heads - half, info, queries, own, other, (attended,))
    *arrived, attended = lax.optimization_barrier((*arrived, attended))
    for piece in arrived:
        before = compose(piece, before)
    recurrent_out = (u + w * before[1:2]).astype(BF16)
    return (recurrent_out, attended)


def solution(mesh):
    finer = Mesh(mesh.devices.reshape(8, 4, 2, mesh.shape["mp"]), (*SEQ, "mp"))
    in_specs = (
        P(SEQ, "mp"),
        P(SEQ, "mp"),
        P(None, "mp"),
        P("mp"),
        P("mp", None, None),
        P("mp"),
        P("mp", None, None),
        P("mp"),
        P("mp"),
        P(SEQ, "mp"),
        P("mp"),
        P("mp", None),
        P(SEQ, "mp"),
    )
    out_specs = (P(SEQ, "mp"), P(SEQ, "mp"))
    return jax.shard_map(
        shards, mesh=finer, in_specs=in_specs, out_specs=out_specs, check_vma=False
    )
```

time: 115 us -> 105 us (0.913)
  the two profiles are of different devices: /device:TPU:6 before, /device:TPU:32 now
where the time goes in v2:
time: 105 us; the launch traced here: 104 us
  starting transfers between devices  39.4 us (38%)
  Pallas kernels  32.1 us (31%)
  waiting for transfers between devices  28.8 us (27%)
  other arithmetic  2.45 us (2%)
    ppermute x9, starting transfers between devices, shifted(): lax.ppermute(value, SEQ, [(k, k + steps) for k in range(count - steps)])  27.7 us
    ppermute x9, waiting for transfers between devices, shifted(): lax.ppermute(value, SEQ, [(k, k + steps) for k in range(count - steps)])  19.8 us
    pallas_call x2, Pallas kernels, recur(): pl.pallas_call(recur_kernel, name='recur', grid=(count,), out_shape=[jax....  15.3 us
    pallas_call x2, Pallas kernels, attend(): pl.pallas_call(attend_kernel, name='attend', grid=(count,), out_shape=jax...  13.5 us
    ppermute x6, starting transfers between devices, turned(): lax.ppermute(value, 'mp', [(k, (k + steps) % PARTS) for k in range(PARTS)])  10.4 us
    ppermute x6, waiting for transfers between devices, turned(): lax.ppermute(value, 'mp', [(k, (k + steps) % PARTS) for k in range(PARTS)])  7.65 us
    pallas_call x1, Pallas kernels, project(): pl.pallas_call(project_kernel, name='project', out_shape=[jax.ShapeDtypeS...  3.07 us
  transfers between devices with their start and end apart: 20, of which 9 were waited for; matrix products, arithmetic and copies ran while one was open for 0% of the time, Pallas kernels for 31%

profile of v2, /device:TPU:32, one launch (start us, length us, event | category | flops | bytes accessed | tf_op | source)
XLA Modules:
  0.0 104.4 jit_solution(4436192148013393857)
XLA Ops:
  0.6 0.7 slice.62
  1.4 1.9 %collective-permute-start = (bf16[3,1024]{1,0:T(4,128)(2,1)S(1)}, bf16[3,1024]{1,0:T(4,128)(2,1)S(1)}, u32[]{:S(2)}, u32[]{:S(2)}) collective-permute-start(bf16[3,1024]{1,0:T(4,128)(2,1)S(1)} %slice.62), channel_id=1, source_target_pairs={{0,4},{4,8},{8,12},{12,16},{16,20},{20,24},{24,28},{28,32},{32,36}... | collective-permute-start | bytes 18440 | tf_op jit(solution)/shard_map/ppermute | solution.py:43
  3.3 3.1 %project.1 = (f32[144,512]{1,0:T(8,128)}, bf16[144,512]{1,0:T(8,128)(2,1)}, bf16[144,512]{1,0:T(8,128)(2,1)}, bf16[144,512]{1,0:T(8,128)(2,1)}) custom-call(s32[1]{0:T(128)} %bitcast.place, bf16[512,1024]{1,0:T(8,128)(2,1)} %stream.1, f32[1,1024]{1,0:T(1,128)} %bitcast.18, bf16[1024,512]{1,0:T(8,128)(2,1)} %weight.1), custom_call_target="tpu_custom_call" | custom-call | flops 536870912 | bytes 3145728 | tf_op jit(solution)/shard_map/project/pallas_call | solution.py:72
  6.4 2.1 %collective-permute-done.edge = bf16[3,1024]{1,0:T(4,128)(2,1)S(1)} collective-permute-done((bf16[3,1024]{1,0:T(4,128)(2,1)S(1)}, bf16[3,1024]{1,0:T(4,128)(2,1)S(1)}, u32[]{:S(2)}, u32[]{:S(2)}) %collective-permute-start) | collective-permute-done | bytes 6176 | tf_op jit(solution)/shard_map/ppermute | solution.py:43
  8.4 1.6 %collective-permute-start.1 = (bf16[144,512]{1,0:T(8,128)(2,1)}, bf16[144,512]{1,0:T(8,128)(2,1)S(1)}, u32[]{:S(2)}, u32[]{:S(2)}) collective-permute-start(bf16[144,512]{1,0:T(8,128)(2,1)} %get-tuple-element.44), channel_id=1, source_target_pairs={{0,1},{1,2},{2,3},{3,0},{4,5},{5,6},{6,7},{7,4},{8,9},{9,10},{10,1... | collective-permute-start | bytes 442376 | tf_op jit(solution)/shard_map/ppermute | solution.py:47
  10.0 2.9 %collective-permute-start.2 = (bf16[144,512]{1,0:T(8,128)(2,1)}, bf16[144,512]{1,0:T(8,128)(2,1)S(1)}, u32[]{:S(2)}, u32[]{:S(2)}) collective-permute-start(bf16[144,512]{1,0:T(8,128)(2,1)} %get-tuple-element.45), channel_id=1, source_target_pairs={{0,2},{1,3},{2,0},{3,1},{4,6},{5,7},{6,4},{7,5},{8,10},{9,11},{10,... | collective-permute-start | bytes 442376 | tf_op jit(solution)/shard_map/ppermute | solution.py:47
  12.9 1.3 %collective-permute-start.3 = (bf16[144,512]{1,0:T(8,128)(2,1)}, bf16[144,512]{1,0:T(8,128)(2,1)S(1)}, u32[]{:S(2)}, u32[]{:S(2)}) collective-permute-start(bf16[144,512]{1,0:T(8,128)(2,1)} %get-tuple-element.46), channel_id=1, source_target_pairs={{0,3},{1,0},{2,1},{3,2},{4,7},{5,4},{6,5},{7,6},{8,11},{9,8},{10,9... | collective-permute-start | bytes 442376 | tf_op jit(solution)/shard_map/ppermute | solution.py:47
  14.3 4.9 %recur.2 = (f32[512,1024]{1,0:T(8,128)}, f32[512,1024]{1,0:T(8,128)}, f32[2,1024]{1,0:T(2,128)}) custom-call(bf16[512,1024]{1,0:T(8,128)(2,1)} %branch.3, bf16[3,1024]{1,0:T(4,128)(2,1)} %copy-done.4, bf16[512,1024]{1,0:T(8,128)(2,1)} %gate.3, f32[4,1024]{1,0:T(4,128)} %taps.3, f32[1,1024]{1,0:T(1,128)} %bitcast.9, bf16[4,256,256]{2,1,0:T(8,128)(2,1)} %in_w.3, ...), custom_call_target="tpu_custom_call" | custom-call | flops 268435456 | bytes 2097152 | tf_op jit(solution)/shard_map/recur/pallas_call | solution.py:175
  19.2 0.0 collective-permute-done.1.b
  19.2 0.4 collective-permute-done.2.c
  19.6 0.0 collective-permute-done.3.d
  19.6 0.2 normed.1
  19.8 4.0 %collective-permute-start.5 = (bf16[128,512]{1,0:T(8,128)(2,1)S(1)}, bf16[128,512]{1,0:T(8,128)(2,1)S(1)}, u32[]{:S(2)}, u32[]{:S(2)}) collective-permute-start(bf16[128,512]{1,0:T(8,128)(2,1)S(1)} %normed.1), channel_id=1, source_target_pairs={{0,16},{4,20},{8,24},{12,28},{16,32},{20,36},{24,40},{28,44},{32,4... | collective-permute-start | bytes 393224 | tf_op jit(solution)/shard_map/ppermute | solution.py:43
  23.8 1.9 %collective-permute-start.4 = (bf16[128,512]{1,0:T(8,128)(2,1)S(1)}, bf16[128,512]{1,0:T(8,128)(2,1)S(1)}, u32[]{:S(2)}, u32[]{:S(2)}) collective-permute-start(bf16[128,512]{1,0:T(8,128)(2,1)S(1)} %normed.1), channel_id=1, source_target_pairs={{0,8},{4,12},{8,16},{12,20},{16,24},{20,28},{24,32},{28,36},{32,40... | collective-permute-start | bytes 393224 | tf_op jit(solution)/shard_map/ppermute | solution.py:43
  25.7 3.3 %collective-permute-done.5 = bf16[128,512]{1,0:T(8,128)(2,1)S(1)} collective-permute-done((bf16[128,512]{1,0:T(8,128)(2,1)S(1)}, bf16[128,512]{1,0:T(8,128)(2,1)S(1)}, u32[]{:S(2)}, u32[]{:S(2)}) %collective-permute-start.5) | collective-permute-done | bytes 131104 | tf_op jit(solution)/shard_map/ppermute | solution.py:43
  29.1 4.0 %collective-permute-done.4 = bf16[128,512]{1,0:T(8,128)(2,1)S(1)} collective-permute-done((bf16[128,512]{1,0:T(8,128)(2,1)S(1)}, bf16[128,512]{1,0:T(8,128)(2,1)S(1)}, u32[]{:S(2)}, u32[]{:S(2)}) %collective-permute-start.4) | collective-permute-done | bytes 131104 | tf_op jit(solution)/shard_map/ppermute | solution.py:43
  33.1 0.0 copy-start.5
  33.1 0.0 copy-start.1
  33.1 2.6 %collective-permute-start.8 = (bf16[384,512]{1,0:T(8,128)(2,1)S(1)}, bf16[384,512]{1,0:T(8,128)(2,1)S(1)}, u32[]{:S(2)}, u32[]{:S(2)}) collective-permute-start(bf16[384,512]{1,0:T(8,128)(2,1)S(1)} %pad_maximum_fusion.refs_0_), channel_id=1, source_target_pairs={{0,3},{1,0},{2,1},{3,2},{4,7},{5,4},{6,5},{7,6},{8,11},{9,8},{10,9... | collective-permute-start | bytes 1179656 | tf_op jit(solution)/shard_map/ppermute | solution.py:47
  35.8 1.3 %collective-permute-start.7 = (bf16[384,512]{1,0:T(8,128)(2,1)S(1)}, bf16[384,512]{1,0:T(8,128)(2,1)S(1)}, u32[]{:S(2)}, u32[]{:S(2)}) collective-permute-start(bf16[384,512]{1,0:T(8,128)(2,1)S(1)} %pad_maximum_fusion.refs_0_), channel_id=1, source_target_pairs={{0,2},{1,3},{2,0},{3,1},{4,6},{5,7},{6,4},{7,5},{8,10},{9,11},{10,... | collective-permute-start | bytes 1179656 | tf_op jit(solution)/shard_map/ppermute | solution.py:47
  37.0 0.7 collective-permute-start.6
  37.7 10.4 %recur.3 = (f32[512,1024]{1,0:T(8,128)}, f32[512,1024]{1,0:T(8,128)}, f32[2,1024]{1,0:T(2,128)}) custom-call(bf16[512,1024]{1,0:T(8,128)(2,1)} %branch.3, bf16[3,1024]{1,0:T(4,128)(2,1)} %copy-done.4, bf16[512,1024]{1,0:T(8,128)(2,1)} %gate.3, f32[4,1024]{1,0:T(4,128)} %taps.3, ...), custom_call_target="tpu_custom_call", output_to_operand_aliasing={{0}: (10, {}), {1}: (11, {}), {2}: (12, {})} | custom-call | flops 805306368 | bytes 6291456 | tf_op jit(solution)/shard_map/recur/pallas_call | solution.py:175
  48.1 3.6 %collective-permute-done.8.refs_3_ = bf16[384,512]{1,0:T(8,128)(2,1)S(1)} collective-permute-done((bf16[384,512]{1,0:T(8,128)(2,1)S(1)}, bf16[384,512]{1,0:T(8,128)(2,1)S(1)}, u32[]{:S(2)}, u32[]{:S(2)}) %collective-permute-start.8) | collective-permute-done | bytes 393248 | tf_op jit(solution)/shard_map/ppermute | solution.py:47
  51.7 0.0 collective-permute-done.7.refs_2_
  51.7 3.7 %collective-permute-done.6.refs_1_ = bf16[384,512]{1,0:T(8,128)(2,1)S(1)} collective-permute-done((bf16[384,512]{1,0:T(8,128)(2,1)S(1)}, bf16[384,512]{1,0:T(8,128)(2,1)S(1)}, u32[]{:S(2)}, u32[]{:S(2)}) %collective-permute-start.6) | collective-permute-done | bytes 393248 | tf_op jit(solution)/shard_map/ppermute | solution.py:47
  55.4 0.0 collective-permute-start.9
  55.4 1.4 %collective-permute-done.9 = f32[2,1024]{1,0:T(2,128)S(1)} collective-permute-done((f32[2,1024]{1,0:T(2,128)}, f32[2,1024]{1,0:T(2,128)S(1)}, u32[]{:S(2)}, u32[]{:S(2)}) %collective-permute-start.9) | collective-permute-done | bytes 8224 | tf_op jit(solution)/shard_map/ppermute | solution.py:51
  56.8 0.7 broadcast_select_fusion.2
  57.5 1.9 %collective-permute-start.10 = (f32[2,1024]{1,0:T(2,128)S(1)}, f32[2,1024]{1,0:T(2,128)S(1)}, u32[]{:S(2)}, u32[]{:S(2)}) collective-permute-start(f32[2,1024]{1,0:T(2,128)S(1)} %pad_maximum_fusion.1), channel_id=1, source_target_pairs={{0,8},{4,12},{8,16},{12,20},{16,24},{20,28},{24,32},{28,36},{32,40... | collective-permute-start | bytes 24584 | tf_op jit(solution)/shard_map/ppermute | solution.py:43
  59.5 0.4 collective-permute-start.13
  59.9 0.3 collective-permute-start.14
  60.2 0.2 collective-permute-start.15
  60.4 0.3 collective-permute-start.16
  60.7 4.4 %collective-permute-done.10 = f32[2,1024]{1,0:T(2,128)S(1)} collective-permute-done((f32[2,1024]{1,0:T(2,128)S(1)}, f32[2,1024]{1,0:T(2,128)S(1)}, u32[]{:S(2)}, u32[]{:S(2)}) %collective-permute-start.10) | collective-permute-done | bytes 8224 | tf_op jit(solution)/shard_map/ppermute | solution.py:43
  65.2 1.9 %collective-permute-start.11 = (f32[2,1024]{1,0:T(2,128)S(1)}, f32[2,1024]{1,0:T(2,128)S(1)}, u32[]{:S(2)}, u32[]{:S(2)}) collective-permute-start(f32[2,1024]{1,0:T(2,128)S(1)} %pad_maximum_fusion.2), channel_id=1, source_target_pairs={{0,16},{4,20},{8,24},{12,28},{16,32},{20,36},{24,40},{28,44},{32,4... | collective-permute-start | bytes 24584 | tf_op jit(solution)/shard_map/ppermute | solution.py:43
  67.1 0.1 pad_add_fusion.info
  67.2 5.9 %collective-permute-done.11 = f32[2,1024]{1,0:T(2,128)S(1)} collective-permute-done((f32[2,1024]{1,0:T(2,128)S(1)}, f32[2,1024]{1,0:T(2,128)S(1)}, u32[]{:S(2)}, u32[]{:S(2)}) %collective-permute-start.11) | collective-permute-done | bytes 8224 | tf_op jit(solution)/shard_map/ppermute | solution.py:43
  73.2 3.8 %collective-permute-start.12 = (f32[2,1024]{1,0:T(2,128)S(1)}, f32[2,1024]{1,0:T(2,128)S(1)}, u32[]{:S(2)}, u32[]{:S(2)}) collective-permute-start(f32[2,1024]{1,0:T(2,128)S(1)} %pad_maximum_fusion.3), channel_id=1, source_target_pairs={{0,32},{4,36},{8,40},{12,44},{16,48},{20,52},{24,56},{28,60},{32,6... | collective-permute-start | bytes 24584 | tf_op jit(solution)/shard_map/ppermute | solution.py:43
  77.0 0.0 collective-permute-done.13.refs_4_
  77.0 0.0 collective-permute-done.14.refs_5_
  77.1 0.0 collective-permute-done.15.refs_6_
  77.1 6.7 %attend.2.refs_8_ = bf16[512,1024]{1,0:T(8,128)(2,1)} custom-call(s32[3]{0:T(128)S(1)} %pad_add_fusion.info, bf16[512,1024]{1,0:T(8,128)(2,1)S(1)} %copy-done.1, bf16[384,512]{1,0:T(8,128)(2,1)S(1)} %pad_maximum_fusion.refs_0_, bf16[384,512]{1,0:T(8,128)(2,1)S(1)} %collective-permute-done.6.refs_1_, bf16[384,512]{1,0:T(8,128)(2,1)S(1)} %collective-permute-done.7.refs_2_, ...), custom_call_target="tpu_custom_call" | custom-call | flops 2147483648 | bytes 4194304 | tf_op jit(solution)/shard_map/attend/pallas_call | solution.py:268
  83.9 5.0 %collective-permute-start.19 = (f32[2,1024]{1,0:T(2,128)S(1)}, f32[2,1024]{1,0:T(2,128)S(1)}, u32[]{:S(2)}, u32[]{:S(2)}) collective-permute-start(f32[2,1024]{1,0:T(2,128)S(1)} %pad_maximum_fusion.4), channel_id=1, source_target_pairs={{0,192},{4,196},{8,200},{12,204},{16,208},{20,212},{24,216},{28,22... | collective-permute-start | bytes 24584 | tf_op jit(solution)/shard_map/ppermute | solution.py:43
  88.9 3.2 %collective-permute-start.18 = (f32[2,1024]{1,0:T(2,128)S(1)}, f32[2,1024]{1,0:T(2,128)S(1)}, u32[]{:S(2)}, u32[]{:S(2)}) collective-permute-start(f32[2,1024]{1,0:T(2,128)S(1)} %pad_maximum_fusion.4), channel_id=1, source_target_pairs={{0,128},{4,132},{8,136},{12,140},{16,144},{20,148},{24,152},{28,15... | collective-permute-start | bytes 24584 | tf_op jit(solution)/shard_map/ppermute | solution.py:43
  92.1 4.0 %collective-permute-start.17 = (f32[2,1024]{1,0:T(2,128)S(1)}, f32[2,1024]{1,0:T(2,128)S(1)}, u32[]{:S(2)}, u32[]{:S(2)}) collective-permute-start(f32[2,1024]{1,0:T(2,128)S(1)} %pad_maximum_fusion.4), channel_id=1, source_target_pairs={{0,64},{4,68},{8,72},{12,76},{16,80},{20,84},{24,88},{28,92},{32,9... | collective-permute-start | bytes 24584 | tf_op jit(solution)/shard_map/ppermute | solution.py:43
  96.1 6.7 %attend.3 = bf16[512,1024]{1,0:T(8,128)(2,1)} custom-call(s32[3]{0:T(128)S(1)} %pad_add_fusion.info, bf16[512,1024]{1,0:T(8,128)(2,1)S(1)} %copy-done.1, bf16[384,512]{1,0:T(8,128)(2,1)S(1)} %pad_maximum_fusion.refs_0_, bf16[384,512]{1,0:T(8,128)(2,1)S(1)} %collective-permute-done.6.refs_1_, ...), custom_call_target="tpu_custom_call", output_to_operand_aliasing={{}: (10, {})} | custom-call | flops 2147483648 | bytes 4194304 | tf_op jit(solution)/shard_map/attend/pallas_call | solution.py:268
  102.9 0.0 collective-permute-done.17
  102.9 1.5 %add_convert_fusion = bf16[512,1024]{1,0:T(8,128)(2,1)} fusion(f32[512,1024]{1,0:T(8,128)S(1)} %copy-done.2, f32[512,1024]{1,0:T(8,128)S(1)} %copy-done.3, f32[1024]{0:T(1024)S(1)} %bitcast.17), kind=kLoop, calls=%fused_computation | loop fusion | flops 1572864 | bytes 5246976 | tf_op jit(solution)/shard_map/convert_element_type | solution.py:355
  (24 shorter events, 0.2 us)
Async XLA Ops:
  1.4 7.1 %collective-permute-start = (bf16[3,1024]{1,0:T(4,128)(2,1)S(1)}, bf16[3,1024]{1,0:T(4,128)(2,1)S(1)}, u32[]{:S(2)}, u32[]{:S(2)}) collective-permute-start(bf16[3,1024]{1,0:T(4,128)(2,1)S(1)} %slice.62), channel_id=1, source_target_pairs={{0,4},{4,8},{8,12},{12,16},{16,20},{20,24},{24,28},{28,32},{32,36}... | collective-permute-start | bytes 18440 | tf_op jit(solution)/shard_map/ppermute | solution.py:43
  6.3 13.3 %copy-start = (f32[144,512]{1,0:T(8,128)S(1)}, f32[144,512]{1,0:T(8,128)}, u32[]{:S(2)}) copy-start(f32[144,512]{1,0:T(8,128)} %get-tuple-element.43.a) | copy-start | bytes 884740
  8.4 5.8 %copy-start.4 = (bf16[3,1024]{1,0:T(4,128)(2,1)}, bf16[3,1024]{1,0:T(4,128)(2,1)S(1)}, u32[]{:S(2)}) copy-start(bf16[3,1024]{1,0:T(4,128)(2,1)S(1)} %collective-permute-done.edge) | copy-start | bytes 18436
  8.4 10.8 %collective-permute-start.1 = (bf16[144,512]{1,0:T(8,128)(2,1)}, bf16[144,512]{1,0:T(8,128)(2,1)S(1)}, u32[]{:S(2)}, u32[]{:S(2)}) collective-permute-start(bf16[144,512]{1,0:T(8,128)(2,1)} %get-tuple-element.44), channel_id=1, source_target_pairs={{0,1},{1,2},{2,3},{3,0},{4,5},{5,6},{6,7},{7,4},{8,9},{9,10},{10,1... | collective-permute-start | bytes 442376 | tf_op jit(solution)/shard_map/ppermute | solution.py:47
  10.0 9.6 %collective-permute-start.2 = (bf16[144,512]{1,0:T(8,128)(2,1)}, bf16[144,512]{1,0:T(8,128)(2,1)S(1)}, u32[]{:S(2)}, u32[]{:S(2)}) collective-permute-start(bf16[144,512]{1,0:T(8,128)(2,1)} %get-tuple-element.45), channel_id=1, source_target_pairs={{0,2},{1,3},{2,0},{3,1},{4,6},{5,7},{6,4},{7,5},{8,10},{9,11},{10,... | collective-permute-start | bytes 442376 | tf_op jit(solution)/shard_map/ppermute | solution.py:47
  12.9 6.7 %collective-permute-start.3 = (bf16[144,512]{1,0:T(8,128)(2,1)}, bf16[144,512]{1,0:T(8,128)(2,1)S(1)}, u32[]{:S(2)}, u32[]{:S(2)}) collective-permute-start(bf16[144,512]{1,0:T(8,128)(2,1)} %get-tuple-element.46), channel_id=1, source_target_pairs={{0,3},{1,0},{2,1},{3,2},{4,7},{5,4},{6,5},{7,6},{8,11},{9,8},{10,9... | collective-permute-start | bytes 442376 | tf_op jit(solution)/shard_map/ppermute | solution.py:47
  19.8 9.3 %collective-permute-start.5 = (bf16[128,512]{1,0:T(8,128)(2,1)S(1)}, bf16[128,512]{1,0:T(8,128)(2,1)S(1)}, u32[]{:S(2)}, u32[]{:S(2)}) collective-permute-start(bf16[128,512]{1,0:T(8,128)(2,1)S(1)} %normed.1), channel_id=1, source_target_pairs={{0,16},{4,20},{8,24},{12,28},{16,32},{20,36},{24,40},{28,44},{32,4... | collective-permute-start | bytes 393224 | tf_op jit(solution)/shard_map/ppermute | solution.py:43
  23.8 9.3 %collective-permute-start.4 = (bf16[128,512]{1,0:T(8,128)(2,1)S(1)}, bf16[128,512]{1,0:T(8,128)(2,1)S(1)}, u32[]{:S(2)}, u32[]{:S(2)}) collective-permute-start(bf16[128,512]{1,0:T(8,128)(2,1)S(1)} %normed.1), channel_id=1, source_target_pairs={{0,8},{4,12},{8,16},{12,20},{16,24},{20,28},{24,32},{28,36},{32,40... | collective-permute-start | bytes 393224 | tf_op jit(solution)/shard_map/ppermute | solution.py:43
  33.1 23.7 %copy-start.5 = (f32[2,1024]{1,0:T(2,128)S(1)}, f32[2,1024]{1,0:T(2,128)}, u32[]{:S(2)}) copy-start(f32[2,1024]{1,0:T(2,128)} %constant.24.clone.1) | copy-start | bytes 24580
  33.1 44.0 %copy-start.1 = (bf16[512,1024]{1,0:T(8,128)(2,1)S(1)}, bf16[512,1024]{1,0:T(8,128)(2,1)}, u32[]{:S(2)}) copy-start(bf16[512,1024]{1,0:T(8,128)(2,1)} %q_ref.3) | copy-start | bytes 3145732
  33.1 18.6 %collective-permute-start.8 = (bf16[384,512]{1,0:T(8,128)(2,1)S(1)}, bf16[384,512]{1,0:T(8,128)(2,1)S(1)}, u32[]{:S(2)}, u32[]{:S(2)}) collective-permute-start(bf16[384,512]{1,0:T(8,128)(2,1)S(1)} %pad_maximum_fusion.refs_0_), channel_id=1, source_target_pairs={{0,3},{1,0},{2,1},{3,2},{4,7},{5,4},{6,5},{7,6},{8,11},{9,8},{10,9... | collective-permute-start | bytes 1179656 | tf_op jit(solution)/shard_map/ppermute | solution.py:47
  35.8 15.9 %collective-permute-start.7 = (bf16[384,512]{1,0:T(8,128)(2,1)S(1)}, bf16[384,512]{1,0:T(8,128)(2,1)S(1)}, u32[]{:S(2)}, u32[]{:S(2)}) collective-permute-start(bf16[384,512]{1,0:T(8,128)(2,1)S(1)} %pad_maximum_fusion.refs_0_), channel_id=1, source_target_pairs={{0,2},{1,3},{2,0},{3,1},{4,6},{5,7},{6,4},{7,5},{8,10},{9,11},{10,... | collective-permute-start | bytes 1179656 | tf_op jit(solution)/shard_map/ppermute | solution.py:47
  37.0 18.3 %collective-permute-start.6 = (bf16[384,512]{1,0:T(8,128)(2,1)S(1)}, bf16[384,512]{1,0:T(8,128)(2,1)S(1)}, u32[]{:S(2)}, u32[]{:S(2)}) collective-permute-start(bf16[384,512]{1,0:T(8,128)(2,1)S(1)} %pad_maximum_fusion.refs_0_), channel_id=1, source_target_pairs={{0,1},{1,2},{2,3},{3,0},{4,5},{5,6},{6,7},{7,4},{8,9},{9,10},{10,1... | collective-permute-start | bytes 1179656 | tf_op jit(solution)/shard_map/ppermute | solution.py:47
  55.4 1.4 %collective-permute-start.9 = (f32[2,1024]{1,0:T(2,128)}, f32[2,1024]{1,0:T(2,128)S(1)}, u32[]{:S(2)}, u32[]{:S(2)}) collective-permute-start(f32[2,1024]{1,0:T(2,128)} %get-tuple-element.55), channel_id=1, source_target_pairs={{0,4},{4,0},{1,5},{5,1},{2,6},{6,2},{3,7},{7,3},{8,12},{12,8},{9,1... | collective-permute-start | bytes 24584 | tf_op jit(solution)/shard_map/ppermute | solution.py:51
  57.5 7.7 %collective-permute-start.10 = (f32[2,1024]{1,0:T(2,128)S(1)}, f32[2,1024]{1,0:T(2,128)S(1)}, u32[]{:S(2)}, u32[]{:S(2)}) collective-permute-start(f32[2,1024]{1,0:T(2,128)S(1)} %pad_maximum_fusion.1), channel_id=1, source_target_pairs={{0,8},{4,12},{8,16},{12,20},{16,24},{20,28},{24,32},{28,36},{32,40... | collective-permute-start | bytes 24584 | tf_op jit(solution)/shard_map/ppermute | solution.py:43
  59.5 17.6 %collective-permute-start.13 = (bf16[384,512]{1,0:T(8,128)(2,1)S(1)}, bf16[384,512]{1,0:T(8,128)(2,1)S(1)}, u32[]{:S(2)}, u32[]{:S(2)}) collective-permute-start(bf16[384,512]{1,0:T(8,128)(2,1)S(1)} %pad_maximum_fusion.refs_0_), channel_id=1, source_target_pairs={{0,4},{4,0},{1,5},{5,1},{2,6},{6,2},{3,7},{7,3},{8,12},{12,8},{9,1... | collective-permute-start | bytes 1179656 | tf_op jit(solution)/shard_map/ppermute | solution.py:51
  59.9 17.2 %collective-permute-start.14 = (bf16[384,512]{1,0:T(8,128)(2,1)S(1)}, bf16[384,512]{1,0:T(8,128)(2,1)S(1)}, u32[]{:S(2)}, u32[]{:S(2)}) collective-permute-start(bf16[384,512]{1,0:T(8,128)(2,1)S(1)} %collective-permute-done.6.refs_1_), channel_id=1, source_target_pairs={{0,4},{4,0},{1,5},{5,1},{2,6},{6,2},{3,7},{7,3},{8,12},{12,8},{9,1... | collective-permute-start | bytes 1179656 | tf_op jit(solution)/shard_map/ppermute | solution.py:51
  60.2 16.8 %collective-permute-start.15 = (bf16[384,512]{1,0:T(8,128)(2,1)S(1)}, bf16[384,512]{1,0:T(8,128)(2,1)S(1)}, u32[]{:S(2)}, u32[]{:S(2)}) collective-permute-start(bf16[384,512]{1,0:T(8,128)(2,1)S(1)} %collective-permute-done.7.refs_2_), channel_id=1, source_target_pairs={{0,4},{4,0},{1,5},{5,1},{2,6},{6,2},{3,7},{7,3},{8,12},{12,8},{9,1... | collective-permute-start | bytes 1179656 | tf_op jit(solution)/shard_map/ppermute | solution.py:51
  60.4 16.7 %collective-permute-start.16 = (bf16[384,512]{1,0:T(8,128)(2,1)S(1)}, bf16[384,512]{1,0:T(8,128)(2,1)S(1)}, u32[]{:S(2)}, u32[]{:S(2)}) collective-permute-start(bf16[384,512]{1,0:T(8,128)(2,1)S(1)} %collective-permute-done.8.refs_3_), channel_id=1, source_target_pairs={{0,4},{4,0},{1,5},{5,1},{2,6},{6,2},{3,7},{7,3},{8,12},{12,8},{9,1... | collective-permute-start | bytes 1179656 | tf_op jit(solution)/shard_map/ppermute | solution.py:51
  65.2 7.9 %collective-permute-start.11 = (f32[2,1024]{1,0:T(2,128)S(1)}, f32[2,1024]{1,0:T(2,128)S(1)}, u32[]{:S(2)}, u32[]{:S(2)}) collective-permute-start(f32[2,1024]{1,0:T(2,128)S(1)} %pad_maximum_fusion.2), channel_id=1, source_target_pairs={{0,16},{4,20},{8,24},{12,28},{16,32},{20,36},{24,40},{28,44},{32,4... | collective-permute-start | bytes 24584 | tf_op jit(solution)/shard_map/ppermute | solution.py:43
  73.2 10.6 %collective-permute-start.12 = (f32[2,1024]{1,0:T(2,128)S(1)}, f32[2,1024]{1,0:T(2,128)S(1)}, u32[]{:S(2)}, u32[]{:S(2)}) collective-permute-start(f32[2,1024]{1,0:T(2,128)S(1)} %pad_maximum_fusion.3), channel_id=1, source_target_pairs={{0,32},{4,36},{8,40},{12,44},{16,48},{20,52},{24,56},{28,60},{32,6... | collective-permute-start | bytes 24584 | tf_op jit(solution)/shard_map/ppermute | solution.py:43
  83.9 19.1 %copy-start.2 = (f32[512,1024]{1,0:T(8,128)S(1)}, f32[512,1024]{1,0:T(8,128)}, u32[]{:S(2)}) copy-start(f32[512,1024]{1,0:T(8,128)} %get-tuple-element.51) | copy-start | bytes 6291460
  83.9 19.1 %copy-start.3 = (f32[512,1024]{1,0:T(8,128)S(1)}, f32[512,1024]{1,0:T(8,128)}, u32[]{:S(2)}) copy-start(f32[512,1024]{1,0:T(8,128)} %get-tuple-element.52) | copy-start | bytes 6291460
  83.9 19.0 %collective-permute-start.19 = (f32[2,1024]{1,0:T(2,128)S(1)}, f32[2,1024]{1,0:T(2,128)S(1)}, u32[]{:S(2)}, u32[]{:S(2)}) collective-permute-start(f32[2,1024]{1,0:T(2,128)S(1)} %pad_maximum_fusion.4), channel_id=1, source_target_pairs={{0,192},{4,196},{8,200},{12,204},{16,208},{20,212},{24,216},{28,22... | collective-permute-start | bytes 24584 | tf_op jit(solution)/shard_map/ppermute | solution.py:43
  88.9 14.0 %collective-permute-start.18 = (f32[2,1024]{1,0:T(2,128)S(1)}, f32[2,1024]{1,0:T(2,128)S(1)}, u32[]{:S(2)}, u32[]{:S(2)}) collective-permute-start(f32[2,1024]{1,0:T(2,128)S(1)} %pad_maximum_fusion.4), channel_id=1, source_target_pairs={{0,128},{4,132},{8,136},{12,140},{16,144},{20,148},{24,152},{28,15... | collective-permute-start | bytes 24584 | tf_op jit(solution)/shard_map/ppermute | solution.py:43
  92.1 10.8 %collective-permute-start.17 = (f32[2,1024]{1,0:T(2,128)S(1)}, f32[2,1024]{1,0:T(2,128)S(1)}, u32[]{:S(2)}, u32[]{:S(2)}) collective-permute-start(f32[2,1024]{1,0:T(2,128)S(1)} %pad_maximum_fusion.4), channel_id=1, source_target_pairs={{0,64},{4,68},{8,72},{12,76},{16,80},{20,84},{24,88},{28,92},{32,9... | collective-permute-start | bytes 24584 | tf_op jit(solution)/shard_map/ppermute | solution.py:43

commit v3 on v2

--- a/solution.py
+++ b/solution.py
@@ -20,6 +20,7 @@
 PARTS = 4
 SEGMENTS = 8
 STEPS = TOK // SEGMENTS
+PITCH = STEPS + 1
 QROWS = 256
 LANES = 128
 EXTRA = 16
@@ -80,25 +81,101 @@
     )(place, stream, gain, weight)
 
 
-def norm_kernel(a, b, c, d, out):
+def split(value):
+    high = value.astype(BF16).astype(F32)
+    rest = value - high
+    middle = rest.astype(BF16).astype(F32)
+    return (high, middle, rest - middle)
+
+
+def norm_kernel(info, a, b, c, d, couple, other, out, before, inclusive):
     total = (a[...] + b[...].astype(F32)) + (c[...].astype(F32) + d[...].astype(F32))
     line = total[QUARTER : QUARTER + 1, 0:QUARTER] + total[QUARTER + 1 : QUARTER + 2, 0:QUARTER]
     column = jnp.broadcast_to(line, (QUARTER, QUARTER)).T[:, 0:1]
     root = jnp.sqrt(column / D + norm_epsilon)
-    out[...] = (total[0:QUARTER] / root).astype(BF16)
-
-
-def normed(parts):
-    shape = (QUARTER, 2 * HD)
+    out[0:QUARTER, :] = (total[0:QUARTER] / root).astype(BF16)
+    first = info[0] == 0
+    mine, theirs = (couple[...], other[...])
+    earlier = jnp.where(first, mine, theirs)
+    later = jnp.where(first, theirs, mine)
+    factor = earlier[0:1] * later[0:1]
+    state = later[0:1] * earlier[1:2] + later[1:2]
+    inclusive[0:1, :] = factor
+    inclusive[1:2, :] = state
+    before[0:1, :] = jnp.where(first, jnp.ones_like(factor), theirs[0:1])
+    before[1:2, :] = jnp.where(first, jnp.zeros_like(state), theirs[1:2])
+    width = 2 * HD
+    lines = [
+        part[:, k : k + width]
+        for value in (factor, state)
+        for part in split(value)
+        for k in range(0, value.shape[1], width)
+    ]
+    lines += [jnp.zeros((1, width), F32)] * (EXTRA - len(lines))
+    out[QUARTER:, :] = jnp.concatenate(lines).astype(BF16)
+
+
+def normed(info, parts, couple, other):
+    shape = parts[0].shape
     return pl.pallas_call(
         norm_kernel,
         name="normed",
-        out_shape=jax.ShapeDtypeStruct(shape, BF16),
-        in_specs=[whole(parts[0].shape)] * PARTS,
-        out_specs=whole(shape),
+        out_shape=[
+            jax.ShapeDtypeStruct(shape, BF16),
+            jax.ShapeDtypeStruct(couple.shape, F32),
+            jax.ShapeDtypeStruct(couple.shape, F32),
+        ],
+        in_specs=[SMEM] + [whole(shape)] * PARTS + [whole(couple.shape)] * 2,
+        out_specs=[whole(shape), whole(couple.shape), whole(couple.shape)],
         compiler_params=pltpu.CompilerParams(vmem_limit_bytes=8 << 20),
         cost_estimate=pl.CostEstimate(flops=1 << 20, bytes_accessed=5 << 17, transcendentals=0),
-    )(*parts)
+    )(info, *parts, couple, other)
+
+
+def received(lines, channels):
+    values = []
+    width = 2 * HD
+    per = channels // width
+    for value in range(2):
+        halves = []
+        for k in range(per):
+            at = [value * 3 * per + part * per + k for part in range(3)]
+            high, middle, low = [lines[row : row + 1] for row in at]
+            halves.append(high + (middle + low))
+        values.append(jnp.concatenate(halves, axis=1))
+    return values
+
+
+def window_kernel(mine, back2, back4, before, inclusive, trio, before_out, inclusive_out):
+    channels = before.shape[1]
+    passed = (before[0:1, :], before[1:2, :])
+    whole_chip = (inclusive[0:1, :], inclusive[1:2, :])
+    trio[0:QUARTER, :] = mine[0:QUARTER, :]
+    for k, ref in enumerate((back2, back4)):
+        trio[(k + 1) * QUARTER : (k + 2) * QUARTER, :] = ref[0:QUARTER, :]
+        factor, state = received(ref[QUARTER:, :].astype(F32), channels)
+        passed = (factor * passed[0], passed[0] * state + passed[1])
+        whole_chip = (factor * whole_chip[0], whole_chip[0] * state + whole_chip[1])
+    before_out[0:1, :], before_out[1:2, :] = passed
+    inclusive_out[0:1, :], inclusive_out[1:2, :] = whole_chip
+
+
+def window(mine, back2, back4, before, inclusive):
+    shape = (3 * QUARTER, 2 * HD)
+    couple = whole(before.shape)
+    return pl.pallas_call(
+        window_kernel,
+        name="window",
+        out_shape=[
+            jax.ShapeDtypeStruct(shape, BF16),
+            jax.ShapeDtypeStruct(before.shape, F32),
+            jax.ShapeDtypeStruct(before.shape, F32),
+        ],
+        in_specs=[whole(mine.shape)] * 3 + [couple] * 2,
+        out_specs=[whole(shape), couple, couple],
+        compiler_params=pltpu.CompilerParams(vmem_limit_bytes=8 << 20),
+        cost_estimate=pl.CostEstimate(flops=1 << 14, bytes_accessed=3 << 18, transcendentals=0),
+    )(mine, back2, back4, before, inclusive)
 
 
 def negative_expm1(y, grown):
@@ -135,14 +212,17 @@
     )
     for lane in range(BLK // LANES):
         there = slice(lane * LANES, (lane + 1) * LANES)
-        factors[lane] = factor[:, there]
-        pushes[lane] = push[:, there]
+        for r in range(SEGMENTS):
+            rows = slice(r * STEPS, (r + 1) * STEPS)
+            kept = slice(r * PITCH, r * PITCH + STEPS)
+            factors[lane, kept, :] = factor[rows, there]
+            pushes[lane, kept, :] = push[rows, there]
 
     lanes = range(BLK // LANES)
     product = [jnp.ones((SEGMENTS, LANES), F32) for _ in lanes]
     state = [jnp.zeros((SEGMENTS, LANES), F32) for _ in lanes]
     for t in range(STEPS):
-        rows = pl.ds(t, SEGMENTS, stride=STEPS)
+        rows = pl.ds(t, SEGMENTS, stride=PITCH)
         for lane in lanes:
             f = factors[lane, rows, :]
             state[lane] = f * state[lane] + pushes[lane, rows, :]
@@ -157,8 +237,9 @@
             rows = slice(r * STEPS, (r + 1) * STEPS)
             g = gate[rows, there].astype(F32)
             g = 0.5 * g * (1.0 + jnp.tanh(0.7978845608028654 * (g + 0.044715 * (g * g * g))))
-            local_f = factors[lane, rows, :]
-            u_out[rows, there] = (pushes[lane, rows, :] + local_f * before_s) * g
+            kept = slice(r * PITCH, r * PITCH + STEPS)
+            local_f = factors[lane, kept, :]
+            u_out[rows, there] = (pushes[lane, kept, :] + local_f * before_s) * g
             w_out[rows, there] = (local_f * before_f) * g
             before_s = product[lane][r : r + 1] * before_s + state[lane][r : r + 1]
             before_f = product[lane][r : r + 1] * before_f
@@ -188,8 +269,8 @@
         out_specs=[lane(TOK), lane(TOK), lane(2)],
         scratch_shapes=[
             pltpu.VMEM((TOK + 8, BLK), F32),
-            pltpu.VMEM((BLK // LANES, TOK, LANES), F32),
-            pltpu.VMEM((BLK // LANES, TOK, LANES), F32),
+            pltpu.VMEM((BLK // LANES, SEGMENTS * PITCH, LANES), F32),
+            pltpu.VMEM((BLK // LANES, SEGMENTS * PITCH, LANES), F32),
         ],
         input_output_aliases={len(inputs) + k: k for k in range(len(filled))},
         compiler_params=pltpu.CompilerParams(vmem_limit_bytes=ROOM),
@@ -285,18 +366,6 @@
     return jnp.stack([earlier[0] * later[0], later[0] * earlier[1] + later[1]])
 
 
-def near_prefix(couple, core):
-    other = swapped(couple)
-    first = core == 0
-    inclusive = compose(jnp.where(first, couple, other), jnp.where(first, other, couple))
-    empty = jnp.stack([jnp.ones_like(couple[0]), jnp.zeros_like(couple[0])])
-    return jnp.where(first, empty, other), inclusive
-
-
-def doubled(before, inclusive, arrived):
-    return compose(arrived, before), compose(arrived, inclusive)
-
-
 def shards(
     branch_in,
     branch_gate,
@@ -328,30 +397,24 @@
         decay_weight, line(decay_bias), line(decay_param),
     )
     groups = branch_in.shape[1] // BLK
-    early = groups // 4
-    filled = recur(0, early, branch_in, edge, *rest, ())
-    own_part, *filled = lax.optimization_barrier((parts[0], *filled))
-    quarter = normed([own_part] + arrived)
-    trio = jnp.concatenate([quarter, shifted(quarter, 2), shifted(quarter, 4)])
-    trio, edge = lax.optimization_barrier((trio, edge))
+    u, w, couple = recur(0, groups, branch_in, edge, *rest, ())
+    mine, before, inclusive = normed(info, [parts[0]] + arrived, couple, swapped(couple))
+    trio, before, inclusive = window(
+        mine, shifted(mine, 2), shifted(mine, 4), before, inclusive
+    )
     own = [trio] + [turned(trio, k) for k in range(1, PARTS)]
-    u, w, couple = recur(early, groups - early, branch_in, edge, *rest, filled)
-    couple, *own = lax.optimization_barrier((couple, *own))
-    before, inclusive = near_prefix(couple, core)
-    before, inclusive = doubled(before, inclusive, shifted(inclusive, 2))
+    far = [shifted(inclusive, 6 * k) for k in (1, 2, 3)]
+    *far, own[1], own[2], own[3] = lax.optimization_barrier((*far, *own[1:]))
+    for couple in far:
+        before = compose(couple, before)
+        inclusive = compose(couple, inclusive)
     other = [swapped(piece) for piece in own]
-    before, inclusive = doubled(before, inclusive, shifted(inclusive, 4))
+    far = [shifted(inclusive, 24 * k) for k in (1, 2)]
     heads = queries.shape[1] // HD
-    half = heads // 2
-    arrived = shifted(inclusive, 8)
-    attended = attend(0, half, info, queries, own, other, ())
-    arrived, attended = lax.optimization_barrier((arrived, attended))
-    before, inclusive = doubled(before, inclusive, arrived)
-    arrived = [shifted(inclusive, 16 * k) for k in range(1, 4)]
-    attended = attend(half, heads - half, info, queries, own, other, (attended,))
-    *arrived, attended = lax.optimization_barrier((*arrived, attended))
-    for piece in arrived:
-        before = compose(piece, before)
+    attended = attend(0, heads, info, queries, own, other, ())
+    *far, attended = lax.optimization_barrier((*far, attended))
+    for couple in far:
+        before = compose(couple, before)
     recurrent_out = (u + w * before[1:2]).astype(BF16)
     return (recurrent_out, attended)
 

time: 105 us -> 88.3 us (0.84)
  the two profiles are of different devices: /device:TPU:32 before, /device:TPU:33 now
where the time goes in v3:
time: 88.3 us; the launch traced here: 87.8 us
  starting transfers between devices  52.4 us (59%)
  Pallas kernels  24.9 us (28%)
  waiting for transfers between devices  6.56 us (7%)
  other arithmetic  1.63 us (2%)
  local copies, waits for them, and re-layouts  1.44 us (2%)
    ppermute x8, starting transfers between devices, shifted(): lax.ppermute(value, SEQ, [(k, k + steps) for k in range(count - steps)])  38 us
    pallas_call x1, Pallas kernels, attend(): pl.pallas_call(attend_kernel, name='attend', grid=(count,), out_shape=jax...  12.1 us
    pallas_call x1, Pallas kernels, recur(): pl.pallas_call(recur_kernel, name='recur', grid=(count,), out_shape=[jax....  8.98 us
    ppermute x6, starting transfers between devices, turned(): lax.ppermute(value, 'mp', [(k, (k + steps) % PARTS) for k in range(PARTS)])  8.02 us
    ppermute x5, starting transfers between devices, swapped(): return lax.ppermute(value, CORE, [(0, 1), (1, 0)])  6.37 us
    ppermute x8, waiting for transfers between devices, shifted(): lax.ppermute(value, SEQ, [(k, k + steps) for k in range(count - steps)])  5.57 us
    pallas_call x1, Pallas kernels, project(): pl.pallas_call(project_kernel, name='project', out_shape=[jax.ShapeDtypeS...  3.05 us
  transfers between devices with their start and end apart: 19, of which 3 were waited for; matrix products, arithmetic and copies ran while one was open for 0% of the time, Pallas kernels for 27%

profile of v3, /device:TPU:33, one launch (start us, length us, event | category | flops | bytes accessed | tf_op | source)
XLA Modules:
  0.0 87.8 jit_solution(10770363397691871172)
XLA Ops:
  0.6 0.7 slice.50
  1.4 3.7 %collective-permute-start = (bf16[3,1024]{1,0:T(4,128)(2,1)S(1)}, bf16[3,1024]{1,0:T(4,128)(2,1)S(1)}, u32[]{:S(2)}, u32[]{:S(2)}) collective-permute-start(bf16[3,1024]{1,0:T(4,128)(2,1)S(1)} %slice.50), channel_id=1, source_target_pairs={{0,4},{4,8},{8,12},{12,16},{16,20},{20,24},{24,28},{28,32},{32,36}... | collective-permute-start | bytes 18440 | tf_op jit(solution)/shard_map/ppermute | solution.py:44
  5.0 3.1 %project.1 = (f32[144,512]{1,0:T(8,128)}, bf16[144,512]{1,0:T(8,128)(2,1)}, bf16[144,512]{1,0:T(8,128)(2,1)}, bf16[144,512]{1,0:T(8,128)(2,1)}) custom-call(s32[1]{0:T(128)} %bitcast.place, bf16[512,1024]{1,0:T(8,128)(2,1)} %stream.1, f32[1,1024]{1,0:T(1,128)} %bitcast.10, bf16[1024,512]{1,0:T(8,128)(2,1)} %weight.1), custom_call_target="tpu_custom_call" | custom-call | flops 536870912 | bytes 3145728 | tf_op jit(solution)/shard_map/project/pallas_call | solution.py:73
  8.1 0.0 collective-permute-done.edge
  8.1 1.4 %collective-permute-start.1 = (bf16[144,512]{1,0:T(8,128)(2,1)}, bf16[144,512]{1,0:T(8,128)(2,1)S(1)}, u32[]{:S(2)}, u32[]{:S(2)}) collective-permute-start(bf16[144,512]{1,0:T(8,128)(2,1)} %get-tuple-element.37), channel_id=1, source_target_pairs={{0,1},{1,2},{2,3},{3,0},{4,5},{5,6},{6,7},{7,4},{8,9},{9,10},{10,1... | collective-permute-start | bytes 442376 | tf_op jit(solution)/shard_map/ppermute | solution.py:48
  9.5 2.6 %collective-permute-start.2 = (bf16[144,512]{1,0:T(8,128)(2,1)}, bf16[144,512]{1,0:T(8,128)(2,1)S(1)}, u32[]{:S(2)}, u32[]{:S(2)}) collective-permute-start(bf16[144,512]{1,0:T(8,128)(2,1)} %get-tuple-element.38), channel_id=1, source_target_pairs={{0,2},{1,3},{2,0},{3,1},{4,6},{5,7},{6,4},{7,5},{8,10},{9,11},{10,... | collective-permute-start | bytes 442376 | tf_op jit(solution)/shard_map/ppermute | solution.py:48
  12.1 1.1 %collective-permute-start.3 = (bf16[144,512]{1,0:T(8,128)(2,1)}, bf16[144,512]{1,0:T(8,128)(2,1)S(1)}, u32[]{:S(2)}, u32[]{:S(2)}) collective-permute-start(bf16[144,512]{1,0:T(8,128)(2,1)} %get-tuple-element.39), channel_id=1, source_target_pairs={{0,3},{1,0},{2,1},{3,2},{4,7},{5,4},{6,5},{7,6},{8,11},{9,8},{10,9... | collective-permute-start | bytes 442376 | tf_op jit(solution)/shard_map/ppermute | solution.py:48
  13.2 9.0 %recur.1 = (f32[512,1024]{1,0:T(8,128)}, f32[512,1024]{1,0:T(8,128)}, f32[2,1024]{1,0:T(2,128)}) custom-call(bf16[512,1024]{1,0:T(8,128)(2,1)} %branch.1, bf16[3,1024]{1,0:T(4,128)(2,1)} %copy-done.5, bf16[512,1024]{1,0:T(8,128)(2,1)} %gate.1, f32[4,1024]{1,0:T(4,128)} %taps.1, f32[1,1024]{1,0:T(1,128)} %bitcast.11, bf16[4,256,256]{2,1,0:T(8,128)(2,1)} %in_w.1, ...), custom_call_target="tpu_custom_call" | custom-call | flops 1073741824 | bytes 8388608 | tf_op jit(solution)/shard_map/recur/pallas_call | solution.py:256
  22.1 1.9 %collective-permute-start.4 = (f32[2,1024]{1,0:T(2,128)}, f32[2,1024]{1,0:T(2,128)S(1)}, u32[]{:S(2)}, u32[]{:S(2)}) collective-permute-start(f32[2,1024]{1,0:T(2,128)} %get-tuple-element.40.couple), channel_id=1, source_target_pairs={{0,4},{4,0},{1,5},{5,1},{2,6},{6,2},{3,7},{7,3},{8,12},{12,8},{9,1... | collective-permute-start | bytes 24584 | tf_op jit(solution)/shard_map/ppermute | solution.py:52
  24.0 0.1 pad_add_fusion.info
  24.1 1.0 %collective-permute-done.4.other = f32[2,1024]{1,0:T(2,128)S(1)} collective-permute-done((f32[2,1024]{1,0:T(2,128)}, f32[2,1024]{1,0:T(2,128)S(1)}, u32[]{:S(2)}, u32[]{:S(2)}) %collective-permute-start.4) | collective-permute-done | bytes 8224 | tf_op jit(solution)/shard_map/ppermute | solution.py:52
  25.0 0.0 collective-permute-done.1.b
  25.0 0.0 collective-permute-done.2.c
  25.1 0.0 collective-permute-done.3.d
  25.1 0.0 copy-done
  25.1 0.7 copy-done.1
  25.8 0.7 normed.1
  26.5 1.9 %collective-permute-start.5 = (bf16[144,512]{1,0:T(8,128)(2,1)S(1)}, bf16[144,512]{1,0:T(8,128)(2,1)S(1)}, u32[]{:S(2)}, u32[]{:S(2)}) collective-permute-start(bf16[144,512]{1,0:T(8,128)(2,1)S(1)} %get-tuple-element.41.mine), channel_id=1, source_target_pairs={{0,8},{4,12},{8,16},{12,20},{16,24},{20,28},{24,32},{28,36},{32,40... | collective-permute-start | bytes 442376 | tf_op jit(solution)/shard_map/ppermute | solution.py:44
  28.4 4.5 %collective-permute-start.6 = (bf16[144,512]{1,0:T(8,128)(2,1)S(1)}, bf16[144,512]{1,0:T(8,128)(2,1)S(1)}, u32[]{:S(2)}, u32[]{:S(2)}) collective-permute-start(bf16[144,512]{1,0:T(8,128)(2,1)S(1)} %get-tuple-element.41.mine), channel_id=1, source_target_pairs={{0,16},{4,20},{8,24},{12,28},{16,32},{20,36},{24,40},{28,44},{32,4... | collective-permute-start | bytes 442376 | tf_op jit(solution)/shard_map/ppermute | solution.py:44
  32.9 2.7 %collective-permute-done.5.back2 = bf16[144,512]{1,0:T(8,128)(2,1)S(1)} collective-permute-done((bf16[144,512]{1,0:T(8,128)(2,1)S(1)}, bf16[144,512]{1,0:T(8,128)(2,1)S(1)}, u32[]{:S(2)}, u32[]{:S(2)}) %collective-permute-start.5) | collective-permute-done | bytes 147488 | tf_op jit(solution)/shard_map/ppermute | solution.py:44
  35.6 2.9 %collective-permute-done.6.back4 = bf16[144,512]{1,0:T(8,128)(2,1)S(1)} collective-permute-done((bf16[144,512]{1,0:T(8,128)(2,1)S(1)}, bf16[144,512]{1,0:T(8,128)(2,1)S(1)}, u32[]{:S(2)}, u32[]{:S(2)}) %collective-permute-start.6) | collective-permute-done | bytes 147488 | tf_op jit(solution)/shard_map/ppermute | solution.py:44
  38.5 0.1 window.1
  38.5 0.5 collective-permute-start.10
  39.0 0.4 collective-permute-start.11
  39.4 2.1 %collective-permute-start.12 = (bf16[384,512]{1,0:T(8,128)(2,1)S(1)}, bf16[384,512]{1,0:T(8,128)(2,1)S(1)}, u32[]{:S(2)}, u32[]{:S(2)}) collective-permute-start(bf16[384,512]{1,0:T(8,128)(2,1)S(1)} %get-tuple-element.45.refs_0_), channel_id=1, source_target_pairs={{0,3},{1,0},{2,1},{3,2},{4,7},{5,4},{6,5},{7,6},{8,11},{9,8},{10,9... | collective-permute-start | bytes 1179656 | tf_op jit(solution)/shard_map/ppermute | solution.py:48
  41.5 4.1 %collective-permute-start.7 = (f32[2,1024]{1,0:T(2,128)S(1)}, f32[2,1024]{1,0:T(2,128)S(1)}, u32[]{:S(2)}, u32[]{:S(2)}) collective-permute-start(f32[2,1024]{1,0:T(2,128)S(1)} %get-tuple-element.44), channel_id=1, source_target_pairs={{0,24},{4,28},{8,32},{12,36},{16,40},{20,44},{24,48},{28,52},{32,5... | collective-permute-start | bytes 24584 | tf_op jit(solution)/shard_map/ppermute | solution.py:44
  45.6 5.7 %collective-permute-start.8 = (f32[2,1024]{1,0:T(2,128)S(1)}, f32[2,1024]{1,0:T(2,128)S(1)}, u32[]{:S(2)}, u32[]{:S(2)}) collective-permute-start(f32[2,1024]{1,0:T(2,128)S(1)} %get-tuple-element.44), channel_id=1, source_target_pairs={{0,48},{4,52},{8,56},{12,60},{16,64},{20,68},{24,72},{28,76},{32,8... | collective-permute-start | bytes 24584 | tf_op jit(solution)/shard_map/ppermute | solution.py:44
  51.3 0.0 collective-permute-done.7
  51.3 5.1 %collective-permute-start.9 = (f32[2,1024]{1,0:T(2,128)S(1)}, f32[2,1024]{1,0:T(2,128)S(1)}, u32[]{:S(2)}, u32[]{:S(2)}) collective-permute-start(f32[2,1024]{1,0:T(2,128)S(1)} %get-tuple-element.44), channel_id=1, source_target_pairs={{0,72},{4,76},{8,80},{12,84},{16,88},{20,92},{24,96},{28,100},{32,... | collective-permute-start | bytes 24584 | tf_op jit(solution)/shard_map/ppermute | solution.py:44
  56.4 0.0 collective-permute-done.8
  56.4 2.7 %collective-permute-start.15 = (bf16[384,512]{1,0:T(8,128)(2,1)S(1)}, bf16[384,512]{1,0:T(8,128)(2,1)S(1)}, u32[]{:S(2)}, u32[]{:S(2)}) collective-permute-start(bf16[384,512]{1,0:T(8,128)(2,1)S(1)} %get-tuple-element.45.refs_0_), channel_id=1, source_target_pairs={{0,4},{4,0},{1,5},{5,1},{2,6},{6,2},{3,7},{7,3},{8,12},{12,8},{9,1... | collective-permute-start | bytes 1179656 | tf_op jit(solution)/shard_map/ppermute | solution.py:52
  59.1 0.0 collective-permute-done.9
  59.1 0.0 collective-permute-done.10.refs_1_
  59.1 0.0 collective-permute-done.11.refs_2_
  59.1 0.0 collective-permute-done.12.refs_3_
  59.1 1.3 %collective-permute-start.16 = (bf16[384,512]{1,0:T(8,128)(2,1)S(1)}, bf16[384,512]{1,0:T(8,128)(2,1)S(1)}, u32[]{:S(2)}, u32[]{:S(2)}) collective-permute-start(bf16[384,512]{1,0:T(8,128)(2,1)S(1)} %collective-permute-done.10.refs_1_), channel_id=1, source_target_pairs={{0,4},{4,0},{1,5},{5,1},{2,6},{6,2},{3,7},{7,3},{8,12},{12,8},{9,1... | collective-permute-start | bytes 1179656 | tf_op jit(solution)/shard_map/ppermute | solution.py:52
  60.5 0.1 collective-permute-start.17
  60.6 0.4 collective-permute-start.18
  61.0 11.6 %collective-permute-start.13 = (f32[2,1024]{1,0:T(2,128)S(1)}, f32[2,1024]{1,0:T(2,128)S(1)}, u32[]{:S(2)}, u32[]{:S(2)}) collective-permute-start(f32[2,1024]{1,0:T(2,128)S(1)} %pad_maximum_fusion), channel_id=1, source_target_pairs={{0,96},{4,100},{8,104},{12,108},{16,112},{20,116},{24,120},{28,124... | collective-permute-start | bytes 24584 | tf_op jit(solution)/shard_map/ppermute | solution.py:44
  72.7 0.0 collective-permute-done.15.refs_4_
  72.7 1.5 %collective-permute-start.14 = (f32[2,1024]{1,0:T(2,128)S(1)}, f32[2,1024]{1,0:T(2,128)S(1)}, u32[]{:S(2)}, u32[]{:S(2)}) collective-permute-start(f32[2,1024]{1,0:T(2,128)S(1)} %pad_maximum_fusion), channel_id=1, source_target_pairs={{0,192},{4,196},{8,200},{12,204},{16,208},{20,212},{24,216},{28,22... | collective-permute-start | bytes 24584 | tf_op jit(solution)/shard_map/ppermute | solution.py:44
  74.2 0.0 collective-permute-done.16.refs_5_
  74.2 0.0 collective-permute-done.17.refs_6_
  74.2 0.0 collective-permute-done.18.refs_7_
  74.2 12.1 %attend.1 = bf16[512,1024]{1,0:T(8,128)(2,1)} custom-call(s32[3]{0:T(128)S(1)} %pad_add_fusion.info, bf16[512,1024]{1,0:T(8,128)(2,1)S(1)} %copy-done.2, bf16[384,512]{1,0:T(8,128)(2,1)S(1)} %get-tuple-element.45.refs_0_, bf16[384,512]{1,0:T(8,128)(2,1)S(1)} %collective-permute-done.10.refs_1_, bf16[384,512]{1,0:T(8,128)(2,1)S(1)} %collective-permute-done.11.refs_2_, ...), custom_call_target="tpu_custom_call" | custom-call | flops 4294967296 | bytes 4194304 | tf_op jit(solution)/shard_map/attend/pallas_call | solution.py:349
  86.3 0.0 collective-permute-done.13
  86.3 0.0 collective-permute-done.14
  86.4 1.5 %add_convert_fusion = bf16[512,1024]{1,0:T(8,128)(2,1)} fusion(f32[512,1024]{1,0:T(8,128)S(1)} %copy-done.3, f32[512,1024]{1,0:T(8,128)S(1)} %copy-done.4, f32[1024]{0:T(1024)S(1)} %bitcast.9), kind=kLoop, calls=%fused_computation | loop fusion | flops 1572864 | bytes 5246976 | tf_op jit(solution)/shard_map/convert_element_type | solution.py:418
  (13 shorter events, 0.1 us)
Async XLA Ops:
  1.4 6.7 %collective-permute-start = (bf16[3,1024]{1,0:T(4,128)(2,1)S(1)}, bf16[3,1024]{1,0:T(4,128)(2,1)S(1)}, u32[]{:S(2)}, u32[]{:S(2)}) collective-permute-start(bf16[3,1024]{1,0:T(4,128)(2,1)S(1)} %slice.50), channel_id=1, source_target_pairs={{0,4},{4,8},{8,12},{12,16},{16,20},{20,24},{24,28},{28,32},{32,36}... | collective-permute-start | bytes 18440 | tf_op jit(solution)/shard_map/ppermute | solution.py:44
  8.1 5.1 %copy-start.5 = (bf16[3,1024]{1,0:T(4,128)(2,1)}, bf16[3,1024]{1,0:T(4,128)(2,1)S(1)}, u32[]{:S(2)}) copy-start(bf16[3,1024]{1,0:T(4,128)(2,1)S(1)} %collective-permute-done.edge) | copy-start | bytes 18436
  8.1 17.0 %collective-permute-start.1 = (bf16[144,512]{1,0:T(8,128)(2,1)}, bf16[144,512]{1,0:T(8,128)(2,1)S(1)}, u32[]{:S(2)}, u32[]{:S(2)}) collective-permute-start(bf16[144,512]{1,0:T(8,128)(2,1)} %get-tuple-element.37), channel_id=1, source_target_pairs={{0,1},{1,2},{2,3},{3,0},{4,5},{5,6},{6,7},{7,4},{8,9},{9,10},{10,1... | collective-permute-start | bytes 442376 | tf_op jit(solution)/shard_map/ppermute | solution.py:48
  9.5 15.6 %collective-permute-start.2 = (bf16[144,512]{1,0:T(8,128)(2,1)}, bf16[144,512]{1,0:T(8,128)(2,1)S(1)}, u32[]{:S(2)}, u32[]{:S(2)}) collective-permute-start(bf16[144,512]{1,0:T(8,128)(2,1)} %get-tuple-element.38), channel_id=1, source_target_pairs={{0,2},{1,3},{2,0},{3,1},{4,6},{5,7},{6,4},{7,5},{8,10},{9,11},{10,... | collective-permute-start | bytes 442376 | tf_op jit(solution)/shard_map/ppermute | solution.py:48
  12.1 13.0 %collective-permute-start.3 = (bf16[144,512]{1,0:T(8,128)(2,1)}, bf16[144,512]{1,0:T(8,128)(2,1)S(1)}, u32[]{:S(2)}, u32[]{:S(2)}) collective-permute-start(bf16[144,512]{1,0:T(8,128)(2,1)} %get-tuple-element.39), channel_id=1, source_target_pairs={{0,3},{1,0},{2,1},{3,2},{4,7},{5,4},{6,5},{7,6},{8,11},{9,8},{10,9... | collective-permute-start | bytes 442376 | tf_op jit(solution)/shard_map/ppermute | solution.py:48
  13.2 11.9 %copy-start = (f32[144,512]{1,0:T(8,128)S(1)}, f32[144,512]{1,0:T(8,128)}, u32[]{:S(2)}) copy-start(f32[144,512]{1,0:T(8,128)} %get-tuple-element.36.a) | copy-start | bytes 884740
  13.2 61.0 %copy-start.2 = (bf16[512,1024]{1,0:T(8,128)(2,1)S(1)}, bf16[512,1024]{1,0:T(8,128)(2,1)}, u32[]{:S(2)}) copy-start(bf16[512,1024]{1,0:T(8,128)(2,1)} %q_ref.1) | copy-start | bytes 3145732
  22.1 2.9 %collective-permute-start.4 = (f32[2,1024]{1,0:T(2,128)}, f32[2,1024]{1,0:T(2,128)S(1)}, u32[]{:S(2)}, u32[]{:S(2)}) collective-permute-start(f32[2,1024]{1,0:T(2,128)} %get-tuple-element.40.couple), channel_id=1, source_target_pairs={{0,4},{4,0},{1,5},{5,1},{2,6},{6,2},{3,7},{7,3},{8,12},{12,8},{9,1... | collective-permute-start | bytes 24584 | tf_op jit(solution)/shard_map/ppermute | solution.py:52
  25.1 0.7 copy-start.1
  26.5 9.1 %collective-permute-start.5 = (bf16[144,512]{1,0:T(8,128)(2,1)S(1)}, bf16[144,512]{1,0:T(8,128)(2,1)S(1)}, u32[]{:S(2)}, u32[]{:S(2)}) collective-permute-start(bf16[144,512]{1,0:T(8,128)(2,1)S(1)} %get-tuple-element.41.mine), channel_id=1, source_target_pairs={{0,8},{4,12},{8,16},{12,20},{16,24},{20,28},{24,32},{28,36},{32,40... | collective-permute-start | bytes 442376 | tf_op jit(solution)/shard_map/ppermute | solution.py:44
  28.4 10.0 %collective-permute-start.6 = (bf16[144,512]{1,0:T(8,128)(2,1)S(1)}, bf16[144,512]{1,0:T(8,128)(2,1)S(1)}, u32[]{:S(2)}, u32[]{:S(2)}) collective-permute-start(bf16[144,512]{1,0:T(8,128)(2,1)S(1)} %get-tuple-element.41.mine), channel_id=1, source_target_pairs={{0,16},{4,20},{8,24},{12,28},{16,32},{20,36},{24,40},{28,44},{32,4... | collective-permute-start | bytes 442376 | tf_op jit(solution)/shard_map/ppermute | solution.py:44
  38.5 20.6 %collective-permute-start.10 = (bf16[384,512]{1,0:T(8,128)(2,1)S(1)}, bf16[384,512]{1,0:T(8,128)(2,1)S(1)}, u32[]{:S(2)}, u32[]{:S(2)}) collective-permute-start(bf16[384,512]{1,0:T(8,128)(2,1)S(1)} %get-tuple-element.45.refs_0_), channel_id=1, source_target_pairs={{0,1},{1,2},{2,3},{3,0},{4,5},{5,6},{6,7},{7,4},{8,9},{9,10},{10,1... | collective-permute-start | bytes 1179656 | tf_op jit(solution)/shard_map/ppermute | solution.py:48
  39.0 20.1 %collective-permute-start.11 = (bf16[384,512]{1,0:T(8,128)(2,1)S(1)}, bf16[384,512]{1,0:T(8,128)(2,1)S(1)}, u32[]{:S(2)}, u32[]{:S(2)}) collective-permute-start(bf16[384,512]{1,0:T(8,128)(2,1)S(1)} %get-tuple-element.45.refs_0_), channel_id=1, source_target_pairs={{0,2},{1,3},{2,0},{3,1},{4,6},{5,7},{6,4},{7,5},{8,10},{9,11},{10,... | collective-permute-start | bytes 1179656 | tf_op jit(solution)/shard_map/ppermute | solution.py:48
  39.4 19.7 %collective-permute-start.12 = (bf16[384,512]{1,0:T(8,128)(2,1)S(1)}, bf16[384,512]{1,0:T(8,128)(2,1)S(1)}, u32[]{:S(2)}, u32[]{:S(2)}) collective-permute-start(bf16[384,512]{1,0:T(8,128)(2,1)S(1)} %get-tuple-element.45.refs_0_), channel_id=1, source_target_pairs={{0,3},{1,0},{2,1},{3,2},{4,7},{5,4},{6,5},{7,6},{8,11},{9,8},{10,9... | collective-permute-start | bytes 1179656 | tf_op jit(solution)/shard_map/ppermute | solution.py:48
  41.5 9.8 %collective-permute-start.7 = (f32[2,1024]{1,0:T(2,128)S(1)}, f32[2,1024]{1,0:T(2,128)S(1)}, u32[]{:S(2)}, u32[]{:S(2)}) collective-permute-start(f32[2,1024]{1,0:T(2,128)S(1)} %get-tuple-element.44), channel_id=1, source_target_pairs={{0,24},{4,28},{8,32},{12,36},{16,40},{20,44},{24,48},{28,52},{32,5... | collective-permute-start | bytes 24584 | tf_op jit(solution)/shard_map/ppermute | solution.py:44
  45.6 10.9 %collective-permute-start.8 = (f32[2,1024]{1,0:T(2,128)S(1)}, f32[2,1024]{1,0:T(2,128)S(1)}, u32[]{:S(2)}, u32[]{:S(2)}) collective-permute-start(f32[2,1024]{1,0:T(2,128)S(1)} %get-tuple-element.44), channel_id=1, source_target_pairs={{0,48},{4,52},{8,56},{12,60},{16,64},{20,68},{24,72},{28,76},{32,8... | collective-permute-start | bytes 24584 | tf_op jit(solution)/shard_map/ppermute | solution.py:44
  51.3 7.8 %collective-permute-start.9 = (f32[2,1024]{1,0:T(2,128)S(1)}, f32[2,1024]{1,0:T(2,128)S(1)}, u32[]{:S(2)}, u32[]{:S(2)}) collective-permute-start(f32[2,1024]{1,0:T(2,128)S(1)} %get-tuple-element.44), channel_id=1, source_target_pairs={{0,72},{4,76},{8,80},{12,84},{16,88},{20,92},{24,96},{28,100},{32,... | collective-permute-start | bytes 24584 | tf_op jit(solution)/shard_map/ppermute | solution.py:44
  56.4 16.2 %collective-permute-start.15 = (bf16[384,512]{1,0:T(8,128)(2,1)S(1)}, bf16[384,512]{1,0:T(8,128)(2,1)S(1)}, u32[]{:S(2)}, u32[]{:S(2)}) collective-permute-start(bf16[384,512]{1,0:T(8,128)(2,1)S(1)} %get-tuple-element.45.refs_0_), channel_id=1, source_target_pairs={{0,4},{4,0},{1,5},{5,1},{2,6},{6,2},{3,7},{7,3},{8,12},{12,8},{9,1... | collective-permute-start | bytes 1179656 | tf_op jit(solution)/shard_map/ppermute | solution.py:52
  59.1 15.0 %collective-permute-start.16 = (bf16[384,512]{1,0:T(8,128)(2,1)S(1)}, bf16[384,512]{1,0:T(8,128)(2,1)S(1)}, u32[]{:S(2)}, u32[]{:S(2)}) collective-permute-start(bf16[384,512]{1,0:T(8,128)(2,1)S(1)} %collective-permute-done.10.refs_1_), channel_id=1, source_target_pairs={{0,4},{4,0},{1,5},{5,1},{2,6},{6,2},{3,7},{7,3},{8,12},{12,8},{9,1... | collective-permute-start | bytes 1179656 | tf_op jit(solution)/shard_map/ppermute | solution.py:52
  60.5 13.7 %collective-permute-start.17 = (bf16[384,512]{1,0:T(8,128)(2,1)S(1)}, bf16[384,512]{1,0:T(8,128)(2,1)S(1)}, u32[]{:S(2)}, u32[]{:S(2)}) collective-permute-start(bf16[384,512]{1,0:T(8,128)(2,1)S(1)} %collective-permute-done.11.refs_2_), channel_id=1, source_target_pairs={{0,4},{4,0},{1,5},{5,1},{2,6},{6,2},{3,7},{7,3},{8,12},{12,8},{9,1... | collective-permute-start | bytes 1179656 | tf_op jit(solution)/shard_map/ppermute | solution.py:52
  60.6 13.6 %collective-permute-start.18 = (bf16[384,512]{1,0:T(8,128)(2,1)S(1)}, bf16[384,512]{1,0:T(8,128)(2,1)S(1)}, u32[]{:S(2)}, u32[]{:S(2)}) collective-permute-start(bf16[384,512]{1,0:T(8,128)(2,1)S(1)} %collective-permute-done.12.refs_3_), channel_id=1, source_target_pairs={{0,4},{4,0},{1,5},{5,1},{2,6},{6,2},{3,7},{7,3},{8,12},{12,8},{9,1... | collective-permute-start | bytes 1179656 | tf_op jit(solution)/shard_map/ppermute | solution.py:52
  61.0 25.3 %copy-start.3 = (f32[512,1024]{1,0:T(8,128)S(1)}, f32[512,1024]{1,0:T(8,128)}, u32[]{:S(2)}) copy-start(f32[512,1024]{1,0:T(8,128)} %get-tuple-element.34) | copy-start | bytes 6291460
  61.0 25.3 %copy-start.4 = (f32[512,1024]{1,0:T(8,128)S(1)}, f32[512,1024]{1,0:T(8,128)}, u32[]{:S(2)}) copy-start(f32[512,1024]{1,0:T(8,128)} %get-tuple-element.35) | copy-start | bytes 6291460
  61.0 25.3 %collective-permute-start.13 = (f32[2,1024]{1,0:T(2,128)S(1)}, f32[2,1024]{1,0:T(2,128)S(1)}, u32[]{:S(2)}, u32[]{:S(2)}) collective-permute-start(f32[2,1024]{1,0:T(2,128)S(1)} %pad_maximum_fusion), channel_id=1, source_target_pairs={{0,96},{4,100},{8,104},{12,108},{16,112},{20,116},{24,120},{28,124... | collective-permute-start | bytes 24584 | tf_op jit(solution)/shard_map/ppermute | solution.py:44
  72.7 13.6 %collective-permute-start.14 = (f32[2,1024]{1,0:T(2,128)S(1)}, f32[2,1024]{1,0:T(2,128)S(1)}, u32[]{:S(2)}, u32[]{:S(2)}) collective-permute-start(f32[2,1024]{1,0:T(2,128)S(1)} %pad_maximum_fusion), channel_id=1, source_target_pairs={{0,192},{4,196},{8,200},{12,204},{16,208},{20,212},{24,216},{28,22... | collective-permute-start | bytes 24584 | tf_op jit(solution)/shard_map/ppermute | solution.py:44

commit v4 on v3

--- a/solution.py
+++ b/solution.py
@@ -280,6 +280,49 @@
     )(*inputs, *filled)
 
 
+def attend_head(q_ref, kv, out, admitted):
+    def scored(q, begin, size):
+        return lax.dot_general(
+            q,
+            kv[begin : begin + size, 0:HD],
+            (((1,), (1,)), ((), ())),
+            preferred_element_type=F32,
+        )
+
+    rows = lax.broadcasted_iota(jnp.int32, (QROWS, QROWS), 0)
+    columns = lax.broadcasted_iota(jnp.int32, (QROWS, QROWS), 1)
+    causal = rows >= columns
+    last = (SHARDS - 1) * TOK
+    q = q_ref[...] * jnp.asarray(HD**-0.5, BF16)
+    most = SHARDS - 1
+    wide = [admitted(scored(q, k * TOK, TOK), most - k) for k in range(1, most)]
+    for half in range(2):
+        low = half * QROWS
+        rows = slice(low, low + QROWS)
+        far = admitted(scored(q[rows], low, QROWS), most)
+        near = scored(q[rows], last + low, QROWS)
+        blocks = [(k * TOK, s[rows]) for k, s in zip(range(1, SHARDS - 1), wide)]
+        blocks.append((low, jnp.where(causal, masked_score, far)))
+        blocks.append((last + low, jnp.where(causal, near, masked_score)))
+        if half == 0:
+            blocks.append((QROWS, admitted(scored(q[rows], QROWS, QROWS), most)))
+        else:
+            blocks.append((last, scored(q[rows], last, QROWS)))
+        tiles = [s[:, k : k + 128] for _, s in blocks for k in range(0, s.shape[1], 128)]
+        peak = jnp.max(functools.reduce(jnp.maximum, tiles), axis=1, keepdims=True)
+        weights = [jnp.exp(s - peak) for _, s in blocks]
+        tiles = [p[:, k : k + 128] for p in weights for k in range(0, p.shape[1], 128)]
+        norm = jnp.sum(functools.reduce(jnp.add, tiles), axis=1, keepdims=True)
+        total = jnp.zeros((QROWS, HD), F32)
+        for p, (begin, _) in zip(weights, blocks):
+            total = total + jnp.dot(
+                p.astype(BF16),
+                kv[begin : begin + p.shape[1], HD:],
+                preferred_element_type=F32,
+            )
+        out[rows, :] = (total / norm).astype(BF16)
+
+
 def attend_kernel(info, q_ref, *refs):
     own, other = (refs[0:PARTS], refs[PARTS : 2 * PARTS])
     out, kv = refs[-2:]
@@ -299,47 +342,15 @@
                     begin = pl.multiple_of(((behind + 1) // 2 - core) * QUARTER, QUARTER)
                     kv[there, :] = other[k][pl.ds(begin, QUARTER), :]
 
-    def bias(behind):
-        return jnp.where(position >= behind, 0.0, masked_score).astype(F32)
-
-    rows = lax.broadcasted_iota(jnp.int32, (QROWS, QROWS), 0)
-    columns = lax.broadcasted_iota(jnp.int32, (QROWS, QROWS), 1)
-    causal = rows >= columns
-    last = (SHARDS - 1) * TOK
-    for half in range(2):
-        low = half * QROWS
-        q = q_ref[low : low + QROWS, :] * jnp.asarray(HD**-0.5, BF16)
-        blocks = [(k * TOK, TOK, bias(SHARDS - 1 - k), None) for k in range(1, SHARDS - 1)]
-        if half == 0:
-            blocks.append((QROWS, QROWS, bias(SHARDS - 1), None))
-        else:
-            blocks.append((last, QROWS, None, None))
-        blocks.append((low, QROWS, bias(SHARDS - 1), ~causal))
-        blocks.append((last + low, QROWS, None, causal))
-        scores = []
-        for begin, size, extra, mask in blocks:
-            s = lax.dot_general(
-                q,
-                kv[begin : begin + size, 0:HD],
-                (((1,), (1,)), ((), ())),
-                preferred_element_type=F32,
-            )
-            if extra is not None:
-                s = s + extra
-            if mask is not None:
-                s = jnp.where(mask, s, masked_score)
-            scores.append(s)
-        tiles = [s[:, k : k + 128] for s in scores for k in range(0, s.shape[1], 128)]
-        peak = jnp.max(functools.reduce(jnp.maximum, tiles), axis=1, keepdims=True)
-        weights = [jnp.exp(s - peak) for s in scores]
-        tiles = [p[:, k : k + 128] for p in weights for k in range(0, p.shape[1], 128)]
-        norm = jnp.sum(functools.reduce(jnp.add, tiles), axis=1, keepdims=True)
-        total = jnp.zeros((QROWS, HD), F32)
-        for p, (begin, size, _, _) in zip(weights, blocks):
-            total = total + jnp.dot(
-                p.astype(BF16), kv[begin : begin + size, HD:], preferred_element_type=F32
-            )
-        out[low : low + QROWS, :] = (total / norm).astype(BF16)
+    @pl.when(position >= SHARDS - 1)
+    def _():
+        attend_head(q_ref, kv, out, lambda s, behind: s)
+
+    @pl.when(position < SHARDS - 1)
+    def _():
+        attend_head(
+            q_ref, kv, out, lambda s, behind: jnp.where(position >= behind, s, masked_score)
+        )
 
 
 def attend(head, count, info, queries, own, other, filled):
@@ -403,13 +414,13 @@
         mine, shifted(mine, 2), shifted(mine, 4), before, inclusive
     )
     own = [trio] + [turned(trio, k) for k in range(1, PARTS)]
-    far = [shifted(inclusive, 6 * k) for k in (1, 2, 3)]
+    far = [shifted(inclusive, 6 * k) for k in (1, 2)]
     *far, own[1], own[2], own[3] = lax.optimization_barrier((*far, *own[1:]))
     for couple in far:
         before = compose(couple, before)
         inclusive = compose(couple, inclusive)
     other = [swapped(piece) for piece in own]
-    far = [shifted(inclusive, 24 * k) for k in (1, 2)]
+    far = [shifted(inclusive, 18 * k) for k in (1, 2, 3)]
     heads = queries.shape[1] // HD
     attended = attend(0, heads, info, queries, own, other, ())
     *far, attended = lax.optimization_barrier((*far, attended))

time: 88.3 us -> 90.2 us (1.022)
  the two profiles are of different devices: /device:TPU:33 before, /device:TPU:3 now
where the time goes in v4:
time: 90.2 us; the launch traced here: 89 us
  starting transfers between devices  50.8 us (56%)
  Pallas kernels  24 us (27%)
  waiting for transfers between devices  10.3 us (11%)
  other arithmetic  1.63 us (2%)
  local copies, waits for them, and re-layouts  1.44 us (2%)
    ppermute x8, starting transfers between devices, shifted(): lax.ppermute(value, SEQ, [(k, k + steps) for k in range(count - steps)])  39.3 us
    pallas_call x1, Pallas kernels, attend(): pl.pallas_call(attend_kernel, name='attend', grid=(count,), out_shape=jax...  11.2 us
    pallas_call x1, Pallas kernels, recur(): pl.pallas_call(recur_kernel, name='recur', grid=(count,), out_shape=[jax....  8.98 us
    ppermute x6, starting transfers between devices, turned(): lax.ppermute(value, 'mp', [(k, (k + steps) % PARTS) for k in range(PARTS)])  7.93 us
    ppermute x6, waiting for transfers between devices, turned(): lax.ppermute(value, 'mp', [(k, (k + steps) % PARTS) for k in range(PARTS)])  6.41 us
    ppermute x5, starting transfers between devices, swapped(): return lax.ppermute(value, CORE, [(0, 1), (1, 0)])  3.59 us
    pallas_call x1, Pallas kernels, project(): pl.pallas_call(project_kernel, name='project', out_shape=[jax.ShapeDtypeS...  3.06 us
    ppermute x8, waiting for transfers between devices, shifted(): lax.ppermute(value, SEQ, [(k, k + steps) for k in range(count - steps)])  2.55 us
  transfers between devices with their start and end apart: 19, of which 4 were waited for; matrix products, arithmetic and copies ran while one was open for 0% of the time, Pallas kernels for 26%

profile of v4, /device:TPU:3, one launch (start us, length us, event | category | flops | bytes accessed | tf_op | source)
XLA Modules:
  0.0 89.0 jit_solution(12817280538802113392)
XLA Ops:
  0.6 0.7 slice.48
  1.4 3.7 %collective-permute-start = (bf16[3,1024]{1,0:T(4,128)(2,1)S(1)}, bf16[3,1024]{1,0:T(4,128)(2,1)S(1)}, u32[]{:S(2)}, u32[]{:S(2)}) collective-permute-start(bf16[3,1024]{1,0:T(4,128)(2,1)S(1)} %slice.48), channel_id=1, source_target_pairs={{0,4},{4,8},{8,12},{12,16},{16,20},{20,24},{24,28},{28,32},{32,36}... | collective-permute-start | bytes 18440 | tf_op jit(solution)/shard_map/ppermute | solution.py:44
  5.0 3.1 %project.1 = (f32[144,512]{1,0:T(8,128)}, bf16[144,512]{1,0:T(8,128)(2,1)}, bf16[144,512]{1,0:T(8,128)(2,1)}, bf16[144,512]{1,0:T(8,128)(2,1)}) custom-call(s32[1]{0:T(128)} %bitcast.place, bf16[512,1024]{1,0:T(8,128)(2,1)} %stream.1, f32[1,1024]{1,0:T(1,128)} %bitcast.10, bf16[1024,512]{1,0:T(8,128)(2,1)} %weight.1), custom_call_target="tpu_custom_call" | custom-call | flops 536870912 | bytes 3145728 | tf_op jit(solution)/shard_map/project/pallas_call | solution.py:73
  8.1 0.0 collective-permute-done.edge
  8.1 1.4 %collective-permute-start.1 = (bf16[144,512]{1,0:T(8,128)(2,1)}, bf16[144,512]{1,0:T(8,128)(2,1)S(1)}, u32[]{:S(2)}, u32[]{:S(2)}) collective-permute-start(bf16[144,512]{1,0:T(8,128)(2,1)} %get-tuple-element.37), channel_id=1, source_target_pairs={{0,1},{1,2},{2,3},{3,0},{4,5},{5,6},{6,7},{7,4},{8,9},{9,10},{10,1... | collective-permute-start | bytes 442376 | tf_op jit(solution)/shard_map/ppermute | solution.py:48
  9.5 2.6 %collective-permute-start.2 = (bf16[144,512]{1,0:T(8,128)(2,1)}, bf16[144,512]{1,0:T(8,128)(2,1)S(1)}, u32[]{:S(2)}, u32[]{:S(2)}) collective-permute-start(bf16[144,512]{1,0:T(8,128)(2,1)} %get-tuple-element.38), channel_id=1, source_target_pairs={{0,2},{1,3},{2,0},{3,1},{4,6},{5,7},{6,4},{7,5},{8,10},{9,11},{10,... | collective-permute-start | bytes 442376 | tf_op jit(solution)/shard_map/ppermute | solution.py:48
  12.1 1.1 %collective-permute-start.3 = (bf16[144,512]{1,0:T(8,128)(2,1)}, bf16[144,512]{1,0:T(8,128)(2,1)S(1)}, u32[]{:S(2)}, u32[]{:S(2)}) collective-permute-start(bf16[144,512]{1,0:T(8,128)(2,1)} %get-tuple-element.39), channel_id=1, source_target_pairs={{0,3},{1,0},{2,1},{3,2},{4,7},{5,4},{6,5},{7,6},{8,11},{9,8},{10,9... | collective-permute-start | bytes 442376 | tf_op jit(solution)/shard_map/ppermute | solution.py:48
  13.2 9.0 %recur.1 = (f32[512,1024]{1,0:T(8,128)}, f32[512,1024]{1,0:T(8,128)}, f32[2,1024]{1,0:T(2,128)}) custom-call(bf16[512,1024]{1,0:T(8,128)(2,1)} %branch.1, bf16[3,1024]{1,0:T(4,128)(2,1)} %copy-done.5, bf16[512,1024]{1,0:T(8,128)(2,1)} %gate.1, f32[4,1024]{1,0:T(4,128)} %taps.1, f32[1,1024]{1,0:T(1,128)} %bitcast.11, bf16[4,256,256]{2,1,0:T(8,128)(2,1)} %in_w.1, ...), custom_call_target="tpu_custom_call" | custom-call | flops 1073741824 | bytes 8388608 | tf_op jit(solution)/shard_map/recur/pallas_call | solution.py:256
  22.1 0.1 collective-permute-start.4
  22.2 0.1 pad_add_fusion.info
  22.3 1.3 %collective-permute-done.4.other = f32[2,1024]{1,0:T(2,128)S(1)} collective-permute-done((f32[2,1024]{1,0:T(2,128)}, f32[2,1024]{1,0:T(2,128)S(1)}, u32[]{:S(2)}, u32[]{:S(2)}) %collective-permute-start.4) | collective-permute-done | bytes 8224 | tf_op jit(solution)/shard_map/ppermute | solution.py:52
  23.6 0.0 collective-permute-done.1.b
  23.6 0.0 collective-permute-done.2.c
  23.6 0.0 collective-permute-done.3.d
  23.6 0.7 copy-done.1
  24.3 0.7 normed.1
  25.1 2.8 %collective-permute-start.5 = (bf16[144,512]{1,0:T(8,128)(2,1)S(1)}, bf16[144,512]{1,0:T(8,128)(2,1)S(1)}, u32[]{:S(2)}, u32[]{:S(2)}) collective-permute-start(bf16[144,512]{1,0:T(8,128)(2,1)S(1)} %get-tuple-element.41.mine), channel_id=1, source_target_pairs={{0,8},{4,12},{8,16},{12,20},{16,24},{20,28},{24,32},{28,36},{32,40... | collective-permute-start | bytes 442376 | tf_op jit(solution)/shard_map/ppermute | solution.py:44
  27.9 5.8 %collective-permute-start.6 = (bf16[144,512]{1,0:T(8,128)(2,1)S(1)}, bf16[144,512]{1,0:T(8,128)(2,1)S(1)}, u32[]{:S(2)}, u32[]{:S(2)}) collective-permute-start(bf16[144,512]{1,0:T(8,128)(2,1)S(1)} %get-tuple-element.41.mine), channel_id=1, source_target_pairs={{0,16},{4,20},{8,24},{12,28},{16,32},{20,36},{24,40},{28,44},{32,4... | collective-permute-start | bytes 442376 | tf_op jit(solution)/shard_map/ppermute | solution.py:44
  33.7 0.0 collective-permute-done.5.back2
  33.8 2.5 %collective-permute-done.6.back4 = bf16[144,512]{1,0:T(8,128)(2,1)S(1)} collective-permute-done((bf16[144,512]{1,0:T(8,128)(2,1)S(1)}, bf16[144,512]{1,0:T(8,128)(2,1)S(1)}, u32[]{:S(2)}, u32[]{:S(2)}) %collective-permute-start.6) | collective-permute-done | bytes 147488 | tf_op jit(solution)/shard_map/ppermute | solution.py:44
  36.3 0.1 window.1
  36.4 0.1 collective-permute-start.10
  36.5 2.7 %collective-permute-start.11 = (bf16[384,512]{1,0:T(8,128)(2,1)S(1)}, bf16[384,512]{1,0:T(8,128)(2,1)S(1)}, u32[]{:S(2)}, u32[]{:S(2)}) collective-permute-start(bf16[384,512]{1,0:T(8,128)(2,1)S(1)} %get-tuple-element.45.refs_0_), channel_id=1, source_target_pairs={{0,3},{1,0},{2,1},{3,2},{4,7},{5,4},{6,5},{7,6},{8,11},{9,8},{10,9... | collective-permute-start | bytes 1179656 | tf_op jit(solution)/shard_map/ppermute | solution.py:48
  39.2 0.0 collective-permute-start.9
  39.2 5.7 %collective-permute-start.7 = (f32[2,1024]{1,0:T(2,128)S(1)}, f32[2,1024]{1,0:T(2,128)S(1)}, u32[]{:S(2)}, u32[]{:S(2)}) collective-permute-start(f32[2,1024]{1,0:T(2,128)S(1)} %get-tuple-element.44), channel_id=1, source_target_pairs={{0,24},{4,28},{8,32},{12,36},{16,40},{20,44},{24,48},{28,52},{32,5... | collective-permute-start | bytes 24584 | tf_op jit(solution)/shard_map/ppermute | solution.py:44
  44.9 3.6 %collective-permute-start.8 = (f32[2,1024]{1,0:T(2,128)S(1)}, f32[2,1024]{1,0:T(2,128)S(1)}, u32[]{:S(2)}, u32[]{:S(2)}) collective-permute-start(f32[2,1024]{1,0:T(2,128)S(1)} %get-tuple-element.44), channel_id=1, source_target_pairs={{0,48},{4,52},{8,56},{12,60},{16,64},{20,68},{24,72},{28,76},{32,8... | collective-permute-start | bytes 24584 | tf_op jit(solution)/shard_map/ppermute | solution.py:44
  48.5 0.0 collective-permute-done.7
  48.5 2.5 %collective-permute-start.15 = (bf16[384,512]{1,0:T(8,128)(2,1)S(1)}, bf16[384,512]{1,0:T(8,128)(2,1)S(1)}, u32[]{:S(2)}, u32[]{:S(2)}) collective-permute-start(bf16[384,512]{1,0:T(8,128)(2,1)S(1)} %get-tuple-element.45.refs_0_), channel_id=1, source_target_pairs={{0,4},{4,0},{1,5},{5,1},{2,6},{6,2},{3,7},{7,3},{8,12},{12,8},{9,1... | collective-permute-start | bytes 1179656 | tf_op jit(solution)/shard_map/ppermute | solution.py:52
  51.0 0.0 collective-permute-done.8
  51.0 0.0 collective-permute-done.10.refs_2_
  51.0 2.8 %collective-permute-done.11.refs_3_ = bf16[384,512]{1,0:T(8,128)(2,1)S(1)} collective-permute-done((bf16[384,512]{1,0:T(8,128)(2,1)S(1)}, bf16[384,512]{1,0:T(8,128)(2,1)S(1)}, u32[]{:S(2)}, u32[]{:S(2)}) %collective-permute-start.11) | collective-permute-done | bytes 393248 | tf_op jit(solution)/shard_map/ppermute | solution.py:48
  53.8 3.6 %collective-permute-done.9.refs_1_ = bf16[384,512]{1,0:T(8,128)(2,1)S(1)} collective-permute-done((bf16[384,512]{1,0:T(8,128)(2,1)S(1)}, bf16[384,512]{1,0:T(8,128)(2,1)S(1)}, u32[]{:S(2)}, u32[]{:S(2)}) %collective-permute-start.9) | collective-permute-done | bytes 393248 | tf_op jit(solution)/shard_map/ppermute | solution.py:48
  57.4 0.5 collective-permute-start.16
  57.9 0.0 collective-permute-start.17
  57.9 0.5 collective-permute-start.18
  58.5 6.4 %collective-permute-start.12 = (f32[2,1024]{1,0:T(2,128)S(1)}, f32[2,1024]{1,0:T(2,128)S(1)}, u32[]{:S(2)}, u32[]{:S(2)}) collective-permute-start(f32[2,1024]{1,0:T(2,128)S(1)} %pad_maximum_fusion), channel_id=1, source_target_pairs={{0,72},{4,76},{8,80},{12,84},{16,88},{20,92},{24,96},{28,100},{32,... | collective-permute-start | bytes 24584 | tf_op jit(solution)/shard_map/ppermute | solution.py:44
  64.9 0.0 collective-permute-done.15.refs_4_
  64.9 9.9 %collective-permute-start.13 = (f32[2,1024]{1,0:T(2,128)S(1)}, f32[2,1024]{1,0:T(2,128)S(1)}, u32[]{:S(2)}, u32[]{:S(2)}) collective-permute-start(f32[2,1024]{1,0:T(2,128)S(1)} %pad_maximum_fusion), channel_id=1, source_target_pairs={{0,144},{4,148},{8,152},{12,156},{16,160},{20,164},{24,168},{28,17... | collective-permute-start | bytes 24584 | tf_op jit(solution)/shard_map/ppermute | solution.py:44
  74.8 0.0 collective-permute-done.16.refs_5_
  74.8 1.5 %collective-permute-start.14 = (f32[2,1024]{1,0:T(2,128)S(1)}, f32[2,1024]{1,0:T(2,128)S(1)}, u32[]{:S(2)}, u32[]{:S(2)}) collective-permute-start(f32[2,1024]{1,0:T(2,128)S(1)} %pad_maximum_fusion), channel_id=1, source_target_pairs={{0,216},{4,220},{8,224},{12,228},{16,232},{20,236},{24,240},{28,24... | collective-permute-start | bytes 24584 | tf_op jit(solution)/shard_map/ppermute | solution.py:44
  76.3 0.0 collective-permute-done.17.refs_6_
  76.3 0.0 collective-permute-done.18.refs_7_
  76.3 0.0 copy-done.2
  76.3 11.2 %attend.1 = bf16[512,1024]{1,0:T(8,128)(2,1)} custom-call(s32[3]{0:T(128)S(1)} %pad_add_fusion.info, bf16[512,1024]{1,0:T(8,128)(2,1)S(1)} %copy-done.2, bf16[384,512]{1,0:T(8,128)(2,1)S(1)} %get-tuple-element.45.refs_0_, bf16[384,512]{1,0:T(8,128)(2,1)S(1)} %collective-permute-done.9.refs_1_, bf16[384,512]{1,0:T(8,128)(2,1)S(1)} %collective-permute-done.10.refs_2_, ...), custom_call_target="tpu_custom_call" | custom-call | flops 4294967296 | bytes 4194304 | tf_op jit(solution)/shard_map/attend/pallas_call | solution.py:360
  87.5 0.0 collective-permute-done.12
  87.5 0.0 collective-permute-done.13
  87.5 0.0 collective-permute-done.14
  87.6 1.5 %add_convert_fusion = bf16[512,1024]{1,0:T(8,128)(2,1)} fusion(f32[512,1024]{1,0:T(8,128)S(1)} %copy-done.3, f32[512,1024]{1,0:T(8,128)S(1)} %copy-done.4, f32[1024]{0:T(1024)S(1)} %bitcast.9), kind=kLoop, calls=%fused_computation | loop fusion | flops 1572864 | bytes 5246976 | tf_op jit(solution)/shard_map/convert_element_type | solution.py:429
  (13 shorter events, 0.1 us)
Async XLA Ops:
  1.4 6.7 %collective-permute-start = (bf16[3,1024]{1,0:T(4,128)(2,1)S(1)}, bf16[3,1024]{1,0:T(4,128)(2,1)S(1)}, u32[]{:S(2)}, u32[]{:S(2)}) collective-permute-start(bf16[3,1024]{1,0:T(4,128)(2,1)S(1)} %slice.48), channel_id=1, source_target_pairs={{0,4},{4,8},{8,12},{12,16},{16,20},{20,24},{24,28},{28,32},{32,36}... | collective-permute-start | bytes 18440 | tf_op jit(solution)/shard_map/ppermute | solution.py:44
  8.1 5.1 %copy-start.5 = (bf16[3,1024]{1,0:T(4,128)(2,1)}, bf16[3,1024]{1,0:T(4,128)(2,1)S(1)}, u32[]{:S(2)}) copy-start(bf16[3,1024]{1,0:T(4,128)(2,1)S(1)} %collective-permute-done.edge) | copy-start | bytes 18436
  8.1 15.5 %collective-permute-start.1 = (bf16[144,512]{1,0:T(8,128)(2,1)}, bf16[144,512]{1,0:T(8,128)(2,1)S(1)}, u32[]{:S(2)}, u32[]{:S(2)}) collective-permute-start(bf16[144,512]{1,0:T(8,128)(2,1)} %get-tuple-element.37), channel_id=1, source_target_pairs={{0,1},{1,2},{2,3},{3,0},{4,5},{5,6},{6,7},{7,4},{8,9},{9,10},{10,1... | collective-permute-start | bytes 442376 | tf_op jit(solution)/shard_map/ppermute | solution.py:48
  9.5 14.2 %collective-permute-start.2 = (bf16[144,512]{1,0:T(8,128)(2,1)}, bf16[144,512]{1,0:T(8,128)(2,1)S(1)}, u32[]{:S(2)}, u32[]{:S(2)}) collective-permute-start(bf16[144,512]{1,0:T(8,128)(2,1)} %get-tuple-element.38), channel_id=1, source_target_pairs={{0,2},{1,3},{2,0},{3,1},{4,6},{5,7},{6,4},{7,5},{8,10},{9,11},{10,... | collective-permute-start | bytes 442376 | tf_op jit(solution)/shard_map/ppermute | solution.py:48
  12.1 11.5 %collective-permute-start.3 = (bf16[144,512]{1,0:T(8,128)(2,1)}, bf16[144,512]{1,0:T(8,128)(2,1)S(1)}, u32[]{:S(2)}, u32[]{:S(2)}) collective-permute-start(bf16[144,512]{1,0:T(8,128)(2,1)} %get-tuple-element.39), channel_id=1, source_target_pairs={{0,3},{1,0},{2,1},{3,2},{4,7},{5,4},{6,5},{7,6},{8,11},{9,8},{10,9... | collective-permute-start | bytes 442376 | tf_op jit(solution)/shard_map/ppermute | solution.py:48
  13.2 10.5 %copy-start = (f32[144,512]{1,0:T(8,128)S(1)}, f32[144,512]{1,0:T(8,128)}, u32[]{:S(2)}) copy-start(f32[144,512]{1,0:T(8,128)} %get-tuple-element.36.a) | copy-start | bytes 884740
  13.2 63.1 %copy-start.2 = (bf16[512,1024]{1,0:T(8,128)(2,1)S(1)}, bf16[512,1024]{1,0:T(8,128)(2,1)}, u32[]{:S(2)}) copy-start(bf16[512,1024]{1,0:T(8,128)(2,1)} %q_ref.1) | copy-start | bytes 3145732
  22.1 1.5 %collective-permute-start.4 = (f32[2,1024]{1,0:T(2,128)}, f32[2,1024]{1,0:T(2,128)S(1)}, u32[]{:S(2)}, u32[]{:S(2)}) collective-permute-start(f32[2,1024]{1,0:T(2,128)} %get-tuple-element.40.couple), channel_id=1, source_target_pairs={{0,4},{4,0},{1,5},{5,1},{2,6},{6,2},{3,7},{7,3},{8,12},{12,8},{9,1... | collective-permute-start | bytes 24584 | tf_op jit(solution)/shard_map/ppermute | solution.py:52
  23.6 0.7 copy-start.1
  25.1 8.7 %collective-permute-start.5 = (bf16[144,512]{1,0:T(8,128)(2,1)S(1)}, bf16[144,512]{1,0:T(8,128)(2,1)S(1)}, u32[]{:S(2)}, u32[]{:S(2)}) collective-permute-start(bf16[144,512]{1,0:T(8,128)(2,1)S(1)} %get-tuple-element.41.mine), channel_id=1, source_target_pairs={{0,8},{4,12},{8,16},{12,20},{16,24},{20,28},{24,32},{28,36},{32,40... | collective-permute-start | bytes 442376 | tf_op jit(solution)/shard_map/ppermute | solution.py:44
  27.9 8.4 %collective-permute-start.6 = (bf16[144,512]{1,0:T(8,128)(2,1)S(1)}, bf16[144,512]{1,0:T(8,128)(2,1)S(1)}, u32[]{:S(2)}, u32[]{:S(2)}) collective-permute-start(bf16[144,512]{1,0:T(8,128)(2,1)S(1)} %get-tuple-element.41.mine), channel_id=1, source_target_pairs={{0,16},{4,20},{8,24},{12,28},{16,32},{20,36},{24,40},{28,44},{32,4... | collective-permute-start | bytes 442376 | tf_op jit(solution)/shard_map/ppermute | solution.py:44
  36.4 14.7 %collective-permute-start.10 = (bf16[384,512]{1,0:T(8,128)(2,1)S(1)}, bf16[384,512]{1,0:T(8,128)(2,1)S(1)}, u32[]{:S(2)}, u32[]{:S(2)}) collective-permute-start(bf16[384,512]{1,0:T(8,128)(2,1)S(1)} %get-tuple-element.45.refs_0_), channel_id=1, source_target_pairs={{0,2},{1,3},{2,0},{3,1},{4,6},{5,7},{6,4},{7,5},{8,10},{9,11},{10,... | collective-permute-start | bytes 1179656 | tf_op jit(solution)/shard_map/ppermute | solution.py:48
  36.5 17.3 %collective-permute-start.11 = (bf16[384,512]{1,0:T(8,128)(2,1)S(1)}, bf16[384,512]{1,0:T(8,128)(2,1)S(1)}, u32[]{:S(2)}, u32[]{:S(2)}) collective-permute-start(bf16[384,512]{1,0:T(8,128)(2,1)S(1)} %get-tuple-element.45.refs_0_), channel_id=1, source_target_pairs={{0,3},{1,0},{2,1},{3,2},{4,7},{5,4},{6,5},{7,6},{8,11},{9,8},{10,9... | collective-permute-start | bytes 1179656 | tf_op jit(solution)/shard_map/ppermute | solution.py:48
  39.2 18.2 %collective-permute-start.9 = (bf16[384,512]{1,0:T(8,128)(2,1)S(1)}, bf16[384,512]{1,0:T(8,128)(2,1)S(1)}, u32[]{:S(2)}, u32[]{:S(2)}) collective-permute-start(bf16[384,512]{1,0:T(8,128)(2,1)S(1)} %get-tuple-element.45.refs_0_), channel_id=1, source_target_pairs={{0,1},{1,2},{2,3},{3,0},{4,5},{5,6},{6,7},{7,4},{8,9},{9,10},{10,1... | collective-permute-start | bytes 1179656 | tf_op jit(solution)/shard_map/ppermute | solution.py:48
  39.2 9.3 %collective-permute-start.7 = (f32[2,1024]{1,0:T(2,128)S(1)}, f32[2,1024]{1,0:T(2,128)S(1)}, u32[]{:S(2)}, u32[]{:S(2)}) collective-permute-start(f32[2,1024]{1,0:T(2,128)S(1)} %get-tuple-element.44), channel_id=1, source_target_pairs={{0,24},{4,28},{8,32},{12,36},{16,40},{20,44},{24,48},{28,52},{32,5... | collective-permute-start | bytes 24584 | tf_op jit(solution)/shard_map/ppermute | solution.py:44
  44.9 6.1 %collective-permute-start.8 = (f32[2,1024]{1,0:T(2,128)S(1)}, f32[2,1024]{1,0:T(2,128)S(1)}, u32[]{:S(2)}, u32[]{:S(2)}) collective-permute-start(f32[2,1024]{1,0:T(2,128)S(1)} %get-tuple-element.44), channel_id=1, source_target_pairs={{0,48},{4,52},{8,56},{12,60},{16,64},{20,68},{24,72},{28,76},{32,8... | collective-permute-start | bytes 24584 | tf_op jit(solution)/shard_map/ppermute | solution.py:44
  48.5 16.4 %collective-permute-start.15 = (bf16[384,512]{1,0:T(8,128)(2,1)S(1)}, bf16[384,512]{1,0:T(8,128)(2,1)S(1)}, u32[]{:S(2)}, u32[]{:S(2)}) collective-permute-start(bf16[384,512]{1,0:T(8,128)(2,1)S(1)} %get-tuple-element.45.refs_0_), channel_id=1, source_target_pairs={{0,4},{4,0},{1,5},{5,1},{2,6},{6,2},{3,7},{7,3},{8,12},{12,8},{9,1... | collective-permute-start | bytes 1179656 | tf_op jit(solution)/shard_map/ppermute | solution.py:52
  57.4 17.4 %collective-permute-start.16 = (bf16[384,512]{1,0:T(8,128)(2,1)S(1)}, bf16[384,512]{1,0:T(8,128)(2,1)S(1)}, u32[]{:S(2)}, u32[]{:S(2)}) collective-permute-start(bf16[384,512]{1,0:T(8,128)(2,1)S(1)} %collective-permute-done.9.refs_1_), channel_id=1, source_target_pairs={{0,4},{4,0},{1,5},{5,1},{2,6},{6,2},{3,7},{7,3},{8,12},{12,8},{9,1... | collective-permute-start | bytes 1179656 | tf_op jit(solution)/shard_map/ppermute | solution.py:52
  57.9 18.4 %collective-permute-start.17 = (bf16[384,512]{1,0:T(8,128)(2,1)S(1)}, bf16[384,512]{1,0:T(8,128)(2,1)S(1)}, u32[]{:S(2)}, u32[]{:S(2)}) collective-permute-start(bf16[384,512]{1,0:T(8,128)(2,1)S(1)} %collective-permute-done.10.refs_2_), channel_id=1, source_target_pairs={{0,4},{4,0},{1,5},{5,1},{2,6},{6,2},{3,7},{7,3},{8,12},{12,8},{9,1... | collective-permute-start | bytes 1179656 | tf_op jit(solution)/shard_map/ppermute | solution.py:52
  57.9 18.4 %collective-permute-start.18 = (bf16[384,512]{1,0:T(8,128)(2,1)S(1)}, bf16[384,512]{1,0:T(8,128)(2,1)S(1)}, u32[]{:S(2)}, u32[]{:S(2)}) collective-permute-start(bf16[384,512]{1,0:T(8,128)(2,1)S(1)} %collective-permute-done.11.refs_3_), channel_id=1, source_target_pairs={{0,4},{4,0},{1,5},{5,1},{2,6},{6,2},{3,7},{7,3},{8,12},{12,8},{9,1... | collective-permute-start | bytes 1179656 | tf_op jit(solution)/shard_map/ppermute | solution.py:52
  58.5 29.1 %copy-start.3 = (f32[512,1024]{1,0:T(8,128)S(1)}, f32[512,1024]{1,0:T(8,128)}, u32[]{:S(2)}) copy-start(f32[512,1024]{1,0:T(8,128)} %get-tuple-element.34) | copy-start | bytes 6291460
  58.5 29.1 %copy-start.4 = (f32[512,1024]{1,0:T(8,128)S(1)}, f32[512,1024]{1,0:T(8,128)}, u32[]{:S(2)}) copy-start(f32[512,1024]{1,0:T(8,128)} %get-tuple-element.35) | copy-start | bytes 6291460
  58.5 29.0 %collective-permute-start.12 = (f32[2,1024]{1,0:T(2,128)S(1)}, f32[2,1024]{1,0:T(2,128)S(1)}, u32[]{:S(2)}, u32[]{:S(2)}) collective-permute-start(f32[2,1024]{1,0:T(2,128)S(1)} %pad_maximum_fusion), channel_id=1, source_target_pairs={{0,72},{4,76},{8,80},{12,84},{16,88},{20,92},{24,96},{28,100},{32,... | collective-permute-start | bytes 24584 | tf_op jit(solution)/shard_map/ppermute | solution.py:44
  64.9 22.6 %collective-permute-start.13 = (f32[2,1024]{1,0:T(2,128)S(1)}, f32[2,1024]{1,0:T(2,128)S(1)}, u32[]{:S(2)}, u32[]{:S(2)}) collective-permute-start(f32[2,1024]{1,0:T(2,128)S(1)} %pad_maximum_fusion), channel_id=1, source_target_pairs={{0,144},{4,148},{8,152},{12,156},{16,160},{20,164},{24,168},{28,17... | collective-permute-start | bytes 24584 | tf_op jit(solution)/shard_map/ppermute | solution.py:44
  74.8 12.7 %collective-permute-start.14 = (f32[2,1024]{1,0:T(2,128)S(1)}, f32[2,1024]{1,0:T(2,128)S(1)}, u32[]{:S(2)}, u32[]{:S(2)}) collective-permute-start(f32[2,1024]{1,0:T(2,128)S(1)} %pad_maximum_fusion), channel_id=1, source_target_pairs={{0,216},{4,220},{8,224},{12,228},{16,232},{20,236},{24,240},{28,24... | collective-permute-start | bytes 24584 | tf_op jit(solution)/shard_map/ppermute | solution.py:44

commit v5 on v4

--- a/solution.py
+++ b/solution.py
@@ -44,6 +44,13 @@
     return lax.ppermute(value, SEQ, [(k, k + steps) for k in range(count - steps)])
 
 
+def forked(value, near, distant):
+    chips = lax.axis_size(SEQ) // 2
+    pairs = [(2 * c, 2 * (c + near)) for c in range(chips - near)]
+    pairs += [(2 * c + 1, 2 * (c + distant) + 1) for c in range(chips - distant)]
+    return lax.ppermute(value, SEQ, pairs)
+
+
 def turned(value, steps):
     return lax.ppermute(value, "mp", [(k, (k + steps) % PARTS) for k in range(PARTS)])
 
@@ -88,26 +95,16 @@
     return (high, middle, rest - middle)
 
 
-def norm_kernel(info, a, b, c, d, couple, other, out, before, inclusive):
+def norm_kernel(a, b, c, d, couple, out):
     total = (a[...] + b[...].astype(F32)) + (c[...].astype(F32) + d[...].astype(F32))
     line = total[QUARTER : QUARTER + 1, 0:QUARTER] + total[QUARTER + 1 : QUARTER + 2, 0:QUARTER]
     column = jnp.broadcast_to(line, (QUARTER, QUARTER)).T[:, 0:1]
     root = jnp.sqrt(column / D + norm_epsilon)
     out[0:QUARTER, :] = (total[0:QUARTER] / root).astype(BF16)
-    first = info[0] == 0
-    mine, theirs = (couple[...], other[...])
-    earlier = jnp.where(first, mine, theirs)
-    later = jnp.where(first, theirs, mine)
-    factor = earlier[0:1] * later[0:1]
-    state = later[0:1] * earlier[1:2] + later[1:2]
-    inclusive[0:1, :] = factor
-    inclusive[1:2, :] = state
-    before[0:1, :] = jnp.where(first, jnp.ones_like(factor), theirs[0:1])
-    before[1:2, :] = jnp.where(first, jnp.zeros_like(state), theirs[1:2])
     width = 2 * HD
     lines = [
         part[:, k : k + width]
-        for value in (factor, state)
+        for value in (couple[0:1, :], couple[1:2, :])
         for part in split(value)
         for k in range(0, value.shape[1], width)
     ]
@@ -115,21 +112,17 @@
     out[QUARTER:, :] = jnp.concatenate(lines).astype(BF16)
 
 
-def normed(info, parts, couple, other):
+def normed(parts, couple):
     shape = parts[0].shape
     return pl.pallas_call(
         norm_kernel,
         name="normed",
-        out_shape=[
-            jax.ShapeDtypeStruct(shape, BF16),
-            jax.ShapeDtypeStruct(couple.shape, F32),
-            jax.ShapeDtypeStruct(couple.shape, F32),
-        ],
-        in_specs=[SMEM] + [whole(shape)] * PARTS + [whole(couple.shape)] * 2,
-        out_specs=[whole(shape), whole(couple.shape), whole(couple.shape)],
+        out_shape=jax.ShapeDtypeStruct(shape, BF16),
+        in_specs=[whole(shape)] * PARTS + [whole(couple.shape)],
+        out_specs=whole(shape),
         compiler_params=pltpu.CompilerParams(vmem_limit_bytes=8 << 20),
         cost_estimate=pl.CostEstimate(flops=1 << 20, bytes_accessed=5 << 17, transcendentals=0),
-    )(info, *parts, couple, other)
+    )(*parts, couple)
 
 
 def received(lines, channels):
@@ -146,36 +139,70 @@
     return values
 
 
-def window_kernel(mine, back2, back4, before, inclusive, trio, before_out, inclusive_out):
+def applied(earlier, later):
+    return (earlier[0] * later[0], later[0] * earlier[1] + later[1])
+
+
+def chosen(flag, first, second):
+    return [jnp.where(flag, x, y) for x, y in zip(first, second)]
+
+
+def window_kernel(info, pair, arrived, trio, before, inclusive, got):
     channels = before.shape[1]
-    passed = (before[0:1, :], before[1:2, :])
-    whole_chip = (inclusive[0:1, :], inclusive[1:2, :])
-    trio[0:QUARTER, :] = mine[0:QUARTER, :]
-    for k, ref in enumerate((back2, back4)):
-        trio[(k + 1) * QUARTER : (k + 2) * QUARTER, :] = ref[0:QUARTER, :]
-        factor, state = received(ref[QUARTER:, :].astype(F32), channels)
-        passed = (factor * passed[0], passed[0] * state + passed[1])
-        whole_chip = (factor * whole_chip[0], whole_chip[0] * state + whole_chip[1])
-    before_out[0:1, :], before_out[1:2, :] = passed
-    inclusive_out[0:1, :], inclusive_out[1:2, :] = whole_chip
-
-
-def window(mine, back2, back4, before, inclusive):
+    first = info[0] == 0
+    each = QUARTER + EXTRA
+    trio[0:QUARTER, :] = pair[0:QUARTER, :]
+    trio[QUARTER : 2 * QUARTER, :] = arrived[0:QUARTER, :]
+    trio[2 * QUARTER :, :] = arrived[each : each + QUARTER, :]
+    for ref, out in ((pair, inclusive), (arrived, got)):
+        mine = received(ref[QUARTER:each, :].astype(F32), channels)
+        theirs = received(ref[each + QUARTER :, :].astype(F32), channels)
+        chip = applied(chosen(first, mine, theirs), chosen(first, theirs, mine))
+        out[0:1, :], out[1:2, :] = chip
+        if ref is pair:
+            none = (jnp.ones_like(theirs[0]), jnp.zeros_like(theirs[1]))
+            before[0:1, :], before[1:2, :] = chosen(first, none, theirs)
+
+
+def window(info, pair, arrived, channels):
     shape = (3 * QUARTER, 2 * HD)
-    couple = whole(before.shape)
+    couple = (2, channels)
     return pl.pallas_call(
         window_kernel,
         name="window",
-        out_shape=[
-            jax.ShapeDtypeStruct(shape, BF16),
-            jax.ShapeDtypeStruct(before.shape, F32),
-            jax.ShapeDtypeStruct(before.shape, F32),
-        ],
-        in_specs=[whole(mine.shape)] * 3 + [couple] * 2,
-        out_specs=[whole(shape), couple, couple],
+        out_shape=[jax.ShapeDtypeStruct(shape, BF16)] + [jax.ShapeDtypeStruct(couple, F32)] * 3,
+        in_specs=[SMEM] + [whole(pair.shape)] * 2,
+        out_specs=[whole(shape)] + [whole(couple)] * 3,
         compiler_params=pltpu.CompilerParams(vmem_limit_bytes=8 << 20),
         cost_estimate=pl.CostEstimate(flops=1 << 14, bytes_accessed=3 << 18, transcendentals=0),
-    )(mine, back2, back4, before, inclusive)
+    )(info, pair, arrived)
+
+
+def merge_kernel(info, before, inclusive, mine, theirs, before_out, inclusive_out):
+    first = info[0] == 0
+    passed = (before[0:1, :], before[1:2, :])
+    covered = (inclusive[0:1, :], inclusive[1:2, :])
+    for at in range(0, mine.shape[0], 2):
+        ours = (mine[at : at + 1, :], mine[at + 1 : at + 2, :])
+        other = (theirs[at : at + 1, :], theirs[at + 1 : at + 2, :])
+        for earlier in (chosen(first, ours, other), chosen(first, other, ours)):
+            passed = applied(earlier, passed)
+            covered = applied(earlier, covered)
+    before_out[0:1, :], before_out[1:2, :] = passed
+    inclusive_out[0:1, :], inclusive_out[1:2, :] = covered
+
+
+def merged(info, before, inclusive, mine, theirs):
+    couple = whole(before.shape)
+    return pl.pallas_call(
+        merge_kernel,
+        name="merged",
+        out_shape=[jax.ShapeDtypeStruct(before.shape, F32)] * 2,
+        in_specs=[SMEM, couple, couple, whole(mine.shape), whole(mine.shape)],
+        out_specs=[couple, couple],
+        compiler_params=pltpu.CompilerParams(vmem_limit_bytes=4 << 20),
+        cost_estimate=pl.CostEstimate(flops=1 << 14, bytes_accessed=1 << 16, transcendentals=0),
+    )(info, before, inclusive, mine, theirs)
 
 
 def negative_expm1(y, grown):
@@ -328,19 +355,21 @@
     out, kv = refs[-2:]
     core, position, place = (info[0], info[1], info[2])
 
-    @pl.when(pl.program_id(0) == 0)
-    def _():
-        for k in range(PARTS):
-            row = lax.rem(place + PARTS - k, PARTS) * QUARTER
-            for behind in range(SHARDS):
-                there = pl.ds(
-                    pl.multiple_of((SHARDS - 1 - behind) * TOK + row, QUARTER), QUARTER
-                )
-                if behind % 2 == 0:
-                    kv[there, :] = own[k][behind // 2 * QUARTER : (behind // 2 + 1) * QUARTER, :]
-                else:
-                    begin = pl.multiple_of(((behind + 1) // 2 - core) * QUARTER, QUARTER)
-                    kv[there, :] = other[k][pl.ds(begin, QUARTER), :]
+    sources = (
+        ((own, 0), (own, 2), (own, 1), (other, 1), (other, 2)),
+        ((own, 0), (other, 0), (other, 2), (other, 1), (own, 1)),
+    )
+    for which in range(2):
+
+        @pl.when((pl.program_id(0) == 0) & (core == which))
+        def _():
+            for k in range(PARTS):
+                row = lax.rem(place + PARTS - k, PARTS) * QUARTER
+                for behind, (pieces, slot) in enumerate(sources[which]):
+                    there = (SHARDS - 1 - behind) * TOK + row
+                    kv[pl.ds(pl.multiple_of(there, QUARTER), QUARTER), :] = pieces[k][
+                        slot * QUARTER : (slot + 1) * QUARTER, :
+                    ]
 
     @pl.when(position >= SHARDS - 1)
     def _():
@@ -371,10 +400,6 @@
             flops=count << 30, bytes_accessed=4 << 20, transcendentals=count << 20
         ),
     )(*inputs, *filled)
-
-
-def compose(earlier, later):
-    return jnp.stack([earlier[0] * later[0], later[0] * earlier[1] + later[1]])
 
 
 def shards(
@@ -409,23 +434,22 @@
     )
     groups = branch_in.shape[1] // BLK
     u, w, couple = recur(0, groups, branch_in, edge, *rest, ())
-    mine, before, inclusive = normed(info, [parts[0]] + arrived, couple, swapped(couple))
-    trio, before, inclusive = window(
-        mine, shifted(mine, 2), shifted(mine, 4), before, inclusive
-    )
+    own_part, couple = lax.optimization_barrier((parts[0], couple))
+    mine = normed([own_part] + arrived, couple)
+    pair = jnp.concatenate([mine, swapped(mine)])
+    trio, before, inclusive, got = window(info, pair, forked(pair, 1, 2), branch_in.shape[1])
     own = [trio] + [turned(trio, k) for k in range(1, PARTS)]
-    far = [shifted(inclusive, 6 * k) for k in (1, 2)]
+    before, inclusive = merged(info, before, inclusive, got, swapped(got))
+    far = [forked(inclusive, 3, 6), forked(inclusive, 9, 12)]
     *far, own[1], own[2], own[3] = lax.optimization_barrier((*far, *own[1:]))
-    for couple in far:
-        before = compose(couple, before)
-        inclusive = compose(couple, inclusive)
+    far = jnp.concatenate(far)
+    before, inclusive = merged(info, before, inclusive, far, swapped(far))
     other = [swapped(piece) for piece in own]
-    far = [shifted(inclusive, 18 * k) for k in (1, 2, 3)]
+    far = forked(inclusive, 15, 30)
     heads = queries.shape[1] // HD
     attended = attend(0, heads, info, queries, own, other, ())
-    *far, attended = lax.optimization_barrier((*far, attended))
-    for couple in far:
-        before = compose(couple, before)
+    far, attended = lax.optimization_barrier((far, attended))
+    before, _ = merged(info, before, inclusive, far, swapped(far))
     recurrent_out = (u + w * before[1:2]).astype(BF16)
     return (recurrent_out, attended)
 

time: 90.2 us -> 91.1 us (level)
  Pallas kernels: 24 us -> 26.3 us
  waiting for transfers between devices: 10.3 us -> 9.01 us
    ppermute x8 -> x1, starting transfers between devices: 39.3 us -> 3.67 us  [shifted(): lax.ppermute(value, SEQ, [(k, k + steps) for k in range(count - steps)])]
    ppermute x0 -> x4, starting transfers between devices: none -> 26.8 us  [forked(): return lax.ppermute(value, SEQ, pairs)]
    ppermute x5 -> x8, starting transfers between devices: 3.59 us -> 13.8 us  [swapped(): return lax.ppermute(value, CORE, [(0, 1), (1, 0)])]
    ppermute x6, waiting for transfers between devices: 6.41 us -> 0.02 us  [turned(): lax.ppermute(value, 'mp', [(k, (k + steps) % PARTS) for k in range(PARTS)])]
    ppermute x0 -> x4, waiting for transfers between devices: none -> 4.22 us  [forked(): return lax.ppermute(value, SEQ, pairs)]
    ppermute x5 -> x8, waiting for transfers between devices: 1.3 us -> 4.77 us  [swapped(): return lax.ppermute(value, CORE, [(0, 1), (1, 0)])]
    ppermute x8 -> x1, waiting for transfers between devices: 2.55 us -> 0.01 us  [shifted(): lax.ppermute(value, SEQ, [(k, k + steps) for k in range(count - steps)])]
    pallas_call x1 -> x4, Pallas kernels: 0.74 us -> 2.45 us  [the longest x3 2.25 us: merged(): pl.pallas_call(merge_kernel, name='merged', out_shape=[jax.ShapeDtypeStru...]
  transfers between devices with their start and end apart: 19 -> 19, of which waited for: 4 -> 6; matrix products, arithmetic and copies ran while one was open for 0% -> 0% of each run, Pallas kernels for 26% -> 27%
where the time goes in v5:
time: 91.1 us; the launch traced here: 90.7 us
  starting transfers between devices  51.5 us (57%)
  Pallas kernels  26.3 us (29%)
  waiting for transfers between devices  9.01 us (10%)
  other arithmetic  1.6 us (2%)
  local copies, waits for them, and re-layouts  1.44 us (2%)
    ppermute x4, starting transfers between devices, forked(): return lax.ppermute(value, SEQ, pairs)  26.8 us
    ppermute x8, starting transfers between devices, swapped(): return lax.ppermute(value, CORE, [(0, 1), (1, 0)])  13.8 us
    pallas_call x1, Pallas kernels, attend(): pl.pallas_call(attend_kernel, name='attend', grid=(count,), out_shape=jax...  11.2 us
    pallas_call x1, Pallas kernels, recur(): pl.pallas_call(recur_kernel, name='recur', grid=(count,), out_shape=[jax....  8.95 us
    ppermute x6, starting transfers between devices, turned(): lax.ppermute(value, 'mp', [(k, (k + steps) % PARTS) for k in range(PARTS)])  7.32 us
    ppermute x8, waiting for transfers between devices, swapped(): return lax.ppermute(value, CORE, [(0, 1), (1, 0)])  4.77 us
    ppermute x4, waiting for transfers between devices, forked(): return lax.ppermute(value, SEQ, pairs)  4.22 us
    ppermute x1, starting transfers between devices, shifted(): lax.ppermute(value, SEQ, [(k, k + steps) for k in range(count - steps)])  3.67 us
  transfers between devices with their start and end apart: 19, of which 6 were waited for; matrix products, arithmetic and copies ran while one was open for 0% of the time, Pallas kernels for 27%

profile of v5, /device:TPU:3, one launch (start us, length us, event | category | flops | bytes accessed | tf_op | source)
XLA Modules:
  0.0 90.7 jit_solution(11557085104599180185)
XLA Ops:
  0.6 0.7 slice.6
  1.4 3.7 %collective-permute-start = (bf16[3,1024]{1,0:T(4,128)(2,1)S(1)}, bf16[3,1024]{1,0:T(4,128)(2,1)S(1)}, u32[]{:S(2)}, u32[]{:S(2)}) collective-permute-start(bf16[3,1024]{1,0:T(4,128)(2,1)S(1)} %slice.6), channel_id=1, source_target_pairs={{0,4},{4,8},{8,12},{12,16},{16,20},{20,24},{24,28},{28,32},{32,36}... | collective-permute-start | bytes 18440 | tf_op jit(solution)/shard_map/ppermute | solution.py:44
  5.0 3.1 %project.1 = (f32[144,512]{1,0:T(8,128)}, bf16[144,512]{1,0:T(8,128)(2,1)}, bf16[144,512]{1,0:T(8,128)(2,1)}, bf16[144,512]{1,0:T(8,128)(2,1)}) custom-call(s32[1]{0:T(128)} %bitcast.place, bf16[512,1024]{1,0:T(8,128)(2,1)} %stream.1, f32[1,1024]{1,0:T(1,128)} %bitcast.10, bf16[1024,512]{1,0:T(8,128)(2,1)} %weight.1), custom_call_target="tpu_custom_call" | custom-call | flops 536870912 | bytes 3145728 | tf_op jit(solution)/shard_map/project/pallas_call | solution.py:80
  8.1 0.0 collective-permute-done.edge
  8.1 1.4 %collective-permute-start.1 = (bf16[144,512]{1,0:T(8,128)(2,1)}, bf16[144,512]{1,0:T(8,128)(2,1)S(1)}, u32[]{:S(2)}, u32[]{:S(2)}) collective-permute-start(bf16[144,512]{1,0:T(8,128)(2,1)} %get-tuple-element.42), channel_id=1, source_target_pairs={{0,1},{1,2},{2,3},{3,0},{4,5},{5,6},{6,7},{7,4},{8,9},{9,10},{10,1... | collective-permute-start | bytes 442376 | tf_op jit(solution)/shard_map/ppermute | solution.py:55
  9.5 2.6 %collective-permute-start.2 = (bf16[144,512]{1,0:T(8,128)(2,1)}, bf16[144,512]{1,0:T(8,128)(2,1)S(1)}, u32[]{:S(2)}, u32[]{:S(2)}) collective-permute-start(bf16[144,512]{1,0:T(8,128)(2,1)} %get-tuple-element.43), channel_id=1, source_target_pairs={{0,2},{1,3},{2,0},{3,1},{4,6},{5,7},{6,4},{7,5},{8,10},{9,11},{10,... | collective-permute-start | bytes 442376 | tf_op jit(solution)/shard_map/ppermute | solution.py:55
  12.1 1.1 %collective-permute-start.3 = (bf16[144,512]{1,0:T(8,128)(2,1)}, bf16[144,512]{1,0:T(8,128)(2,1)S(1)}, u32[]{:S(2)}, u32[]{:S(2)}) collective-permute-start(bf16[144,512]{1,0:T(8,128)(2,1)} %get-tuple-element.44), channel_id=1, source_target_pairs={{0,3},{1,0},{2,1},{3,2},{4,7},{5,4},{6,5},{7,6},{8,11},{9,8},{10,9... | collective-permute-start | bytes 442376 | tf_op jit(solution)/shard_map/ppermute | solution.py:55
  13.2 8.9 %recur.1 = (f32[512,1024]{1,0:T(8,128)}, f32[512,1024]{1,0:T(8,128)}, f32[2,1024]{1,0:T(2,128)}) custom-call(bf16[512,1024]{1,0:T(8,128)(2,1)} %branch.1, bf16[3,1024]{1,0:T(4,128)(2,1)} %copy-done.5, bf16[512,1024]{1,0:T(8,128)(2,1)} %gate.1, f32[4,1024]{1,0:T(4,128)} %taps.1, f32[1,1024]{1,0:T(1,128)} %bitcast.11, bf16[4,256,256]{2,1,0:T(8,128)(2,1)} %in_w.1, ...), custom_call_target="tpu_custom_call" | custom-call | flops 1073741824 | bytes 8388608 | tf_op jit(solution)/shard_map/recur/pallas_call | solution.py:283
  22.1 0.0 collective-permute-done.1.b
  22.1 0.0 collective-permute-done.2.c
  22.1 0.0 collective-permute-done.3.d
  22.2 0.7 copy-done.1
  22.9 0.2 normed.1
  23.1 0.1 collective-permute-start.4
  23.2 1.4 %collective-permute-done.4 = bf16[144,512]{1,0:T(8,128)(2,1)S(1)} collective-permute-done((bf16[144,512]{1,0:T(8,128)(2,1)S(1)}, bf16[144,512]{1,0:T(8,128)(2,1)S(1)}, u32[]{:S(2)}, u32[]{:S(2)}) %collective-permute-start.4) | collective-permute-done | bytes 147488 | tf_op jit(solution)/shard_map/ppermute | solution.py:59
  24.5 4.1 %collective-permute-start.5 = (bf16[288,512]{1,0:T(8,128)(2,1)S(1)}, bf16[288,512]{1,0:T(8,128)(2,1)S(1)}, u32[]{:S(2)}, u32[]{:S(2)}) collective-permute-start(bf16[288,512]{1,0:T(8,128)(2,1)S(1)} %pad_maximum_fusion.pair), channel_id=1, source_target_pairs={{0,8},{8,16},{16,24},{24,32},{32,40},{40,48},{48,56},{56,64},{64,7... | collective-permute-start | bytes 884744 | tf_op jit(solution)/shard_map/ppermute | solution.py:51
  28.7 0.1 pad_add_fusion.info
  28.7 3.5 %collective-permute-done.5.arrived = bf16[288,512]{1,0:T(8,128)(2,1)S(1)} collective-permute-done((bf16[288,512]{1,0:T(8,128)(2,1)S(1)}, bf16[288,512]{1,0:T(8,128)(2,1)S(1)}, u32[]{:S(2)}, u32[]{:S(2)}) %collective-permute-start.5) | collective-permute-done | bytes 294944 | tf_op jit(solution)/shard_map/ppermute | solution.py:51
  32.3 0.6 window.1
  32.9 0.1 collective-permute-start.11
  33.0 2.2 %collective-permute-start.10 = (bf16[384,512]{1,0:T(8,128)(2,1)S(1)}, bf16[384,512]{1,0:T(8,128)(2,1)S(1)}, u32[]{:S(2)}, u32[]{:S(2)}) collective-permute-start(bf16[384,512]{1,0:T(8,128)(2,1)S(1)} %get-tuple-element.51.refs_0_), channel_id=1, source_target_pairs={{0,2},{1,3},{2,0},{3,1},{4,6},{5,7},{6,4},{7,5},{8,10},{9,11},{10,... | collective-permute-start | bytes 1179656 | tf_op jit(solution)/shard_map/ppermute | solution.py:55
  35.2 0.0 collective-permute-start.9
  35.2 4.2 %collective-permute-start.6 = (f32[2,1024]{1,0:T(2,128)S(1)}, f32[2,1024]{1,0:T(2,128)S(1)}, u32[]{:S(2)}, u32[]{:S(2)}) collective-permute-start(f32[2,1024]{1,0:T(2,128)S(1)} %get-tuple-element.48.mine), channel_id=1, source_target_pairs={{0,4},{4,0},{1,5},{5,1},{2,6},{6,2},{3,7},{7,3},{8,12},{12,8},{9,1... | collective-permute-start | bytes 24584 | tf_op jit(solution)/shard_map/ppermute | solution.py:59
  39.4 0.8 collective-permute-done.6.theirs
  40.2 0.6 merged.3
  40.7 6.6 %collective-permute-start.8 = (f32[2,1024]{1,0:T(2,128)S(1)}, f32[2,1024]{1,0:T(2,128)S(1)}, u32[]{:S(2)}, u32[]{:S(2)}) collective-permute-start(f32[2,1024]{1,0:T(2,128)S(1)} %get-tuple-element.50.inclusive), channel_id=1, source_target_pairs={{0,72},{8,80},{16,88},{24,96},{32,104},{40,112},{48,120},{56,128},... | collective-permute-start | bytes 24584 | tf_op jit(solution)/shard_map/ppermute | solution.py:51
  47.3 6.2 %collective-permute-start.7 = (f32[2,1024]{1,0:T(2,128)S(1)}, f32[2,1024]{1,0:T(2,128)S(1)}, u32[]{:S(2)}, u32[]{:S(2)}) collective-permute-start(f32[2,1024]{1,0:T(2,128)S(1)} %get-tuple-element.50.inclusive), channel_id=1, source_target_pairs={{0,24},{8,32},{16,40},{24,48},{32,56},{40,64},{48,72},{56,80},{64,... | collective-permute-start | bytes 24584 | tf_op jit(solution)/shard_map/ppermute | solution.py:51
  53.5 0.0 collective-permute-done.8
  53.5 0.1 collective-permute-start.14
  53.6 0.7 collective-permute-done.7
  54.3 0.0 collective-permute-done.11.refs_3_
  54.3 0.0 collective-permute-done.10.refs_2_
  54.3 0.0 collective-permute-done.9.refs_1_
  54.3 0.3 collective-permute-start.15
  54.6 0.3 collective-permute-start.16
  54.9 0.2 collective-permute-start.17
  55.1 0.4 collective-permute-start.12
  55.5 1.7 %collective-permute-done.12.theirs = f32[4,1024]{1,0:T(4,128)S(1)} collective-permute-done((f32[4,1024]{1,0:T(4,128)S(1)}, f32[4,1024]{1,0:T(4,128)S(1)}, u32[]{:S(2)}, u32[]{:S(2)}) %collective-permute-start.12) | collective-permute-done | bytes 16416 | tf_op jit(solution)/shard_map/ppermute | solution.py:59
  57.2 0.6 merged.4
  57.8 9.9 %collective-permute-start.13 = (f32[2,1024]{1,0:T(2,128)S(1)}, f32[2,1024]{1,0:T(2,128)S(1)}, u32[]{:S(2)}, u32[]{:S(2)}) collective-permute-start(f32[2,1024]{1,0:T(2,128)S(1)} %get-tuple-element.55.inclusive), channel_id=1, source_target_pairs={{0,120},{8,128},{16,136},{24,144},{32,152},{40,160},{48,168},{56,1... | collective-permute-start | bytes 24584 | tf_op jit(solution)/shard_map/ppermute | solution.py:51
  67.7 0.0 collective-permute-done.14.refs_4_
  67.8 0.0 collective-permute-done.15.refs_5_
  67.8 0.0 collective-permute-done.17.refs_7_
  67.8 11.2 %attend.1 = bf16[512,1024]{1,0:T(8,128)(2,1)} custom-call(s32[3]{0:T(128)S(1)} %pad_add_fusion.info, bf16[512,1024]{1,0:T(8,128)(2,1)S(1)} %copy-done.2, bf16[384,512]{1,0:T(8,128)(2,1)S(1)} %get-tuple-element.51.refs_0_, bf16[384,512]{1,0:T(8,128)(2,1)S(1)} %collective-permute-done.9.refs_1_, bf16[384,512]{1,0:T(8,128)(2,1)S(1)} %collective-permute-done.10.refs_2_, ...), custom_call_target="tpu_custom_call" | custom-call | flops 4294967296 | bytes 4194304 | tf_op jit(solution)/shard_map/attend/pallas_call | solution.py:389
  79.0 8.2 %collective-permute-start.18 = (f32[2,1024]{1,0:T(2,128)S(1)}, f32[2,1024]{1,0:T(2,128)S(1)}, u32[]{:S(2)}, u32[]{:S(2)}) collective-permute-start(f32[2,1024]{1,0:T(2,128)S(1)} %collective-permute-done.13.mine), channel_id=1, source_target_pairs={{0,4},{4,0},{1,5},{5,1},{2,6},{6,2},{3,7},{7,3},{8,12},{12,8},{9,1... | collective-permute-start | bytes 24584 | tf_op jit(solution)/shard_map/ppermute | solution.py:59
  87.2 0.8 collective-permute-done.18.theirs
  88.1 1.1 %merged.5 = (f32[2,1024]{1,0:T(2,128)S(1)}, f32[2,1024]{1,0:T(2,128)}) custom-call(s32[3]{0:T(128)S(1)} %pad_add_fusion.info, f32[2,1024]{1,0:T(2,128)S(1)} %get-tuple-element.54.before, f32[2,1024]{1,0:T(2,128)S(1)} %get-tuple-element.55.inclusive, f32[2,1024]{1,0:T(2,128)S(1)} %collective-permute-done.13.mine, f32[2,1024]{1,0:T(2,128)S(1)} %collective-permute-done.18.theirs), custom_call_target="tpu_custom_call" | custom-call | flops 16384 | bytes 65536 | tf_op jit(solution)/shard_map/merged/pallas_call | solution.py:197
  89.2 1.5 %add_convert_fusion = bf16[512,1024]{1,0:T(8,128)(2,1)} fusion(f32[512,1024]{1,0:T(8,128)S(1)} %copy-done.3, f32[512,1024]{1,0:T(8,128)S(1)} %copy-done.4, f32[1024]{0:T(1024)S(1)} %bitcast.9), kind=kLoop, calls=%fused_computation | loop fusion | flops 1572864 | bytes 5246976 | tf_op jit(solution)/shard_map/convert_element_type | solution.py:453
  (16 shorter events, 0.1 us)
Async XLA Ops:
  1.4 6.7 %collective-permute-start = (bf16[3,1024]{1,0:T(4,128)(2,1)S(1)}, bf16[3,1024]{1,0:T(4,128)(2,1)S(1)}, u32[]{:S(2)}, u32[]{:S(2)}) collective-permute-start(bf16[3,1024]{1,0:T(4,128)(2,1)S(1)} %slice.6), channel_id=1, source_target_pairs={{0,4},{4,8},{8,12},{12,16},{16,20},{20,24},{24,28},{28,32},{32,36}... | collective-permute-start | bytes 18440 | tf_op jit(solution)/shard_map/ppermute | solution.py:44
  8.1 5.1 %copy-start.5 = (bf16[3,1024]{1,0:T(4,128)(2,1)}, bf16[3,1024]{1,0:T(4,128)(2,1)S(1)}, u32[]{:S(2)}) copy-start(bf16[3,1024]{1,0:T(4,128)(2,1)S(1)} %collective-permute-done.edge) | copy-start | bytes 18436
  8.1 14.0 %collective-permute-start.1 = (bf16[144,512]{1,0:T(8,128)(2,1)}, bf16[144,512]{1,0:T(8,128)(2,1)S(1)}, u32[]{:S(2)}, u32[]{:S(2)}) collective-permute-start(bf16[144,512]{1,0:T(8,128)(2,1)} %get-tuple-element.42), channel_id=1, source_target_pairs={{0,1},{1,2},{2,3},{3,0},{4,5},{5,6},{6,7},{7,4},{8,9},{9,10},{10,1... | collective-permute-start | bytes 442376 | tf_op jit(solution)/shard_map/ppermute | solution.py:55
  9.5 12.7 %collective-permute-start.2 = (bf16[144,512]{1,0:T(8,128)(2,1)}, bf16[144,512]{1,0:T(8,128)(2,1)S(1)}, u32[]{:S(2)}, u32[]{:S(2)}) collective-permute-start(bf16[144,512]{1,0:T(8,128)(2,1)} %get-tuple-element.43), channel_id=1, source_target_pairs={{0,2},{1,3},{2,0},{3,1},{4,6},{5,7},{6,4},{7,5},{8,10},{9,11},{10,... | collective-permute-start | bytes 442376 | tf_op jit(solution)/shard_map/ppermute | solution.py:55
  12.1 10.0 %collective-permute-start.3 = (bf16[144,512]{1,0:T(8,128)(2,1)}, bf16[144,512]{1,0:T(8,128)(2,1)S(1)}, u32[]{:S(2)}, u32[]{:S(2)}) collective-permute-start(bf16[144,512]{1,0:T(8,128)(2,1)} %get-tuple-element.44), channel_id=1, source_target_pairs={{0,3},{1,0},{2,1},{3,2},{4,7},{5,4},{6,5},{7,6},{8,11},{9,8},{10,9... | collective-permute-start | bytes 442376 | tf_op jit(solution)/shard_map/ppermute | solution.py:55
  13.2 9.0 %copy-start = (f32[144,512]{1,0:T(8,128)S(1)}, f32[144,512]{1,0:T(8,128)}, u32[]{:S(2)}) copy-start(f32[144,512]{1,0:T(8,128)} %get-tuple-element.41.a) | copy-start | bytes 884740
  13.2 54.6 %copy-start.2 = (bf16[512,1024]{1,0:T(8,128)(2,1)S(1)}, bf16[512,1024]{1,0:T(8,128)(2,1)}, u32[]{:S(2)}) copy-start(bf16[512,1024]{1,0:T(8,128)(2,1)} %q_ref.1) | copy-start | bytes 3145732
  22.2 0.7 copy-start.1
  23.1 1.5 %collective-permute-start.4 = (bf16[144,512]{1,0:T(8,128)(2,1)S(1)}, bf16[144,512]{1,0:T(8,128)(2,1)S(1)}, u32[]{:S(2)}, u32[]{:S(2)}) collective-permute-start(bf16[144,512]{1,0:T(8,128)(2,1)S(1)} %normed.1), channel_id=1, source_target_pairs={{0,4},{4,0},{1,5},{5,1},{2,6},{6,2},{3,7},{7,3},{8,12},{12,8},{9,1... | collective-permute-start | bytes 442376 | tf_op jit(solution)/shard_map/ppermute | solution.py:59
  24.5 7.7 %collective-permute-start.5 = (bf16[288,512]{1,0:T(8,128)(2,1)S(1)}, bf16[288,512]{1,0:T(8,128)(2,1)S(1)}, u32[]{:S(2)}, u32[]{:S(2)}) collective-permute-start(bf16[288,512]{1,0:T(8,128)(2,1)S(1)} %pad_maximum_fusion.pair), channel_id=1, source_target_pairs={{0,8},{8,16},{16,24},{24,32},{32,40},{40,48},{48,56},{56,64},{64,7... | collective-permute-start | bytes 884744 | tf_op jit(solution)/shard_map/ppermute | solution.py:51
  32.9 21.3 %collective-permute-start.11 = (bf16[384,512]{1,0:T(8,128)(2,1)S(1)}, bf16[384,512]{1,0:T(8,128)(2,1)S(1)}, u32[]{:S(2)}, u32[]{:S(2)}) collective-permute-start(bf16[384,512]{1,0:T(8,128)(2,1)S(1)} %get-tuple-element.51.refs_0_), channel_id=1, source_target_pairs={{0,3},{1,0},{2,1},{3,2},{4,7},{5,4},{6,5},{7,6},{8,11},{9,8},{10,9... | collective-permute-start | bytes 1179656 | tf_op jit(solution)/shard_map/ppermute | solution.py:55
  33.0 21.2 %collective-permute-start.10 = (bf16[384,512]{1,0:T(8,128)(2,1)S(1)}, bf16[384,512]{1,0:T(8,128)(2,1)S(1)}, u32[]{:S(2)}, u32[]{:S(2)}) collective-permute-start(bf16[384,512]{1,0:T(8,128)(2,1)S(1)} %get-tuple-element.51.refs_0_), channel_id=1, source_target_pairs={{0,2},{1,3},{2,0},{3,1},{4,6},{5,7},{6,4},{7,5},{8,10},{9,11},{10,... | collective-permute-start | bytes 1179656 | tf_op jit(solution)/shard_map/ppermute | solution.py:55
  35.2 19.1 %collective-permute-start.9 = (bf16[384,512]{1,0:T(8,128)(2,1)S(1)}, bf16[384,512]{1,0:T(8,128)(2,1)S(1)}, u32[]{:S(2)}, u32[]{:S(2)}) collective-permute-start(bf16[384,512]{1,0:T(8,128)(2,1)S(1)} %get-tuple-element.51.refs_0_), channel_id=1, source_target_pairs={{0,1},{1,2},{2,3},{3,0},{4,5},{5,6},{6,7},{7,4},{8,9},{9,10},{10,1... | collective-permute-start | bytes 1179656 | tf_op jit(solution)/shard_map/ppermute | solution.py:55
  35.2 5.0 %collective-permute-start.6 = (f32[2,1024]{1,0:T(2,128)S(1)}, f32[2,1024]{1,0:T(2,128)S(1)}, u32[]{:S(2)}, u32[]{:S(2)}) collective-permute-start(f32[2,1024]{1,0:T(2,128)S(1)} %get-tuple-element.48.mine), channel_id=1, source_target_pairs={{0,4},{4,0},{1,5},{5,1},{2,6},{6,2},{3,7},{7,3},{8,12},{12,8},{9,1... | collective-permute-start | bytes 24584 | tf_op jit(solution)/shard_map/ppermute | solution.py:59
  40.7 12.7 %collective-permute-start.8 = (f32[2,1024]{1,0:T(2,128)S(1)}, f32[2,1024]{1,0:T(2,128)S(1)}, u32[]{:S(2)}, u32[]{:S(2)}) collective-permute-start(f32[2,1024]{1,0:T(2,128)S(1)} %get-tuple-element.50.inclusive), channel_id=1, source_target_pairs={{0,72},{8,80},{16,88},{24,96},{32,104},{40,112},{48,120},{56,128},... | collective-permute-start | bytes 24584 | tf_op jit(solution)/shard_map/ppermute | solution.py:51
  47.3 7.0 %collective-permute-start.7 = (f32[2,1024]{1,0:T(2,128)S(1)}, f32[2,1024]{1,0:T(2,128)S(1)}, u32[]{:S(2)}, u32[]{:S(2)}) collective-permute-start(f32[2,1024]{1,0:T(2,128)S(1)} %get-tuple-element.50.inclusive), channel_id=1, source_target_pairs={{0,24},{8,32},{16,40},{24,48},{32,56},{40,64},{48,72},{56,80},{64,... | collective-permute-start | bytes 24584 | tf_op jit(solution)/shard_map/ppermute | solution.py:51
  53.5 14.3 %collective-permute-start.14 = (bf16[384,512]{1,0:T(8,128)(2,1)S(1)}, bf16[384,512]{1,0:T(8,128)(2,1)S(1)}, u32[]{:S(2)}, u32[]{:S(2)}) collective-permute-start(bf16[384,512]{1,0:T(8,128)(2,1)S(1)} %get-tuple-element.51.refs_0_), channel_id=1, source_target_pairs={{0,4},{4,0},{1,5},{5,1},{2,6},{6,2},{3,7},{7,3},{8,12},{12,8},{9,1... | collective-permute-start | bytes 1179656 | tf_op jit(solution)/shard_map/ppermute | solution.py:59
  54.3 13.5 %collective-permute-start.15 = (bf16[384,512]{1,0:T(8,128)(2,1)S(1)}, bf16[384,512]{1,0:T(8,128)(2,1)S(1)}, u32[]{:S(2)}, u32[]{:S(2)}) collective-permute-start(bf16[384,512]{1,0:T(8,128)(2,1)S(1)} %collective-permute-done.9.refs_1_), channel_id=1, source_target_pairs={{0,4},{4,0},{1,5},{5,1},{2,6},{6,2},{3,7},{7,3},{8,12},{12,8},{9,1... | collective-permute-start | bytes 1179656 | tf_op jit(solution)/shard_map/ppermute | solution.py:59
  54.6 13.2 %collective-permute-start.16 = (bf16[384,512]{1,0:T(8,128)(2,1)S(1)}, bf16[384,512]{1,0:T(8,128)(2,1)S(1)}, u32[]{:S(2)}, u32[]{:S(2)}) collective-permute-start(bf16[384,512]{1,0:T(8,128)(2,1)S(1)} %collective-permute-done.10.refs_2_), channel_id=1, source_target_pairs={{0,4},{4,0},{1,5},{5,1},{2,6},{6,2},{3,7},{7,3},{8,12},{12,8},{9,1... | collective-permute-start | bytes 1179656 | tf_op jit(solution)/shard_map/ppermute | solution.py:59
  54.9 12.9 %collective-permute-start.17 = (bf16[384,512]{1,0:T(8,128)(2,1)S(1)}, bf16[384,512]{1,0:T(8,128)(2,1)S(1)}, u32[]{:S(2)}, u32[]{:S(2)}) collective-permute-start(bf16[384,512]{1,0:T(8,128)(2,1)S(1)} %collective-permute-done.11.refs_3_), channel_id=1, source_target_pairs={{0,4},{4,0},{1,5},{5,1},{2,6},{6,2},{3,7},{7,3},{8,12},{12,8},{9,1... | collective-permute-start | bytes 1179656 | tf_op jit(solution)/shard_map/ppermute | solution.py:59
  55.1 2.1 %collective-permute-start.12 = (f32[4,1024]{1,0:T(4,128)S(1)}, f32[4,1024]{1,0:T(4,128)S(1)}, u32[]{:S(2)}, u32[]{:S(2)}) collective-permute-start(f32[4,1024]{1,0:T(4,128)S(1)} %pad_maximum_fusion.1.mine), channel_id=1, source_target_pairs={{0,4},{4,0},{1,5},{5,1},{2,6},{6,2},{3,7},{7,3},{8,12},{12,8},{9,1... | collective-permute-start | bytes 49160 | tf_op jit(solution)/shard_map/ppermute | solution.py:59
  57.8 31.4 %copy-start.3 = (f32[512,1024]{1,0:T(8,128)S(1)}, f32[512,1024]{1,0:T(8,128)}, u32[]{:S(2)}) copy-start(f32[512,1024]{1,0:T(8,128)} %get-tuple-element.37) | copy-start | bytes 6291460
  57.8 31.4 %copy-start.4 = (f32[512,1024]{1,0:T(8,128)S(1)}, f32[512,1024]{1,0:T(8,128)}, u32[]{:S(2)}) copy-start(f32[512,1024]{1,0:T(8,128)} %get-tuple-element.38) | copy-start | bytes 6291460
  57.8 21.2 %collective-permute-start.13 = (f32[2,1024]{1,0:T(2,128)S(1)}, f32[2,1024]{1,0:T(2,128)S(1)}, u32[]{:S(2)}, u32[]{:S(2)}) collective-permute-start(f32[2,1024]{1,0:T(2,128)S(1)} %get-tuple-element.55.inclusive), channel_id=1, source_target_pairs={{0,120},{8,128},{16,136},{24,144},{32,152},{40,160},{48,168},{56,1... | collective-permute-start | bytes 24584 | tf_op jit(solution)/shard_map/ppermute | solution.py:51
  79.0 9.1 %collective-permute-start.18 = (f32[2,1024]{1,0:T(2,128)S(1)}, f32[2,1024]{1,0:T(2,128)S(1)}, u32[]{:S(2)}, u32[]{:S(2)}) collective-permute-start(f32[2,1024]{1,0:T(2,128)S(1)} %collective-permute-done.13.mine), channel_id=1, source_target_pairs={{0,4},{4,0},{1,5},{5,1},{2,6},{6,2},{3,7},{7,3},{8,12},{12,8},{9,1... | collective-permute-start | bytes 24584 | tf_op jit(solution)/shard_map/ppermute | solution.py:59

commit v6 on v5

--- a/solution.py
+++ b/solution.py
@@ -147,13 +147,12 @@
     return [jnp.where(flag, x, y) for x, y in zip(first, second)]
 
 
-def window_kernel(info, pair, arrived, trio, before, inclusive, got):
+def window_kernel(info, pair, arrived, duo, before, inclusive, got):
     channels = before.shape[1]
     first = info[0] == 0
     each = QUARTER + EXTRA
-    trio[0:QUARTER, :] = pair[0:QUARTER, :]
-    trio[QUARTER : 2 * QUARTER, :] = arrived[0:QUARTER, :]
-    trio[2 * QUARTER :, :] = arrived[each : each + QUARTER, :]
+    duo[0:QUARTER, :] = arrived[0:QUARTER, :]
+    duo[QUARTER:, :] = arrived[each : each + QUARTER, :]
     for ref, out in ((pair, inclusive), (arrived, got)):
         mine = received(ref[QUARTER:each, :].astype(F32), channels)
         theirs = received(ref[each + QUARTER :, :].astype(F32), channels)
@@ -165,7 +164,7 @@
 
 
 def window(info, pair, arrived, channels):
-    shape = (3 * QUARTER, 2 * HD)
+    shape = (2 * QUARTER, 2 * HD)
     couple = (2, channels)
     return pl.pallas_call(
         window_kernel,
@@ -351,13 +350,13 @@
 
 
 def attend_kernel(info, q_ref, *refs):
-    own, other = (refs[0:PARTS], refs[PARTS : 2 * PARTS])
+    own, two, other, others = [refs[k * PARTS : (k + 1) * PARTS] for k in range(4)]
     out, kv = refs[-2:]
     core, position, place = (info[0], info[1], info[2])
 
     sources = (
-        ((own, 0), (own, 2), (own, 1), (other, 1), (other, 2)),
-        ((own, 0), (other, 0), (other, 2), (other, 1), (own, 1)),
+        ((own, 0), (two, 1), (two, 0), (others, 0), (others, 1)),
+        ((own, 0), (other, 0), (others, 1), (others, 0), (two, 0)),
     )
     for which in range(2):
 
@@ -382,16 +381,16 @@
         )
 
 
-def attend(head, count, info, queries, own, other, filled):
+def attend(head, count, info, queries, pieces, filled):
     block = pl.BlockSpec((TOK, HD), lambda h: (0, h + head))
     kept = pl.BlockSpec(memory_space=pl.ANY)
-    inputs = (info, queries, *own, *other)
+    inputs = (info, queries, *pieces)
     return pl.pallas_call(
         attend_kernel,
         name="attend",
         grid=(count,),
         out_shape=jax.ShapeDtypeStruct(queries.shape, BF16),
-        in_specs=[SMEM, block] + [whole(own[0].shape)] * (2 * PARTS) + [kept] * len(filled),
+        in_specs=[SMEM, block] + [whole(piece.shape) for piece in pieces] + [kept] * len(filled),
         out_specs=block,
         scratch_shapes=[pltpu.VMEM((SHARDS * TOK, 2 * HD), BF16)],
         input_output_aliases={len(inputs) + k: k for k in range(len(filled))},
@@ -436,21 +435,28 @@
     u, w, couple = recur(0, groups, branch_in, edge, *rest, ())
     own_part, couple = lax.optimization_barrier((parts[0], couple))
     mine = normed([own_part] + arrived, couple)
-    pair = jnp.concatenate([mine, swapped(mine)])
-    trio, before, inclusive, got = window(info, pair, forked(pair, 1, 2), branch_in.shape[1])
-    own = [trio] + [turned(trio, k) for k in range(1, PARTS)]
+    beside = swapped(mine)
+    pair = jnp.concatenate([mine, beside])
+    own = [turned(mine, k) for k in range(1, PARTS)]
+    arrived, *own = lax.optimization_barrier((forked(pair, 1, 2), *own))
+    duo, before, inclusive, got = window(info, pair, arrived, branch_in.shape[1])
+    two = [turned(duo, k) for k in range(1, PARTS)]
     before, inclusive = merged(info, before, inclusive, got, swapped(got))
     far = [forked(inclusive, 3, 6), forked(inclusive, 9, 12)]
-    *far, own[1], own[2], own[3] = lax.optimization_barrier((*far, *own[1:]))
+    far, two, own, duo = lax.optimization_barrier((far, two, own, duo))
+    other = [swapped(piece) for piece in own]
     far = jnp.concatenate(far)
     before, inclusive = merged(info, before, inclusive, far, swapped(far))
-    other = [swapped(piece) for piece in own]
-    far = forked(inclusive, 15, 30)
+    two = [duo] + two
+    others = [swapped(piece) for piece in two]
+    far = [shifted(inclusive, 30), shifted(inclusive, 60)]
     heads = queries.shape[1] // HD
-    attended = attend(0, heads, info, queries, own, other, ())
-    far, attended = lax.optimization_barrier((far, attended))
-    before, _ = merged(info, before, inclusive, far, swapped(far))
-    recurrent_out = (u + w * before[1:2]).astype(BF16)
+    pieces = (mine, *own, *two, beside, *other, *others)
+    attended = attend(0, heads, info, queries, pieces, ())
+    *far, attended = lax.optimization_barrier((*far, attended))
+    state = far[0][0:1] * far[1][1:2] + far[0][1:2]
+    state = before[0:1] * state + before[1:2]
+    recurrent_out = (u + w * state).astype(BF16)
     return (recurrent_out, attended)
 
 

time: 91.1 us -> 85.3 us (0.936)
  starting transfers between devices: 51.5 us -> 42.8 us
  waiting for transfers between devices: 9.01 us -> 12.4 us
  Pallas kernels: 26.3 us -> 25.2 us
    ppermute x4 -> x3, starting transfers between devices: 26.8 us -> 16.1 us  [forked(): return lax.ppermute(value, SEQ, pairs)]
    ppermute x8 -> x10, starting transfers between devices: 13.8 us -> 3.55 us  [swapped(): return lax.ppermute(value, CORE, [(0, 1), (1, 0)])]
    ppermute x1 -> x3, starting transfers between devices: 3.67 us -> 13.4 us  [shifted(): lax.ppermute(value, SEQ, [(k, k + steps) for k in range(count - steps)])]
    ppermute x6 -> x9, waiting for transfers between devices: 0.02 us -> 8.16 us  [turned(): lax.ppermute(value, 'mp', [(k, (k + steps) % PARTS) for k in range(PARTS)])]
    ppermute x4 -> x3, waiting for transfers between devices: 4.22 us -> 0.77 us  [forked(): return lax.ppermute(value, SEQ, pairs)]
    ppermute x6 -> x9, starting transfers between devices: 7.32 us -> 9.86 us  [turned(): lax.ppermute(value, 'mp', [(k, (k + steps) % PARTS) for k in range(PARTS)])]
    ppermute x8 -> x10, waiting for transfers between devices: 4.77 us -> 3.47 us  [swapped(): return lax.ppermute(value, CORE, [(0, 1), (1, 0)])]
    pallas_call x3 -> x2, Pallas kernels: 2.25 us -> 1.1 us  [merged(): pl.pallas_call(merge_kernel, name='merged', out_shape=[jax.ShapeDtypeStru...]
  transfers between devices with their start and end apart: 19 -> 25, of which waited for: 6 -> 8; matrix products, arithmetic and copies ran while one was open for 0% -> 0% of each run, Pallas kernels for 27% -> 29%
where the time goes in v6:
time: 85.3 us; the launch traced here: 84.3 us
  starting transfers between devices  42.8 us (50%)
  Pallas kernels  25.2 us (30%)
  waiting for transfers between devices  12.4 us (15%)
  other arithmetic  1.62 us (2%)
  local copies, waits for them, and re-layouts  1.44 us (2%)
  between operations  0.87 us (1%)
    ppermute x3, starting transfers between devices, forked(): return lax.ppermute(value, SEQ, pairs)  16.1 us
    ppermute x3, starting transfers between devices, shifted(): lax.ppermute(value, SEQ, [(k, k + steps) for k in range(count - steps)])  13.4 us
    pallas_call x1, Pallas kernels, attend(): pl.pallas_call(attend_kernel, name='attend', grid=(count,), out_shape=jax...  11.2 us
    ppermute x9, starting transfers between devices, turned(): lax.ppermute(value, 'mp', [(k, (k + steps) % PARTS) for k in range(PARTS)])  9.86 us
    pallas_call x1, Pallas kernels, recur(): pl.pallas_call(recur_kernel, name='recur', grid=(count,), out_shape=[jax....  8.95 us
    ppermute x9, waiting for transfers between devices, turned(): lax.ppermute(value, 'mp', [(k, (k + steps) % PARTS) for k in range(PARTS)])  8.16 us
    ppermute x10, starting transfers between devices, swapped(): return lax.ppermute(value, CORE, [(0, 1), (1, 0)])  3.55 us
    ppermute x10, waiting for transfers between devices, swapped(): return lax.ppermute(value, CORE, [(0, 1), (1, 0)])  3.47 us
  transfers between devices with their start and end apart: 25, of which 8 were waited for; matrix products, arithmetic and copies ran while one was open for 0% of the time, Pallas kernels for 29%

profile of v6, /device:TPU:3, one launch (start us, length us, event | category | flops | bytes accessed | tf_op | source)
XLA Modules:
  0.0 84.3 jit_solution(7109087069374834380)
XLA Ops:
  0.6 0.7 slice.18
  1.4 3.7 %collective-permute-start = (bf16[3,1024]{1,0:T(4,128)(2,1)S(1)}, bf16[3,1024]{1,0:T(4,128)(2,1)S(1)}, u32[]{:S(2)}, u32[]{:S(2)}) collective-permute-start(bf16[3,1024]{1,0:T(4,128)(2,1)S(1)} %slice.18), channel_id=1, source_target_pairs={{0,4},{4,8},{8,12},{12,16},{16,20},{20,24},{24,28},{28,32},{32,36}... | collective-permute-start | bytes 18440 | tf_op jit(solution)/shard_map/ppermute | solution.py:44
  5.0 3.1 %project.1 = (f32[144,512]{1,0:T(8,128)}, bf16[144,512]{1,0:T(8,128)(2,1)}, bf16[144,512]{1,0:T(8,128)(2,1)}, bf16[144,512]{1,0:T(8,128)(2,1)}) custom-call(s32[1]{0:T(128)} %bitcast.place, bf16[512,1024]{1,0:T(8,128)(2,1)} %stream.1, f32[1,1024]{1,0:T(1,128)} %bitcast.10, bf16[1024,512]{1,0:T(8,128)(2,1)} %weight.1), custom_call_target="tpu_custom_call" | custom-call | flops 536870912 | bytes 3145728 | tf_op jit(solution)/shard_map/project/pallas_call | solution.py:80
  8.1 0.0 collective-permute-done.edge
  8.1 1.4 %collective-permute-start.1 = (bf16[144,512]{1,0:T(8,128)(2,1)}, bf16[144,512]{1,0:T(8,128)(2,1)S(1)}, u32[]{:S(2)}, u32[]{:S(2)}) collective-permute-start(bf16[144,512]{1,0:T(8,128)(2,1)} %get-tuple-element.50), channel_id=1, source_target_pairs={{0,1},{1,2},{2,3},{3,0},{4,5},{5,6},{6,7},{7,4},{8,9},{9,10},{10,1... | collective-permute-start | bytes 442376 | tf_op jit(solution)/shard_map/ppermute | solution.py:55
  9.5 2.6 %collective-permute-start.2 = (bf16[144,512]{1,0:T(8,128)(2,1)}, bf16[144,512]{1,0:T(8,128)(2,1)S(1)}, u32[]{:S(2)}, u32[]{:S(2)}) collective-permute-start(bf16[144,512]{1,0:T(8,128)(2,1)} %get-tuple-element.51), channel_id=1, source_target_pairs={{0,2},{1,3},{2,0},{3,1},{4,6},{5,7},{6,4},{7,5},{8,10},{9,11},{10,... | collective-permute-start | bytes 442376 | tf_op jit(solution)/shard_map/ppermute | solution.py:55
  12.1 1.1 %collective-permute-start.3 = (bf16[144,512]{1,0:T(8,128)(2,1)}, bf16[144,512]{1,0:T(8,128)(2,1)S(1)}, u32[]{:S(2)}, u32[]{:S(2)}) collective-permute-start(bf16[144,512]{1,0:T(8,128)(2,1)} %get-tuple-element.52), channel_id=1, source_target_pairs={{0,3},{1,0},{2,1},{3,2},{4,7},{5,4},{6,5},{7,6},{8,11},{9,8},{10,9... | collective-permute-start | bytes 442376 | tf_op jit(solution)/shard_map/ppermute | solution.py:55
  13.2 9.0 %recur.1 = (f32[512,1024]{1,0:T(8,128)}, f32[512,1024]{1,0:T(8,128)}, f32[2,1024]{1,0:T(2,128)}) custom-call(bf16[512,1024]{1,0:T(8,128)(2,1)} %branch.1, bf16[3,1024]{1,0:T(4,128)(2,1)} %copy-done.5, bf16[512,1024]{1,0:T(8,128)(2,1)} %gate.1, f32[4,1024]{1,0:T(4,128)} %taps.1, f32[1,1024]{1,0:T(1,128)} %bitcast.11, bf16[4,256,256]{2,1,0:T(8,128)(2,1)} %in_w.1, ...), custom_call_target="tpu_custom_call" | custom-call | flops 1073741824 | bytes 8388608 | tf_op jit(solution)/shard_map/recur/pallas_call | solution.py:282
  22.1 0.0 collective-permute-done.1.b
  22.1 0.0 collective-permute-done.2.c
  22.2 0.7 copy-done.1
  22.9 0.2 normed.1.refs_0_
  23.1 0.1 collective-permute-start.4
  23.2 1.4 %collective-permute-done.4.refs_8_ = bf16[144,512]{1,0:T(8,128)(2,1)S(1)} collective-permute-done((bf16[144,512]{1,0:T(8,128)(2,1)S(1)}, bf16[144,512]{1,0:T(8,128)(2,1)S(1)}, u32[]{:S(2)}, u32[]{:S(2)}) %collective-permute-start.4) | collective-permute-done | bytes 147488 | tf_op jit(solution)/shard_map/ppermute | solution.py:59
  24.5 4.1 %collective-permute-start.5 = (bf16[288,512]{1,0:T(8,128)(2,1)S(1)}, bf16[288,512]{1,0:T(8,128)(2,1)S(1)}, u32[]{:S(2)}, u32[]{:S(2)}) collective-permute-start(bf16[288,512]{1,0:T(8,128)(2,1)S(1)} %pad_maximum_fusion.pair), channel_id=1, source_target_pairs={{0,8},{8,16},{16,24},{24,32},{32,40},{40,48},{48,56},{56,64},{64,7... | collective-permute-start | bytes 884744 | tf_op jit(solution)/shard_map/ppermute | solution.py:51
  28.7 0.1 collective-permute-start.8
  28.8 2.2 %collective-permute-start.7 = (bf16[144,512]{1,0:T(8,128)(2,1)S(1)}, bf16[144,512]{1,0:T(8,128)(2,1)S(1)}, u32[]{:S(2)}, u32[]{:S(2)}) collective-permute-start(bf16[144,512]{1,0:T(8,128)(2,1)S(1)} %normed.1.refs_0_), channel_id=1, source_target_pairs={{0,2},{1,3},{2,0},{3,1},{4,6},{5,7},{6,4},{7,5},{8,10},{9,11},{10,... | collective-permute-start | bytes 442376 | tf_op jit(solution)/shard_map/ppermute | solution.py:55
  30.9 0.0 collective-permute-start.6
  30.9 0.1 pad_add_fusion.info
  31.0 3.5 %collective-permute-done.8.refs_3_ = bf16[144,512]{1,0:T(8,128)(2,1)S(1)} collective-permute-done((bf16[144,512]{1,0:T(8,128)(2,1)S(1)}, bf16[144,512]{1,0:T(8,128)(2,1)S(1)}, u32[]{:S(2)}, u32[]{:S(2)}) %collective-permute-start.8) | collective-permute-done | bytes 147488 | tf_op jit(solution)/shard_map/ppermute | solution.py:55
  34.5 1.4 %collective-permute-done.7.refs_2_ = bf16[144,512]{1,0:T(8,128)(2,1)S(1)} collective-permute-done((bf16[144,512]{1,0:T(8,128)(2,1)S(1)}, bf16[144,512]{1,0:T(8,128)(2,1)S(1)}, u32[]{:S(2)}, u32[]{:S(2)}) %collective-permute-start.7) | collective-permute-done | bytes 147488 | tf_op jit(solution)/shard_map/ppermute | solution.py:55
  35.9 3.2 %collective-permute-done.6.refs_1_ = bf16[144,512]{1,0:T(8,128)(2,1)S(1)} collective-permute-done((bf16[144,512]{1,0:T(8,128)(2,1)S(1)}, bf16[144,512]{1,0:T(8,128)(2,1)S(1)}, u32[]{:S(2)}, u32[]{:S(2)}) %collective-permute-start.6) | collective-permute-done | bytes 147488 | tf_op jit(solution)/shard_map/ppermute | solution.py:55
  39.2 0.0 collective-permute-done.5.arrived
  39.2 0.6 window.1
  39.8 0.4 collective-permute-start.14
  40.2 2.1 %collective-permute-start.13 = (bf16[256,512]{1,0:T(8,128)(2,1)S(1)}, bf16[256,512]{1,0:T(8,128)(2,1)S(1)}, u32[]{:S(2)}, u32[]{:S(2)}) collective-permute-start(bf16[256,512]{1,0:T(8,128)(2,1)S(1)} %get-tuple-element.71.refs_4_), channel_id=1, source_target_pairs={{0,2},{1,3},{2,0},{3,1},{4,6},{5,7},{6,4},{7,5},{8,10},{9,11},{10,... | collective-permute-start | bytes 786440 | tf_op jit(solution)/shard_map/ppermute | solution.py:55
  42.2 0.1 collective-permute-start.12
  42.3 1.3 %collective-permute-start.9 = (f32[2,1024]{1,0:T(2,128)S(1)}, f32[2,1024]{1,0:T(2,128)S(1)}, u32[]{:S(2)}, u32[]{:S(2)}) collective-permute-start(f32[2,1024]{1,0:T(2,128)S(1)} %get-tuple-element.57.mine), channel_id=1, source_target_pairs={{0,4},{4,0},{1,5},{5,1},{2,6},{6,2},{3,7},{7,3},{8,12},{12,8},{9,1... | collective-permute-start | bytes 24584 | tf_op jit(solution)/shard_map/ppermute | solution.py:59
  43.6 0.8 collective-permute-done.9.theirs
  44.5 0.6 merged.2
  45.0 5.8 %collective-permute-start.11 = (f32[2,1024]{1,0:T(2,128)S(1)}, f32[2,1024]{1,0:T(2,128)S(1)}, u32[]{:S(2)}, u32[]{:S(2)}) collective-permute-start(f32[2,1024]{1,0:T(2,128)S(1)} %get-tuple-element.59.inclusive), channel_id=1, source_target_pairs={{0,72},{8,80},{16,88},{24,96},{32,104},{40,112},{48,120},{56,128},... | collective-permute-start | bytes 24584 | tf_op jit(solution)/shard_map/ppermute | solution.py:51
  50.8 6.1 %collective-permute-start.10 = (f32[2,1024]{1,0:T(2,128)S(1)}, f32[2,1024]{1,0:T(2,128)S(1)}, u32[]{:S(2)}, u32[]{:S(2)}) collective-permute-start(f32[2,1024]{1,0:T(2,128)S(1)} %get-tuple-element.59.inclusive), channel_id=1, source_target_pairs={{0,24},{8,32},{16,40},{24,48},{32,56},{40,64},{48,72},{56,80},{64,... | collective-permute-start | bytes 24584 | tf_op jit(solution)/shard_map/ppermute | solution.py:51
  57.0 0.8 collective-permute-done.10
  57.8 0.1 collective-permute-start.18
  57.9 0.5 collective-permute-start.19
  58.4 0.2 collective-permute-start.15
  58.6 0.4 collective-permute-start.21
  59.0 0.3 collective-permute-start.22
  59.3 0.4 collective-permute-done.15.theirs
  59.7 0.2 collective-permute-start.23
  59.8 0.3 collective-permute-start.24
  60.2 0.2 collective-permute-start.20
  60.3 0.6 merged.3
  60.9 0.9 %collective-permute-done.20.refs_11_ = bf16[144,512]{1,0:T(8,128)(2,1)S(1)} collective-permute-done((bf16[144,512]{1,0:T(8,128)(2,1)S(1)}, bf16[144,512]{1,0:T(8,128)(2,1)S(1)}, u32[]{:S(2)}, u32[]{:S(2)}) %collective-permute-start.20) | collective-permute-done | bytes 147488 | tf_op jit(solution)/shard_map/ppermute | solution.py:59
  61.8 3.6 %collective-permute-start.17 = (f32[2,1024]{1,0:T(2,128)S(1)}, f32[2,1024]{1,0:T(2,128)S(1)}, u32[]{:S(2)}, u32[]{:S(2)}) collective-permute-start(f32[2,1024]{1,0:T(2,128)S(1)} %get-tuple-element.67), channel_id=1, source_target_pairs={{0,240},{4,244},{8,248},{12,252},{1,241},{5,245},{9,249},{13,253},... | collective-permute-start | bytes 24584 | tf_op jit(solution)/shard_map/ppermute | solution.py:44
  65.4 6.1 %collective-permute-start.16 = (f32[2,1024]{1,0:T(2,128)S(1)}, f32[2,1024]{1,0:T(2,128)S(1)}, u32[]{:S(2)}, u32[]{:S(2)}) collective-permute-start(f32[2,1024]{1,0:T(2,128)S(1)} %get-tuple-element.67), channel_id=1, source_target_pairs={{0,120},{4,124},{8,128},{12,132},{16,136},{20,140},{24,144},{28,14... | collective-permute-start | bytes 24584 | tf_op jit(solution)/shard_map/ppermute | solution.py:44
  71.6 11.2 %attend.1 = bf16[512,1024]{1,0:T(8,128)(2,1)} custom-call(s32[3]{0:T(128)S(1)} %pad_add_fusion.info, bf16[512,1024]{1,0:T(8,128)(2,1)S(1)} %copy-done.2, bf16[144,512]{1,0:T(8,128)(2,1)S(1)} %normed.1.refs_0_, bf16[144,512]{1,0:T(8,128)(2,1)S(1)} %collective-permute-done.6.refs_1_, bf16[144,512]{1,0:T(8,128)(2,1)S(1)} %collective-permute-done.7.refs_2_, ...), custom_call_target="tpu_custom_call" | custom-call | flops 4294967296 | bytes 4194304 | tf_op jit(solution)/shard_map/attend/pallas_call | solution.py:388
  82.8 1.5 %add_convert_fusion = bf16[512,1024]{1,0:T(8,128)(2,1)} fusion(f32[512,1024]{1,0:T(8,128)S(1)} %copy-done.3, f32[512,1024]{1,0:T(8,128)S(1)} %copy-done.4, f32[1024]{0:T(1024)S(1)} %bitcast.9), kind=kLoop, calls=%fused_computation | loop fusion | flops 1572864 | bytes 5246976 | tf_op jit(solution)/shard_map/convert_element_type | solution.py:459
  (27 shorter events, 0.1 us)
Async XLA Ops:
  1.4 6.7 %collective-permute-start = (bf16[3,1024]{1,0:T(4,128)(2,1)S(1)}, bf16[3,1024]{1,0:T(4,128)(2,1)S(1)}, u32[]{:S(2)}, u32[]{:S(2)}) collective-permute-start(bf16[3,1024]{1,0:T(4,128)(2,1)S(1)} %slice.18), channel_id=1, source_target_pairs={{0,4},{4,8},{8,12},{12,16},{16,20},{20,24},{24,28},{28,32},{32,36}... | collective-permute-start | bytes 18440 | tf_op jit(solution)/shard_map/ppermute | solution.py:44
  8.1 5.1 %copy-start.5 = (bf16[3,1024]{1,0:T(4,128)(2,1)}, bf16[3,1024]{1,0:T(4,128)(2,1)S(1)}, u32[]{:S(2)}) copy-start(bf16[3,1024]{1,0:T(4,128)(2,1)S(1)} %collective-permute-done.edge) | copy-start | bytes 18436
  8.1 14.0 %collective-permute-start.1 = (bf16[144,512]{1,0:T(8,128)(2,1)}, bf16[144,512]{1,0:T(8,128)(2,1)S(1)}, u32[]{:S(2)}, u32[]{:S(2)}) collective-permute-start(bf16[144,512]{1,0:T(8,128)(2,1)} %get-tuple-element.50), channel_id=1, source_target_pairs={{0,1},{1,2},{2,3},{3,0},{4,5},{5,6},{6,7},{7,4},{8,9},{9,10},{10,1... | collective-permute-start | bytes 442376 | tf_op jit(solution)/shard_map/ppermute | solution.py:55
  9.5 12.7 %collective-permute-start.2 = (bf16[144,512]{1,0:T(8,128)(2,1)}, bf16[144,512]{1,0:T(8,128)(2,1)S(1)}, u32[]{:S(2)}, u32[]{:S(2)}) collective-permute-start(bf16[144,512]{1,0:T(8,128)(2,1)} %get-tuple-element.51), channel_id=1, source_target_pairs={{0,2},{1,3},{2,0},{3,1},{4,6},{5,7},{6,4},{7,5},{8,10},{9,11},{10,... | collective-permute-start | bytes 442376 | tf_op jit(solution)/shard_map/ppermute | solution.py:55
  12.1 10.1 %collective-permute-start.3 = (bf16[144,512]{1,0:T(8,128)(2,1)}, bf16[144,512]{1,0:T(8,128)(2,1)S(1)}, u32[]{:S(2)}, u32[]{:S(2)}) collective-permute-start(bf16[144,512]{1,0:T(8,128)(2,1)} %get-tuple-element.52), channel_id=1, source_target_pairs={{0,3},{1,0},{2,1},{3,2},{4,7},{5,4},{6,5},{7,6},{8,11},{9,8},{10,9... | collective-permute-start | bytes 442376 | tf_op jit(solution)/shard_map/ppermute | solution.py:55
  13.2 9.0 %copy-start = (f32[144,512]{1,0:T(8,128)S(1)}, f32[144,512]{1,0:T(8,128)}, u32[]{:S(2)}) copy-start(f32[144,512]{1,0:T(8,128)} %get-tuple-element.49.a) | copy-start | bytes 884740
  13.2 58.4 %copy-start.2 = (bf16[512,1024]{1,0:T(8,128)(2,1)S(1)}, bf16[512,1024]{1,0:T(8,128)(2,1)}, u32[]{:S(2)}) copy-start(bf16[512,1024]{1,0:T(8,128)(2,1)} %q_ref.1) | copy-start | bytes 3145732
  22.2 0.7 copy-start.1
  23.1 1.5 %collective-permute-start.4 = (bf16[144,512]{1,0:T(8,128)(2,1)S(1)}, bf16[144,512]{1,0:T(8,128)(2,1)S(1)}, u32[]{:S(2)}, u32[]{:S(2)}) collective-permute-start(bf16[144,512]{1,0:T(8,128)(2,1)S(1)} %normed.1.refs_0_), channel_id=1, source_target_pairs={{0,4},{4,0},{1,5},{5,1},{2,6},{6,2},{3,7},{7,3},{8,12},{12,8},{9,1... | collective-permute-start | bytes 442376 | tf_op jit(solution)/shard_map/ppermute | solution.py:59
  24.5 14.6 %collective-permute-start.5 = (bf16[288,512]{1,0:T(8,128)(2,1)S(1)}, bf16[288,512]{1,0:T(8,128)(2,1)S(1)}, u32[]{:S(2)}, u32[]{:S(2)}) collective-permute-start(bf16[288,512]{1,0:T(8,128)(2,1)S(1)} %pad_maximum_fusion.pair), channel_id=1, source_target_pairs={{0,8},{8,16},{16,24},{24,32},{32,40},{40,48},{48,56},{56,64},{64,7... | collective-permute-start | bytes 884744 | tf_op jit(solution)/shard_map/ppermute | solution.py:51
  28.7 5.9 %collective-permute-start.8 = (bf16[144,512]{1,0:T(8,128)(2,1)S(1)}, bf16[144,512]{1,0:T(8,128)(2,1)S(1)}, u32[]{:S(2)}, u32[]{:S(2)}) collective-permute-start(bf16[144,512]{1,0:T(8,128)(2,1)S(1)} %normed.1.refs_0_), channel_id=1, source_target_pairs={{0,3},{1,0},{2,1},{3,2},{4,7},{5,4},{6,5},{7,6},{8,11},{9,8},{10,9... | collective-permute-start | bytes 442376 | tf_op jit(solution)/shard_map/ppermute | solution.py:55
  28.8 7.2 %collective-permute-start.7 = (bf16[144,512]{1,0:T(8,128)(2,1)S(1)}, bf16[144,512]{1,0:T(8,128)(2,1)S(1)}, u32[]{:S(2)}, u32[]{:S(2)}) collective-permute-start(bf16[144,512]{1,0:T(8,128)(2,1)S(1)} %normed.1.refs_0_), channel_id=1, source_target_pairs={{0,2},{1,3},{2,0},{3,1},{4,6},{5,7},{6,4},{7,5},{8,10},{9,11},{10,... | collective-permute-start | bytes 442376 | tf_op jit(solution)/shard_map/ppermute | solution.py:55
  30.9 8.2 %collective-permute-start.6 = (bf16[144,512]{1,0:T(8,128)(2,1)S(1)}, bf16[144,512]{1,0:T(8,128)(2,1)S(1)}, u32[]{:S(2)}, u32[]{:S(2)}) collective-permute-start(bf16[144,512]{1,0:T(8,128)(2,1)S(1)} %normed.1.refs_0_), channel_id=1, source_target_pairs={{0,1},{1,2},{2,3},{3,0},{4,5},{5,6},{6,7},{7,4},{8,9},{9,10},{10,1... | collective-permute-start | bytes 442376 | tf_op jit(solution)/shard_map/ppermute | solution.py:55
  39.8 18.0 %collective-permute-start.14 = (bf16[256,512]{1,0:T(8,128)(2,1)S(1)}, bf16[256,512]{1,0:T(8,128)(2,1)S(1)}, u32[]{:S(2)}, u32[]{:S(2)}) collective-permute-start(bf16[256,512]{1,0:T(8,128)(2,1)S(1)} %get-tuple-element.71.refs_4_), channel_id=1, source_target_pairs={{0,3},{1,0},{2,1},{3,2},{4,7},{5,4},{6,5},{7,6},{8,11},{9,8},{10,9... | collective-permute-start | bytes 786440 | tf_op jit(solution)/shard_map/ppermute | solution.py:55
  40.2 17.6 %collective-permute-start.13 = (bf16[256,512]{1,0:T(8,128)(2,1)S(1)}, bf16[256,512]{1,0:T(8,128)(2,1)S(1)}, u32[]{:S(2)}, u32[]{:S(2)}) collective-permute-start(bf16[256,512]{1,0:T(8,128)(2,1)S(1)} %get-tuple-element.71.refs_4_), channel_id=1, source_target_pairs={{0,2},{1,3},{2,0},{3,1},{4,6},{5,7},{6,4},{7,5},{8,10},{9,11},{10,... | collective-permute-start | bytes 786440 | tf_op jit(solution)/shard_map/ppermute | solution.py:55
  42.2 15.5 %collective-permute-start.12 = (bf16[256,512]{1,0:T(8,128)(2,1)S(1)}, bf16[256,512]{1,0:T(8,128)(2,1)S(1)}, u32[]{:S(2)}, u32[]{:S(2)}) collective-permute-start(bf16[256,512]{1,0:T(8,128)(2,1)S(1)} %get-tuple-element.71.refs_4_), channel_id=1, source_target_pairs={{0,1},{1,2},{2,3},{3,0},{4,5},{5,6},{6,7},{7,4},{8,9},{9,10},{10,1... | collective-permute-start | bytes 786440 | tf_op jit(solution)/shard_map/ppermute | solution.py:55
  42.3 2.1 %collective-permute-start.9 = (f32[2,1024]{1,0:T(2,128)S(1)}, f32[2,1024]{1,0:T(2,128)S(1)}, u32[]{:S(2)}, u32[]{:S(2)}) collective-permute-start(f32[2,1024]{1,0:T(2,128)S(1)} %get-tuple-element.57.mine), channel_id=1, source_target_pairs={{0,4},{4,0},{1,5},{5,1},{2,6},{6,2},{3,7},{7,3},{8,12},{12,8},{9,1... | collective-permute-start | bytes 24584 | tf_op jit(solution)/shard_map/ppermute | solution.py:59
  45.0 12.0 %collective-permute-start.11 = (f32[2,1024]{1,0:T(2,128)S(1)}, f32[2,1024]{1,0:T(2,128)S(1)}, u32[]{:S(2)}, u32[]{:S(2)}) collective-permute-start(f32[2,1024]{1,0:T(2,128)S(1)} %get-tuple-element.59.inclusive), channel_id=1, source_target_pairs={{0,72},{8,80},{16,88},{24,96},{32,104},{40,112},{48,120},{56,128},... | collective-permute-start | bytes 24584 | tf_op jit(solution)/shard_map/ppermute | solution.py:51
  50.8 6.9 %collective-permute-start.10 = (f32[2,1024]{1,0:T(2,128)S(1)}, f32[2,1024]{1,0:T(2,128)S(1)}, u32[]{:S(2)}, u32[]{:S(2)}) collective-permute-start(f32[2,1024]{1,0:T(2,128)S(1)} %get-tuple-element.59.inclusive), channel_id=1, source_target_pairs={{0,24},{8,32},{16,40},{24,48},{32,56},{40,64},{48,72},{56,80},{64,... | collective-permute-start | bytes 24584 | tf_op jit(solution)/shard_map/ppermute | solution.py:51
  57.8 2.1 %collective-permute-start.18 = (bf16[144,512]{1,0:T(8,128)(2,1)S(1)}, bf16[144,512]{1,0:T(8,128)(2,1)S(1)}, u32[]{:S(2)}, u32[]{:S(2)}) collective-permute-start(bf16[144,512]{1,0:T(8,128)(2,1)S(1)} %collective-permute-done.6.refs_1_), channel_id=1, source_target_pairs={{0,4},{4,0},{1,5},{5,1},{2,6},{6,2},{3,7},{7,3},{8,12},{12,8},{9,1... | collective-permute-start | bytes 442376 | tf_op jit(solution)/shard_map/ppermute | solution.py:59
  57.9 2.3 %collective-permute-start.19 = (bf16[144,512]{1,0:T(8,128)(2,1)S(1)}, bf16[144,512]{1,0:T(8,128)(2,1)S(1)}, u32[]{:S(2)}, u32[]{:S(2)}) collective-permute-start(bf16[144,512]{1,0:T(8,128)(2,1)S(1)} %collective-permute-done.7.refs_2_), channel_id=1, source_target_pairs={{0,4},{4,0},{1,5},{5,1},{2,6},{6,2},{3,7},{7,3},{8,12},{12,8},{9,1... | collective-permute-start | bytes 442376 | tf_op jit(solution)/shard_map/ppermute | solution.py:59
  58.4 1.3 %collective-permute-start.15 = (f32[4,1024]{1,0:T(4,128)S(1)}, f32[4,1024]{1,0:T(4,128)S(1)}, u32[]{:S(2)}, u32[]{:S(2)}) collective-permute-start(f32[4,1024]{1,0:T(4,128)S(1)} %pad_maximum_fusion.1.mine), channel_id=1, source_target_pairs={{0,4},{4,0},{1,5},{5,1},{2,6},{6,2},{3,7},{7,3},{8,12},{12,8},{9,1... | collective-permute-start | bytes 49160 | tf_op jit(solution)/shard_map/ppermute | solution.py:59
  58.6 6.8 %collective-permute-start.21 = (bf16[256,512]{1,0:T(8,128)(2,1)S(1)}, bf16[256,512]{1,0:T(8,128)(2,1)S(1)}, u32[]{:S(2)}, u32[]{:S(2)}) collective-permute-start(bf16[256,512]{1,0:T(8,128)(2,1)S(1)} %get-tuple-element.71.refs_4_), channel_id=1, source_target_pairs={{0,4},{4,0},{1,5},{5,1},{2,6},{6,2},{3,7},{7,3},{8,12},{12,8},{9,1... | collective-permute-start | bytes 786440 | tf_op jit(solution)/shard_map/ppermute | solution.py:59
  59.0 12.5 %collective-permute-start.22 = (bf16[256,512]{1,0:T(8,128)(2,1)S(1)}, bf16[256,512]{1,0:T(8,128)(2,1)S(1)}, u32[]{:S(2)}, u32[]{:S(2)}) collective-permute-start(bf16[256,512]{1,0:T(8,128)(2,1)S(1)} %collective-permute-done.12.refs_5_), channel_id=1, source_target_pairs={{0,4},{4,0},{1,5},{5,1},{2,6},{6,2},{3,7},{7,3},{8,12},{12,8},{9,1... | collective-permute-start | bytes 786440 | tf_op jit(solution)/shard_map/ppermute | solution.py:59
  59.7 11.9 %collective-permute-start.23 = (bf16[256,512]{1,0:T(8,128)(2,1)S(1)}, bf16[256,512]{1,0:T(8,128)(2,1)S(1)}, u32[]{:S(2)}, u32[]{:S(2)}) collective-permute-start(bf16[256,512]{1,0:T(8,128)(2,1)S(1)} %collective-permute-done.13.refs_6_), channel_id=1, source_target_pairs={{0,4},{4,0},{1,5},{5,1},{2,6},{6,2},{3,7},{7,3},{8,12},{12,8},{9,1... | collective-permute-start | bytes 786440 | tf_op jit(solution)/shard_map/ppermute | solution.py:59
  59.8 11.7 %collective-permute-start.24 = (bf16[256,512]{1,0:T(8,128)(2,1)S(1)}, bf16[256,512]{1,0:T(8,128)(2,1)S(1)}, u32[]{:S(2)}, u32[]{:S(2)}) collective-permute-start(bf16[256,512]{1,0:T(8,128)(2,1)S(1)} %collective-permute-done.14.refs_7_), channel_id=1, source_target_pairs={{0,4},{4,0},{1,5},{5,1},{2,6},{6,2},{3,7},{7,3},{8,12},{12,8},{9,1... | collective-permute-start | bytes 786440 | tf_op jit(solution)/shard_map/ppermute | solution.py:59
  60.2 1.6 %collective-permute-start.20 = (bf16[144,512]{1,0:T(8,128)(2,1)S(1)}, bf16[144,512]{1,0:T(8,128)(2,1)S(1)}, u32[]{:S(2)}, u32[]{:S(2)}) collective-permute-start(bf16[144,512]{1,0:T(8,128)(2,1)S(1)} %collective-permute-done.8.refs_3_), channel_id=1, source_target_pairs={{0,4},{4,0},{1,5},{5,1},{2,6},{6,2},{3,7},{7,3},{8,12},{12,8},{9,1... | collective-permute-start | bytes 442376 | tf_op jit(solution)/shard_map/ppermute | solution.py:59
  61.8 21.0 %copy-start.3 = (f32[512,1024]{1,0:T(8,128)S(1)}, f32[512,1024]{1,0:T(8,128)}, u32[]{:S(2)}) copy-start(f32[512,1024]{1,0:T(8,128)} %get-tuple-element.45) | copy-start | bytes 6291460
  61.8 21.0 %copy-start.4 = (f32[512,1024]{1,0:T(8,128)S(1)}, f32[512,1024]{1,0:T(8,128)}, u32[]{:S(2)}) copy-start(f32[512,1024]{1,0:T(8,128)} %get-tuple-element.46) | copy-start | bytes 6291460
  61.8 21.0 %collective-permute-start.17 = (f32[2,1024]{1,0:T(2,128)S(1)}, f32[2,1024]{1,0:T(2,128)S(1)}, u32[]{:S(2)}, u32[]{:S(2)}) collective-permute-start(f32[2,1024]{1,0:T(2,128)S(1)} %get-tuple-element.67), channel_id=1, source_target_pairs={{0,240},{4,244},{8,248},{12,252},{1,241},{5,245},{9,249},{13,253},... | collective-permute-start | bytes 24584 | tf_op jit(solution)/shard_map/ppermute | solution.py:44
  65.4 17.4 %collective-permute-start.16 = (f32[2,1024]{1,0:T(2,128)S(1)}, f32[2,1024]{1,0:T(2,128)S(1)}, u32[]{:S(2)}, u32[]{:S(2)}) collective-permute-start(f32[2,1024]{1,0:T(2,128)S(1)} %get-tuple-element.67), channel_id=1, source_target_pairs={{0,120},{4,124},{8,128},{12,132},{16,136},{20,140},{24,144},{28,14... | collective-permute-start | bytes 24584 | tf_op jit(solution)/shard_map/ppermute | solution.py:44

commit v7 on v6

--- a/solution.py
+++ b/solution.py
@@ -306,7 +306,7 @@
     )(*inputs, *filled)
 
 
-def attend_head(q_ref, kv, out, admitted):
+def attend_head(q_ref, kv, out, earlier):
     def scored(q, begin, size):
         return lax.dot_general(
             q,
@@ -321,18 +321,20 @@
     last = (SHARDS - 1) * TOK
     q = q_ref[...] * jnp.asarray(HD**-0.5, BF16)
     most = SHARDS - 1
-    wide = [admitted(scored(q, k * TOK, TOK), most - k) for k in range(1, most)]
+    whole_shards = range(max(1, most - earlier), most)
+    wide = [scored(q, k * TOK, TOK) for k in whole_shards]
     for half in range(2):
         low = half * QROWS
         rows = slice(low, low + QROWS)
-        far = admitted(scored(q[rows], low, QROWS), most)
         near = scored(q[rows], last + low, QROWS)
-        blocks = [(k * TOK, s[rows]) for k, s in zip(range(1, SHARDS - 1), wide)]
-        blocks.append((low, jnp.where(causal, masked_score, far)))
+        blocks = [(k * TOK, s[rows]) for k, s in zip(whole_shards, wide)]
+        if earlier == most:
+            far = scored(q[rows], low, QROWS)
+            blocks.append((low, jnp.where(causal, masked_score, far)))
         blocks.append((last + low, jnp.where(causal, near, masked_score)))
-        if half == 0:
-            blocks.append((QROWS, admitted(scored(q[rows], QROWS, QROWS), most)))
-        else:
+        if half == 0 and earlier == most:
+            blocks.append((QROWS, scored(q[rows], QROWS, QROWS)))
+        if half == 1:
             blocks.append((last, scored(q[rows], last, QROWS)))
         tiles = [s[:, k : k + 128] for _, s in blocks for k in range(0, s.shape[1], 128)]
         peak = jnp.max(functools.reduce(jnp.maximum, tiles), axis=1, keepdims=True)
@@ -370,15 +372,11 @@
                         slot * QUARTER : (slot + 1) * QUARTER, :
                     ]
 
-    @pl.when(position >= SHARDS - 1)
-    def _():
-        attend_head(q_ref, kv, out, lambda s, behind: s)
-
-    @pl.when(position < SHARDS - 1)
-    def _():
-        attend_head(
-            q_ref, kv, out, lambda s, behind: jnp.where(position >= behind, s, masked_score)
-        )
+    for earlier in range(SHARDS):
+
+        @pl.when(jnp.minimum(position, SHARDS - 1) == earlier)
+        def _():
+            attend_head(q_ref, kv, out, earlier)
 
 
 def attend(head, count, info, queries, pieces, filled):
@@ -442,20 +440,20 @@
     duo, before, inclusive, got = window(info, pair, arrived, branch_in.shape[1])
     two = [turned(duo, k) for k in range(1, PARTS)]
     before, inclusive = merged(info, before, inclusive, got, swapped(got))
-    far = [forked(inclusive, 3, 6), forked(inclusive, 9, 12)]
+    far = forked(inclusive, 3, 6)
     far, two, own, duo = lax.optimization_barrier((far, two, own, duo))
     other = [swapped(piece) for piece in own]
-    far = jnp.concatenate(far)
     before, inclusive = merged(info, before, inclusive, far, swapped(far))
     two = [duo] + two
     others = [swapped(piece) for piece in two]
-    far = [shifted(inclusive, 30), shifted(inclusive, 60)]
+    far = [shifted(inclusive, 18 * k) for k in (1, 2, 3)]
     heads = queries.shape[1] // HD
     pieces = (mine, *own, *two, beside, *other, *others)
     attended = attend(0, heads, info, queries, pieces, ())
     *far, attended = lax.optimization_barrier((*far, attended))
-    state = far[0][0:1] * far[1][1:2] + far[0][1:2]
-    state = before[0:1] * state + before[1:2]
+    factor, state = (before[0:1], before[1:2])
+    for couple in far:
+        factor, state = (couple[0:1] * factor, factor * couple[1:2] + state)
     recurrent_out = (u + w * state).astype(BF16)
     return (recurrent_out, attended)
 

time: 85.3 us -> 86.9 us (1.019)
  waiting for transfers between devices: 12.4 us -> 14.6 us
  starting transfers between devices: 42.8 us -> 44.9 us
  Pallas kernels: 25.2 us -> 23.1 us
    ppermute x3 -> x2, starting transfers between devices: 16.1 us -> 9.73 us  [forked(): return lax.ppermute(value, SEQ, pairs)]
    ppermute x3 -> x4, starting transfers between devices: 13.4 us -> 19.5 us  [shifted(): lax.ppermute(value, SEQ, [(k, k + steps) for k in range(count - steps)])]
    ppermute x9, waiting for transfers between devices: 8.16 us -> 10.5 us  [turned(): lax.ppermute(value, 'mp', [(k, (k + steps) % PARTS) for k in range(PARTS)])]
    pallas_call x1, Pallas kernels: 11.2 us -> 9.18 us  [attend(): pl.pallas_call(attend_kernel, name='attend', grid=(count,), out_shape=jax...]
    ppermute x9, starting transfers between devices: 9.86 us -> 11.6 us  [turned(): lax.ppermute(value, 'mp', [(k, (k + steps) % PARTS) for k in range(PARTS)])]
  transfers between devices with their start and end apart: 25 -> 25, of which waited for: 8 -> 8; matrix products, arithmetic and copies ran while one was open for 0% -> 0% of each run, Pallas kernels for 29% -> 26%
where the time goes in v7:
time: 86.9 us; the launch traced here: 86.5 us
  starting transfers between devices  44.9 us (52%)
  Pallas kernels  23.1 us (27%)
  waiting for transfers between devices  14.6 us (17%)
  other arithmetic  1.61 us (2%)
  local copies, waits for them, and re-layouts  1.44 us (2%)
    ppermute x4, starting transfers between devices, shifted(): lax.ppermute(value, SEQ, [(k, k + steps) for k in range(count - steps)])  19.5 us
    ppermute x9, starting transfers between devices, turned(): lax.ppermute(value, 'mp', [(k, (k + steps) % PARTS) for k in range(PARTS)])  11.6 us
    ppermute x9, waiting for transfers between devices, turned(): lax.ppermute(value, 'mp', [(k, (k + steps) % PARTS) for k in range(PARTS)])  10.5 us
    ppermute x2, starting transfers between devices, forked(): return lax.ppermute(value, SEQ, pairs)  9.73 us
    pallas_call x1, Pallas kernels, attend(): pl.pallas_call(attend_kernel, name='attend', grid=(count,), out_shape=jax...  9.18 us
    pallas_call x1, Pallas kernels, recur(): pl.pallas_call(recur_kernel, name='recur', grid=(count,), out_shape=[jax....  8.95 us
    ppermute x10, starting transfers between devices, swapped(): return lax.ppermute(value, CORE, [(0, 1), (1, 0)])  4.11 us
    ppermute x10, waiting for transfers between devices, swapped(): return lax.ppermute(value, CORE, [(0, 1), (1, 0)])  3.31 us
  transfers between devices with their start and end apart: 25, of which 8 were waited for; matrix products, arithmetic and copies ran while one was open for 0% of the time, Pallas kernels for 26%

profile of v7, /device:TPU:3, one launch (start us, length us, event | category | flops | bytes accessed | tf_op | source)
XLA Modules:
  0.0 86.5 jit_solution(4263760339899683813)
XLA Ops:
  0.6 0.7 slice.24
  1.4 3.7 %collective-permute-start = (bf16[3,1024]{1,0:T(4,128)(2,1)S(1)}, bf16[3,1024]{1,0:T(4,128)(2,1)S(1)}, u32[]{:S(2)}, u32[]{:S(2)}) collective-permute-start(bf16[3,1024]{1,0:T(4,128)(2,1)S(1)} %slice.24), channel_id=1, source_target_pairs={{0,4},{4,8},{8,12},{12,16},{16,20},{20,24},{24,28},{28,32},{32,36}... | collective-permute-start | bytes 18440 | tf_op jit(solution)/shard_map/ppermute | solution.py:44
  5.0 3.1 %project.1 = (f32[144,512]{1,0:T(8,128)}, bf16[144,512]{1,0:T(8,128)(2,1)}, bf16[144,512]{1,0:T(8,128)(2,1)}, bf16[144,512]{1,0:T(8,128)(2,1)}) custom-call(s32[1]{0:T(128)} %bitcast.place, bf16[512,1024]{1,0:T(8,128)(2,1)} %stream.1, f32[1,1024]{1,0:T(1,128)} %bitcast.10, bf16[1024,512]{1,0:T(8,128)(2,1)} %weight.1), custom_call_target="tpu_custom_call" | custom-call | flops 536870912 | bytes 3145728 | tf_op jit(solution)/shard_map/project/pallas_call | solution.py:80
  8.1 1.4 %collective-permute-start.1 = (bf16[144,512]{1,0:T(8,128)(2,1)}, bf16[144,512]{1,0:T(8,128)(2,1)S(1)}, u32[]{:S(2)}, u32[]{:S(2)}) collective-permute-start(bf16[144,512]{1,0:T(8,128)(2,1)} %get-tuple-element.50), channel_id=1, source_target_pairs={{0,1},{1,2},{2,3},{3,0},{4,5},{5,6},{6,7},{7,4},{8,9},{9,10},{10,1... | collective-permute-start | bytes 442376 | tf_op jit(solution)/shard_map/ppermute | solution.py:55
  9.5 2.6 %collective-permute-start.2 = (bf16[144,512]{1,0:T(8,128)(2,1)}, bf16[144,512]{1,0:T(8,128)(2,1)S(1)}, u32[]{:S(2)}, u32[]{:S(2)}) collective-permute-start(bf16[144,512]{1,0:T(8,128)(2,1)} %get-tuple-element.51), channel_id=1, source_target_pairs={{0,2},{1,3},{2,0},{3,1},{4,6},{5,7},{6,4},{7,5},{8,10},{9,11},{10,... | collective-permute-start | bytes 442376 | tf_op jit(solution)/shard_map/ppermute | solution.py:55
  12.1 1.1 %collective-permute-start.3 = (bf16[144,512]{1,0:T(8,128)(2,1)}, bf16[144,512]{1,0:T(8,128)(2,1)S(1)}, u32[]{:S(2)}, u32[]{:S(2)}) collective-permute-start(bf16[144,512]{1,0:T(8,128)(2,1)} %get-tuple-element.52), channel_id=1, source_target_pairs={{0,3},{1,0},{2,1},{3,2},{4,7},{5,4},{6,5},{7,6},{8,11},{9,8},{10,9... | collective-permute-start | bytes 442376 | tf_op jit(solution)/shard_map/ppermute | solution.py:55
  13.2 9.0 %recur.1 = (f32[512,1024]{1,0:T(8,128)}, f32[512,1024]{1,0:T(8,128)}, f32[2,1024]{1,0:T(2,128)}) custom-call(bf16[512,1024]{1,0:T(8,128)(2,1)} %branch.1, bf16[3,1024]{1,0:T(4,128)(2,1)} %copy-done.5, bf16[512,1024]{1,0:T(8,128)(2,1)} %gate.1, f32[4,1024]{1,0:T(4,128)} %taps.1, f32[1,1024]{1,0:T(1,128)} %bitcast.11, bf16[4,256,256]{2,1,0:T(8,128)(2,1)} %in_w.1, ...), custom_call_target="tpu_custom_call" | custom-call | flops 1073741824 | bytes 8388608 | tf_op jit(solution)/shard_map/recur/pallas_call | solution.py:282
  22.1 0.0 collective-permute-done.2.c
  22.1 0.0 collective-permute-done.3.d
  22.2 0.7 copy-done.1
  22.9 0.2 normed.1.refs_0_
  23.1 0.1 collective-permute-start.4
  23.2 1.4 %collective-permute-done.4.refs_8_ = bf16[144,512]{1,0:T(8,128)(2,1)S(1)} collective-permute-done((bf16[144,512]{1,0:T(8,128)(2,1)S(1)}, bf16[144,512]{1,0:T(8,128)(2,1)S(1)}, u32[]{:S(2)}, u32[]{:S(2)}) %collective-permute-start.4) | collective-permute-done | bytes 147488 | tf_op jit(solution)/shard_map/ppermute | solution.py:59
  24.5 4.1 %collective-permute-start.5 = (bf16[288,512]{1,0:T(8,128)(2,1)S(1)}, bf16[288,512]{1,0:T(8,128)(2,1)S(1)}, u32[]{:S(2)}, u32[]{:S(2)}) collective-permute-start(bf16[288,512]{1,0:T(8,128)(2,1)S(1)} %pad_maximum_fusion.pair), channel_id=1, source_target_pairs={{0,8},{8,16},{16,24},{24,32},{32,40},{40,48},{48,56},{56,64},{64,7... | collective-permute-start | bytes 884744 | tf_op jit(solution)/shard_map/ppermute | solution.py:51
  28.7 0.5 collective-permute-start.6
  29.1 0.8 collective-permute-start.7
  29.9 1.7 %collective-permute-start.8 = (bf16[144,512]{1,0:T(8,128)(2,1)S(1)}, bf16[144,512]{1,0:T(8,128)(2,1)S(1)}, u32[]{:S(2)}, u32[]{:S(2)}) collective-permute-start(bf16[144,512]{1,0:T(8,128)(2,1)S(1)} %normed.1.refs_0_), channel_id=1, source_target_pairs={{0,3},{1,0},{2,1},{3,2},{4,7},{5,4},{6,5},{7,6},{8,11},{9,8},{10,9... | collective-permute-start | bytes 442376 | tf_op jit(solution)/shard_map/ppermute | solution.py:55
  31.6 0.1 pad_add_fusion.info
  31.7 6.6 %collective-permute-done.6.refs_1_ = bf16[144,512]{1,0:T(8,128)(2,1)S(1)} collective-permute-done((bf16[144,512]{1,0:T(8,128)(2,1)S(1)}, bf16[144,512]{1,0:T(8,128)(2,1)S(1)}, u32[]{:S(2)}, u32[]{:S(2)}) %collective-permute-start.6) | collective-permute-done | bytes 147488 | tf_op jit(solution)/shard_map/ppermute | solution.py:55
  38.3 0.0 collective-permute-done.7.refs_2_
  38.3 1.1 %collective-permute-done.8.refs_3_ = bf16[144,512]{1,0:T(8,128)(2,1)S(1)} collective-permute-done((bf16[144,512]{1,0:T(8,128)(2,1)S(1)}, bf16[144,512]{1,0:T(8,128)(2,1)S(1)}, u32[]{:S(2)}, u32[]{:S(2)}) %collective-permute-start.8) | collective-permute-done | bytes 147488 | tf_op jit(solution)/shard_map/ppermute | solution.py:55
  39.3 0.6 window.1
  40.0 0.1 collective-permute-start.11
  40.1 3.4 %collective-permute-start.12 = (bf16[256,512]{1,0:T(8,128)(2,1)S(1)}, bf16[256,512]{1,0:T(8,128)(2,1)S(1)}, u32[]{:S(2)}, u32[]{:S(2)}) collective-permute-start(bf16[256,512]{1,0:T(8,128)(2,1)S(1)} %get-tuple-element.69.refs_4_), channel_id=1, source_target_pairs={{0,2},{1,3},{2,0},{3,1},{4,6},{5,7},{6,4},{7,5},{8,10},{9,11},{10,... | collective-permute-start | bytes 786440 | tf_op jit(solution)/shard_map/ppermute | solution.py:55
  43.5 1.0 %collective-permute-start.9 = (f32[2,1024]{1,0:T(2,128)S(1)}, f32[2,1024]{1,0:T(2,128)S(1)}, u32[]{:S(2)}, u32[]{:S(2)}) collective-permute-start(f32[2,1024]{1,0:T(2,128)S(1)} %get-tuple-element.57.mine), channel_id=1, source_target_pairs={{0,4},{4,0},{1,5},{5,1},{2,6},{6,2},{3,7},{7,3},{8,12},{12,8},{9,1... | collective-permute-start | bytes 24584 | tf_op jit(solution)/shard_map/ppermute | solution.py:59
  44.5 0.8 collective-permute-done.9.theirs
  45.3 0.6 merged.2
  45.9 5.6 %collective-permute-start.10 = (f32[2,1024]{1,0:T(2,128)S(1)}, f32[2,1024]{1,0:T(2,128)S(1)}, u32[]{:S(2)}, u32[]{:S(2)}) collective-permute-start(f32[2,1024]{1,0:T(2,128)S(1)} %get-tuple-element.59.inclusive), channel_id=1, source_target_pairs={{0,24},{8,32},{16,40},{24,48},{32,56},{40,64},{48,72},{56,80},{64,... | collective-permute-start | bytes 24584 | tf_op jit(solution)/shard_map/ppermute | solution.py:51
  51.5 0.8 collective-permute-done.10.mine
  52.3 2.9 %collective-permute-done.12.refs_6_ = bf16[256,512]{1,0:T(8,128)(2,1)S(1)} collective-permute-done((bf16[256,512]{1,0:T(8,128)(2,1)S(1)}, bf16[256,512]{1,0:T(8,128)(2,1)S(1)}, u32[]{:S(2)}, u32[]{:S(2)}) %collective-permute-start.12) | collective-permute-done | bytes 262176 | tf_op jit(solution)/shard_map/ppermute | solution.py:55
  55.2 0.0 collective-permute-done.13.refs_7_
  55.2 1.2 %collective-permute-start.18 = (bf16[144,512]{1,0:T(8,128)(2,1)S(1)}, bf16[144,512]{1,0:T(8,128)(2,1)S(1)}, u32[]{:S(2)}, u32[]{:S(2)}) collective-permute-start(bf16[144,512]{1,0:T(8,128)(2,1)S(1)} %collective-permute-done.6.refs_1_), channel_id=1, source_target_pairs={{0,4},{4,0},{1,5},{5,1},{2,6},{6,2},{3,7},{7,3},{8,12},{12,8},{9,1... | collective-permute-start | bytes 442376 | tf_op jit(solution)/shard_map/ppermute | solution.py:59
  56.4 0.0 collective-permute-start.19
  56.4 0.5 collective-permute-start.14
  56.9 0.0 collective-permute-start.21
  56.9 0.5 collective-permute-start.22
  57.4 0.4 collective-permute-done.14.theirs
  57.8 0.3 collective-permute-start.23
  58.1 0.2 collective-permute-start.24
  58.3 0.0 collective-permute-done.19.refs_10_
  58.3 0.3 collective-permute-start.20
  58.6 0.6 merged.3
  59.2 0.7 collective-permute-done.20.refs_11_
  59.9 6.4 %collective-permute-start.15 = (f32[2,1024]{1,0:T(2,128)S(1)}, f32[2,1024]{1,0:T(2,128)S(1)}, u32[]{:S(2)}, u32[]{:S(2)}) collective-permute-start(f32[2,1024]{1,0:T(2,128)S(1)} %get-tuple-element.65), channel_id=1, source_target_pairs={{0,72},{4,76},{8,80},{12,84},{16,88},{20,92},{24,96},{28,100},{32,... | collective-permute-start | bytes 24584 | tf_op jit(solution)/shard_map/ppermute | solution.py:44
  66.3 8.1 %collective-permute-start.16 = (f32[2,1024]{1,0:T(2,128)S(1)}, f32[2,1024]{1,0:T(2,128)S(1)}, u32[]{:S(2)}, u32[]{:S(2)}) collective-permute-start(f32[2,1024]{1,0:T(2,128)S(1)} %get-tuple-element.65), channel_id=1, source_target_pairs={{0,144},{4,148},{8,152},{12,156},{16,160},{20,164},{24,168},{28,17... | collective-permute-start | bytes 24584 | tf_op jit(solution)/shard_map/ppermute | solution.py:44
  74.5 1.3 %collective-permute-start.17 = (f32[2,1024]{1,0:T(2,128)S(1)}, f32[2,1024]{1,0:T(2,128)S(1)}, u32[]{:S(2)}, u32[]{:S(2)}) collective-permute-start(f32[2,1024]{1,0:T(2,128)S(1)} %get-tuple-element.65), channel_id=1, source_target_pairs={{0,216},{4,220},{8,224},{12,228},{16,232},{20,236},{24,240},{28,24... | collective-permute-start | bytes 24584 | tf_op jit(solution)/shard_map/ppermute | solution.py:44
  75.8 9.2 %attend.1 = bf16[512,1024]{1,0:T(8,128)(2,1)} custom-call(s32[3]{0:T(128)S(1)} %pad_add_fusion.info, bf16[512,1024]{1,0:T(8,128)(2,1)S(1)} %copy-done.2, bf16[144,512]{1,0:T(8,128)(2,1)S(1)} %normed.1.refs_0_, bf16[144,512]{1,0:T(8,128)(2,1)S(1)} %collective-permute-done.6.refs_1_, bf16[144,512]{1,0:T(8,128)(2,1)S(1)} %collective-permute-done.7.refs_2_, ...), custom_call_target="tpu_custom_call" | custom-call | flops 4294967296 | bytes 4194304 | tf_op jit(solution)/shard_map/attend/pallas_call | solution.py:386
  85.0 1.5 %add_convert_fusion = bf16[512,1024]{1,0:T(8,128)(2,1)} fusion(f32[512,1024]{1,0:T(8,128)S(1)} %copy-done.3, f32[512,1024]{1,0:T(8,128)S(1)} %copy-done.4, f32[1024]{0:T(1024)S(1)} %bitcast.9), kind=kLoop, calls=%fused_computation | loop fusion | flops 1572864 | bytes 5246976 | tf_op jit(solution)/shard_map/convert_element_type | solution.py:457
  (26 shorter events, 0.1 us)
Async XLA Ops:
  1.4 6.7 %collective-permute-start = (bf16[3,1024]{1,0:T(4,128)(2,1)S(1)}, bf16[3,1024]{1,0:T(4,128)(2,1)S(1)}, u32[]{:S(2)}, u32[]{:S(2)}) collective-permute-start(bf16[3,1024]{1,0:T(4,128)(2,1)S(1)} %slice.24), channel_id=1, source_target_pairs={{0,4},{4,8},{8,12},{12,16},{16,20},{20,24},{24,28},{28,32},{32,36}... | collective-permute-start | bytes 18440 | tf_op jit(solution)/shard_map/ppermute | solution.py:44
  8.1 5.1 %copy-start.5 = (bf16[3,1024]{1,0:T(4,128)(2,1)}, bf16[3,1024]{1,0:T(4,128)(2,1)S(1)}, u32[]{:S(2)}) copy-start(bf16[3,1024]{1,0:T(4,128)(2,1)S(1)} %collective-permute-done.edge) | copy-start | bytes 18436
  8.1 14.0 %collective-permute-start.1 = (bf16[144,512]{1,0:T(8,128)(2,1)}, bf16[144,512]{1,0:T(8,128)(2,1)S(1)}, u32[]{:S(2)}, u32[]{:S(2)}) collective-permute-start(bf16[144,512]{1,0:T(8,128)(2,1)} %get-tuple-element.50), channel_id=1, source_target_pairs={{0,1},{1,2},{2,3},{3,0},{4,5},{5,6},{6,7},{7,4},{8,9},{9,10},{10,1... | collective-permute-start | bytes 442376 | tf_op jit(solution)/shard_map/ppermute | solution.py:55
  9.5 12.7 %collective-permute-start.2 = (bf16[144,512]{1,0:T(8,128)(2,1)}, bf16[144,512]{1,0:T(8,128)(2,1)S(1)}, u32[]{:S(2)}, u32[]{:S(2)}) collective-permute-start(bf16[144,512]{1,0:T(8,128)(2,1)} %get-tuple-element.51), channel_id=1, source_target_pairs={{0,2},{1,3},{2,0},{3,1},{4,6},{5,7},{6,4},{7,5},{8,10},{9,11},{10,... | collective-permute-start | bytes 442376 | tf_op jit(solution)/shard_map/ppermute | solution.py:55
  12.1 10.1 %collective-permute-start.3 = (bf16[144,512]{1,0:T(8,128)(2,1)}, bf16[144,512]{1,0:T(8,128)(2,1)S(1)}, u32[]{:S(2)}, u32[]{:S(2)}) collective-permute-start(bf16[144,512]{1,0:T(8,128)(2,1)} %get-tuple-element.52), channel_id=1, source_target_pairs={{0,3},{1,0},{2,1},{3,2},{4,7},{5,4},{6,5},{7,6},{8,11},{9,8},{10,9... | collective-permute-start | bytes 442376 | tf_op jit(solution)/shard_map/ppermute | solution.py:55
  13.2 9.0 %copy-start = (f32[144,512]{1,0:T(8,128)S(1)}, f32[144,512]{1,0:T(8,128)}, u32[]{:S(2)}) copy-start(f32[144,512]{1,0:T(8,128)} %get-tuple-element.49.a) | copy-start | bytes 884740
  13.2 62.6 %copy-start.2 = (bf16[512,1024]{1,0:T(8,128)(2,1)S(1)}, bf16[512,1024]{1,0:T(8,128)(2,1)}, u32[]{:S(2)}) copy-start(bf16[512,1024]{1,0:T(8,128)(2,1)} %q_ref.1) | copy-start | bytes 3145732
  22.2 0.7 copy-start.1
  23.1 1.5 %collective-permute-start.4 = (bf16[144,512]{1,0:T(8,128)(2,1)S(1)}, bf16[144,512]{1,0:T(8,128)(2,1)S(1)}, u32[]{:S(2)}, u32[]{:S(2)}) collective-permute-start(bf16[144,512]{1,0:T(8,128)(2,1)S(1)} %normed.1.refs_0_), channel_id=1, source_target_pairs={{0,4},{4,0},{1,5},{5,1},{2,6},{6,2},{3,7},{7,3},{8,12},{12,8},{9,1... | collective-permute-start | bytes 442376 | tf_op jit(solution)/shard_map/ppermute | solution.py:59
  24.5 14.8 %collective-permute-start.5 = (bf16[288,512]{1,0:T(8,128)(2,1)S(1)}, bf16[288,512]{1,0:T(8,128)(2,1)S(1)}, u32[]{:S(2)}, u32[]{:S(2)}) collective-permute-start(bf16[288,512]{1,0:T(8,128)(2,1)S(1)} %pad_maximum_fusion.pair), channel_id=1, source_target_pairs={{0,8},{8,16},{16,24},{24,32},{32,40},{40,48},{48,56},{56,64},{64,7... | collective-permute-start | bytes 884744 | tf_op jit(solution)/shard_map/ppermute | solution.py:51
  28.7 9.6 %collective-permute-start.6 = (bf16[144,512]{1,0:T(8,128)(2,1)S(1)}, bf16[144,512]{1,0:T(8,128)(2,1)S(1)}, u32[]{:S(2)}, u32[]{:S(2)}) collective-permute-start(bf16[144,512]{1,0:T(8,128)(2,1)S(1)} %normed.1.refs_0_), channel_id=1, source_target_pairs={{0,1},{1,2},{2,3},{3,0},{4,5},{5,6},{6,7},{7,4},{8,9},{9,10},{10,1... | collective-permute-start | bytes 442376 | tf_op jit(solution)/shard_map/ppermute | solution.py:55
  29.1 9.1 %collective-permute-start.7 = (bf16[144,512]{1,0:T(8,128)(2,1)S(1)}, bf16[144,512]{1,0:T(8,128)(2,1)S(1)}, u32[]{:S(2)}, u32[]{:S(2)}) collective-permute-start(bf16[144,512]{1,0:T(8,128)(2,1)S(1)} %normed.1.refs_0_), channel_id=1, source_target_pairs={{0,2},{1,3},{2,0},{3,1},{4,6},{5,7},{6,4},{7,5},{8,10},{9,11},{10,... | collective-permute-start | bytes 442376 | tf_op jit(solution)/shard_map/ppermute | solution.py:55
  29.9 9.4 %collective-permute-start.8 = (bf16[144,512]{1,0:T(8,128)(2,1)S(1)}, bf16[144,512]{1,0:T(8,128)(2,1)S(1)}, u32[]{:S(2)}, u32[]{:S(2)}) collective-permute-start(bf16[144,512]{1,0:T(8,128)(2,1)S(1)} %normed.1.refs_0_), channel_id=1, source_target_pairs={{0,3},{1,0},{2,1},{3,2},{4,7},{5,4},{6,5},{7,6},{8,11},{9,8},{10,9... | collective-permute-start | bytes 442376 | tf_op jit(solution)/shard_map/ppermute | solution.py:55
  40.0 12.3 %collective-permute-start.11 = (bf16[256,512]{1,0:T(8,128)(2,1)S(1)}, bf16[256,512]{1,0:T(8,128)(2,1)S(1)}, u32[]{:S(2)}, u32[]{:S(2)}) collective-permute-start(bf16[256,512]{1,0:T(8,128)(2,1)S(1)} %get-tuple-element.69.refs_4_), channel_id=1, source_target_pairs={{0,1},{1,2},{2,3},{3,0},{4,5},{5,6},{6,7},{7,4},{8,9},{9,10},{10,1... | collective-permute-start | bytes 786440 | tf_op jit(solution)/shard_map/ppermute | solution.py:55
  40.1 15.1 %collective-permute-start.12 = (bf16[256,512]{1,0:T(8,128)(2,1)S(1)}, bf16[256,512]{1,0:T(8,128)(2,1)S(1)}, u32[]{:S(2)}, u32[]{:S(2)}) collective-permute-start(bf16[256,512]{1,0:T(8,128)(2,1)S(1)} %get-tuple-element.69.refs_4_), channel_id=1, source_target_pairs={{0,2},{1,3},{2,0},{3,1},{4,6},{5,7},{6,4},{7,5},{8,10},{9,11},{10,... | collective-permute-start | bytes 786440 | tf_op jit(solution)/shard_map/ppermute | solution.py:55
  43.5 11.6 %collective-permute-start.13 = (bf16[256,512]{1,0:T(8,128)(2,1)S(1)}, bf16[256,512]{1,0:T(8,128)(2,1)S(1)}, u32[]{:S(2)}, u32[]{:S(2)}) collective-permute-start(bf16[256,512]{1,0:T(8,128)(2,1)S(1)} %get-tuple-element.69.refs_4_), channel_id=1, source_target_pairs={{0,3},{1,0},{2,1},{3,2},{4,7},{5,4},{6,5},{7,6},{8,11},{9,8},{10,9... | collective-permute-start | bytes 786440 | tf_op jit(solution)/shard_map/ppermute | solution.py:55
  43.5 1.8 %collective-permute-start.9 = (f32[2,1024]{1,0:T(2,128)S(1)}, f32[2,1024]{1,0:T(2,128)S(1)}, u32[]{:S(2)}, u32[]{:S(2)}) collective-permute-start(f32[2,1024]{1,0:T(2,128)S(1)} %get-tuple-element.57.mine), channel_id=1, source_target_pairs={{0,4},{4,0},{1,5},{5,1},{2,6},{6,2},{3,7},{7,3},{8,12},{12,8},{9,1... | collective-permute-start | bytes 24584 | tf_op jit(solution)/shard_map/ppermute | solution.py:59
  45.9 6.4 %collective-permute-start.10 = (f32[2,1024]{1,0:T(2,128)S(1)}, f32[2,1024]{1,0:T(2,128)S(1)}, u32[]{:S(2)}, u32[]{:S(2)}) collective-permute-start(f32[2,1024]{1,0:T(2,128)S(1)} %get-tuple-element.59.inclusive), channel_id=1, source_target_pairs={{0,24},{8,32},{16,40},{24,48},{32,56},{40,64},{48,72},{56,80},{64,... | collective-permute-start | bytes 24584 | tf_op jit(solution)/shard_map/ppermute | solution.py:51
  55.2 2.9 %collective-permute-start.18 = (bf16[144,512]{1,0:T(8,128)(2,1)S(1)}, bf16[144,512]{1,0:T(8,128)(2,1)S(1)}, u32[]{:S(2)}, u32[]{:S(2)}) collective-permute-start(bf16[144,512]{1,0:T(8,128)(2,1)S(1)} %collective-permute-done.6.refs_1_), channel_id=1, source_target_pairs={{0,4},{4,0},{1,5},{5,1},{2,6},{6,2},{3,7},{7,3},{8,12},{12,8},{9,1... | collective-permute-start | bytes 442376 | tf_op jit(solution)/shard_map/ppermute | solution.py:59
  56.4 1.9 %collective-permute-start.19 = (bf16[144,512]{1,0:T(8,128)(2,1)S(1)}, bf16[144,512]{1,0:T(8,128)(2,1)S(1)}, u32[]{:S(2)}, u32[]{:S(2)}) collective-permute-start(bf16[144,512]{1,0:T(8,128)(2,1)S(1)} %collective-permute-done.7.refs_2_), channel_id=1, source_target_pairs={{0,4},{4,0},{1,5},{5,1},{2,6},{6,2},{3,7},{7,3},{8,12},{12,8},{9,1... | collective-permute-start | bytes 442376 | tf_op jit(solution)/shard_map/ppermute | solution.py:59
  56.4 1.4 %collective-permute-start.14 = (f32[2,1024]{1,0:T(2,128)S(1)}, f32[2,1024]{1,0:T(2,128)S(1)}, u32[]{:S(2)}, u32[]{:S(2)}) collective-permute-start(f32[2,1024]{1,0:T(2,128)S(1)} %collective-permute-done.10.mine), channel_id=1, source_target_pairs={{0,4},{4,0},{1,5},{5,1},{2,6},{6,2},{3,7},{7,3},{8,12},{12,8},{9,1... | collective-permute-start | bytes 24584 | tf_op jit(solution)/shard_map/ppermute | solution.py:59
  56.9 9.4 %collective-permute-start.21 = (bf16[256,512]{1,0:T(8,128)(2,1)S(1)}, bf16[256,512]{1,0:T(8,128)(2,1)S(1)}, u32[]{:S(2)}, u32[]{:S(2)}) collective-permute-start(bf16[256,512]{1,0:T(8,128)(2,1)S(1)} %get-tuple-element.69.refs_4_), channel_id=1, source_target_pairs={{0,4},{4,0},{1,5},{5,1},{2,6},{6,2},{3,7},{7,3},{8,12},{12,8},{9,1... | collective-permute-start | bytes 786440 | tf_op jit(solution)/shard_map/ppermute | solution.py:59
  56.9 17.5 %collective-permute-start.22 = (bf16[256,512]{1,0:T(8,128)(2,1)S(1)}, bf16[256,512]{1,0:T(8,128)(2,1)S(1)}, u32[]{:S(2)}, u32[]{:S(2)}) collective-permute-start(bf16[256,512]{1,0:T(8,128)(2,1)S(1)} %collective-permute-done.11.refs_5_), channel_id=1, source_target_pairs={{0,4},{4,0},{1,5},{5,1},{2,6},{6,2},{3,7},{7,3},{8,12},{12,8},{9,1... | collective-permute-start | bytes 786440 | tf_op jit(solution)/shard_map/ppermute | solution.py:59
  57.8 18.0 %collective-permute-start.23 = (bf16[256,512]{1,0:T(8,128)(2,1)S(1)}, bf16[256,512]{1,0:T(8,128)(2,1)S(1)}, u32[]{:S(2)}, u32[]{:S(2)}) collective-permute-start(bf16[256,512]{1,0:T(8,128)(2,1)S(1)} %collective-permute-done.12.refs_6_), channel_id=1, source_target_pairs={{0,4},{4,0},{1,5},{5,1},{2,6},{6,2},{3,7},{7,3},{8,12},{12,8},{9,1... | collective-permute-start | bytes 786440 | tf_op jit(solution)/shard_map/ppermute | solution.py:59
  58.1 17.7 %collective-permute-start.24 = (bf16[256,512]{1,0:T(8,128)(2,1)S(1)}, bf16[256,512]{1,0:T(8,128)(2,1)S(1)}, u32[]{:S(2)}, u32[]{:S(2)}) collective-permute-start(bf16[256,512]{1,0:T(8,128)(2,1)S(1)} %collective-permute-done.13.refs_7_), channel_id=1, source_target_pairs={{0,4},{4,0},{1,5},{5,1},{2,6},{6,2},{3,7},{7,3},{8,12},{12,8},{9,1... | collective-permute-start | bytes 786440 | tf_op jit(solution)/shard_map/ppermute | solution.py:59
  58.3 1.6 %collective-permute-start.20 = (bf16[144,512]{1,0:T(8,128)(2,1)S(1)}, bf16[144,512]{1,0:T(8,128)(2,1)S(1)}, u32[]{:S(2)}, u32[]{:S(2)}) collective-permute-start(bf16[144,512]{1,0:T(8,128)(2,1)S(1)} %collective-permute-done.8.refs_3_), channel_id=1, source_target_pairs={{0,4},{4,0},{1,5},{5,1},{2,6},{6,2},{3,7},{7,3},{8,12},{12,8},{9,1... | collective-permute-start | bytes 442376 | tf_op jit(solution)/shard_map/ppermute | solution.py:59
  59.9 25.1 %copy-start.3 = (f32[512,1024]{1,0:T(8,128)S(1)}, f32[512,1024]{1,0:T(8,128)}, u32[]{:S(2)}) copy-start(f32[512,1024]{1,0:T(8,128)} %get-tuple-element.45) | copy-start | bytes 6291460
  59.9 25.1 %copy-start.4 = (f32[512,1024]{1,0:T(8,128)S(1)}, f32[512,1024]{1,0:T(8,128)}, u32[]{:S(2)}) copy-start(f32[512,1024]{1,0:T(8,128)} %get-tuple-element.46) | copy-start | bytes 6291460
  59.9 25.1 %collective-permute-start.15 = (f32[2,1024]{1,0:T(2,128)S(1)}, f32[2,1024]{1,0:T(2,128)S(1)}, u32[]{:S(2)}, u32[]{:S(2)}) collective-permute-start(f32[2,1024]{1,0:T(2,128)S(1)} %get-tuple-element.65), channel_id=1, source_target_pairs={{0,72},{4,76},{8,80},{12,84},{16,88},{20,92},{24,96},{28,100},{32,... | collective-permute-start | bytes 24584 | tf_op jit(solution)/shard_map/ppermute | solution.py:44
  66.3 18.7 %collective-permute-start.16 = (f32[2,1024]{1,0:T(2,128)S(1)}, f32[2,1024]{1,0:T(2,128)S(1)}, u32[]{:S(2)}, u32[]{:S(2)}) collective-permute-start(f32[2,1024]{1,0:T(2,128)S(1)} %get-tuple-element.65), channel_id=1, source_target_pairs={{0,144},{4,148},{8,152},{12,156},{16,160},{20,164},{24,168},{28,17... | collective-permute-start | bytes 24584 | tf_op jit(solution)/shard_map/ppermute | solution.py:44
  74.5 10.5 %collective-permute-start.17 = (f32[2,1024]{1,0:T(2,128)S(1)}, f32[2,1024]{1,0:T(2,128)S(1)}, u32[]{:S(2)}, u32[]{:S(2)}) collective-permute-start(f32[2,1024]{1,0:T(2,128)S(1)} %get-tuple-element.65), channel_id=1, source_target_pairs={{0,216},{4,220},{8,224},{12,228},{16,232},{20,236},{24,240},{28,24... | collective-permute-start | bytes 24584 | tf_op jit(solution)/shard_map/ppermute | solution.py:44

commit v8 on v7

--- a/solution.py
+++ b/solution.py
@@ -440,20 +440,20 @@
     duo, before, inclusive, got = window(info, pair, arrived, branch_in.shape[1])
     two = [turned(duo, k) for k in range(1, PARTS)]
     before, inclusive = merged(info, before, inclusive, got, swapped(got))
-    far = forked(inclusive, 3, 6)
+    far = [forked(inclusive, 3, 6), forked(inclusive, 9, 12)]
     far, two, own, duo = lax.optimization_barrier((far, two, own, duo))
     other = [swapped(piece) for piece in own]
+    far = jnp.concatenate(far)
     before, inclusive = merged(info, before, inclusive, far, swapped(far))
     two = [duo] + two
     others = [swapped(piece) for piece in two]
-    far = [shifted(inclusive, 18 * k) for k in (1, 2, 3)]
+    far = [shifted(inclusive, 30), shifted(inclusive, 60)]
     heads = queries.shape[1] // HD
     pieces = (mine, *own, *two, beside, *other, *others)
     attended = attend(0, heads, info, queries, pieces, ())
     *far, attended = lax.optimization_barrier((*far, attended))
-    factor, state = (before[0:1], before[1:2])
-    for couple in far:
-        factor, state = (couple[0:1] * factor, factor * couple[1:2] + state)
+    state = far[0][0:1] * far[1][1:2] + far[0][1:2]
+    state = before[0:1] * state + before[1:2]
     recurrent_out = (u + w * state).astype(BF16)
     return (recurrent_out, attended)
 

time: 86.9 us -> 82.9 us (0.954)
  waiting for transfers between devices: 14.6 us -> 12.4 us
  starting transfers between devices: 44.9 us -> 42.8 us
    ppermute x2 -> x3, starting transfers between devices: 9.73 us -> 16.1 us  [forked(): return lax.ppermute(value, SEQ, pairs)]
    ppermute x4 -> x3, starting transfers between devices: 19.5 us -> 13.4 us  [shifted(): lax.ppermute(value, SEQ, [(k, k + steps) for k in range(count - steps)])]
    ppermute x9, waiting for transfers between devices: 10.5 us -> 8.16 us  [turned(): lax.ppermute(value, 'mp', [(k, (k + steps) % PARTS) for k in range(PARTS)])]
    ppermute x9, starting transfers between devices: 11.6 us -> 9.86 us  [turned(): lax.ppermute(value, 'mp', [(k, (k + steps) % PARTS) for k in range(PARTS)])]
  transfers between devices with their start and end apart: 25 -> 25, of which waited for: 8 -> 8; matrix products, arithmetic and copies ran while one was open for 0% -> 0% of each run, Pallas kernels for 26% -> 27%
where the time goes in v8:
time: 82.9 us; the launch traced here: 82.3 us
  starting transfers between devices  42.8 us (52%)
  Pallas kernels  23.1 us (28%)
  waiting for transfers between devices  12.4 us (15%)
  other arithmetic  1.62 us (2%)
  local copies, waits for them, and re-layouts  1.44 us (2%)
  between operations  0.87 us (1%)
    ppermute x3, starting transfers between devices, forked(): return lax.ppermute(value, SEQ, pairs)  16.1 us
    ppermute x3, starting transfers between devices, shifted(): lax.ppermute(value, SEQ, [(k, k + steps) for k in range(count - steps)])  13.4 us
    ppermute x9, starting transfers between devices, turned(): lax.ppermute(value, 'mp', [(k, (k + steps) % PARTS) for k in range(PARTS)])  9.86 us
    pallas_call x1, Pallas kernels, attend(): pl.pallas_call(attend_kernel, name='attend', grid=(count,), out_shape=jax...  9.18 us
    pallas_call x1, Pallas kernels, recur(): pl.pallas_call(recur_kernel, name='recur', grid=(count,), out_shape=[jax....  8.95 us
    ppermute x9, waiting for transfers between devices, turned(): lax.ppermute(value, 'mp', [(k, (k + steps) % PARTS) for k in range(PARTS)])  8.16 us
    ppermute x10, starting transfers between devices, swapped(): return lax.ppermute(value, CORE, [(0, 1), (1, 0)])  3.55 us
    ppermute x10, waiting for transfers between devices, swapped(): return lax.ppermute(value, CORE, [(0, 1), (1, 0)])  3.47 us
  transfers between devices with their start and end apart: 25, of which 8 were waited for; matrix products, arithmetic and copies ran while one was open for 0% of the time, Pallas kernels for 27%

profile of v8, /device:TPU:3, one launch (start us, length us, event | category | flops | bytes accessed | tf_op | source)
XLA Modules:
  0.0 82.3 jit_solution(1723519318382824482)
XLA Ops:
  0.6 0.7 slice.18
  1.4 3.7 %collective-permute-start = (bf16[3,1024]{1,0:T(4,128)(2,1)S(1)}, bf16[3,1024]{1,0:T(4,128)(2,1)S(1)}, u32[]{:S(2)}, u32[]{:S(2)}) collective-permute-start(bf16[3,1024]{1,0:T(4,128)(2,1)S(1)} %slice.18), channel_id=1, source_target_pairs={{0,4},{4,8},{8,12},{12,16},{16,20},{20,24},{24,28},{28,32},{32,36}... | collective-permute-start | bytes 18440 | tf_op jit(solution)/shard_map/ppermute | solution.py:44
  5.0 3.1 %project.1 = (f32[144,512]{1,0:T(8,128)}, bf16[144,512]{1,0:T(8,128)(2,1)}, bf16[144,512]{1,0:T(8,128)(2,1)}, bf16[144,512]{1,0:T(8,128)(2,1)}) custom-call(s32[1]{0:T(128)} %bitcast.place, bf16[512,1024]{1,0:T(8,128)(2,1)} %stream.1, f32[1,1024]{1,0:T(1,128)} %bitcast.10, bf16[1024,512]{1,0:T(8,128)(2,1)} %weight.1), custom_call_target="tpu_custom_call" | custom-call | flops 536870912 | bytes 3145728 | tf_op jit(solution)/shard_map/project/pallas_call | solution.py:80
  8.1 0.0 collective-permute-done.edge
  8.1 1.4 %collective-permute-start.1 = (bf16[144,512]{1,0:T(8,128)(2,1)}, bf16[144,512]{1,0:T(8,128)(2,1)S(1)}, u32[]{:S(2)}, u32[]{:S(2)}) collective-permute-start(bf16[144,512]{1,0:T(8,128)(2,1)} %get-tuple-element.50), channel_id=1, source_target_pairs={{0,1},{1,2},{2,3},{3,0},{4,5},{5,6},{6,7},{7,4},{8,9},{9,10},{10,1... | collective-permute-start | bytes 442376 | tf_op jit(solution)/shard_map/ppermute | solution.py:55
  9.5 2.6 %collective-permute-start.2 = (bf16[144,512]{1,0:T(8,128)(2,1)}, bf16[144,512]{1,0:T(8,128)(2,1)S(1)}, u32[]{:S(2)}, u32[]{:S(2)}) collective-permute-start(bf16[144,512]{1,0:T(8,128)(2,1)} %get-tuple-element.51), channel_id=1, source_target_pairs={{0,2},{1,3},{2,0},{3,1},{4,6},{5,7},{6,4},{7,5},{8,10},{9,11},{10,... | collective-permute-start | bytes 442376 | tf_op jit(solution)/shard_map/ppermute | solution.py:55
  12.1 1.1 %collective-permute-start.3 = (bf16[144,512]{1,0:T(8,128)(2,1)}, bf16[144,512]{1,0:T(8,128)(2,1)S(1)}, u32[]{:S(2)}, u32[]{:S(2)}) collective-permute-start(bf16[144,512]{1,0:T(8,128)(2,1)} %get-tuple-element.52), channel_id=1, source_target_pairs={{0,3},{1,0},{2,1},{3,2},{4,7},{5,4},{6,5},{7,6},{8,11},{9,8},{10,9... | collective-permute-start | bytes 442376 | tf_op jit(solution)/shard_map/ppermute | solution.py:55
  13.2 9.0 %recur.1 = (f32[512,1024]{1,0:T(8,128)}, f32[512,1024]{1,0:T(8,128)}, f32[2,1024]{1,0:T(2,128)}) custom-call(bf16[512,1024]{1,0:T(8,128)(2,1)} %branch.1, bf16[3,1024]{1,0:T(4,128)(2,1)} %copy-done.5, bf16[512,1024]{1,0:T(8,128)(2,1)} %gate.1, f32[4,1024]{1,0:T(4,128)} %taps.1, f32[1,1024]{1,0:T(1,128)} %bitcast.11, bf16[4,256,256]{2,1,0:T(8,128)(2,1)} %in_w.1, ...), custom_call_target="tpu_custom_call" | custom-call | flops 1073741824 | bytes 8388608 | tf_op jit(solution)/shard_map/recur/pallas_call | solution.py:282
  22.1 0.0 collective-permute-done.1.b
  22.2 0.7 copy-done.1
  22.9 0.2 normed.1.refs_0_
  23.1 0.1 collective-permute-start.4
  23.2 1.4 %collective-permute-done.4.refs_8_ = bf16[144,512]{1,0:T(8,128)(2,1)S(1)} collective-permute-done((bf16[144,512]{1,0:T(8,128)(2,1)S(1)}, bf16[144,512]{1,0:T(8,128)(2,1)S(1)}, u32[]{:S(2)}, u32[]{:S(2)}) %collective-permute-start.4) | collective-permute-done | bytes 147488 | tf_op jit(solution)/shard_map/ppermute | solution.py:59
  24.5 4.1 %collective-permute-start.5 = (bf16[288,512]{1,0:T(8,128)(2,1)S(1)}, bf16[288,512]{1,0:T(8,128)(2,1)S(1)}, u32[]{:S(2)}, u32[]{:S(2)}) collective-permute-start(bf16[288,512]{1,0:T(8,128)(2,1)S(1)} %pad_maximum_fusion.pair), channel_id=1, source_target_pairs={{0,8},{8,16},{16,24},{24,32},{32,40},{40,48},{48,56},{56,64},{64,7... | collective-permute-start | bytes 884744 | tf_op jit(solution)/shard_map/ppermute | solution.py:51
  28.7 0.1 collective-permute-start.8
  28.8 2.2 %collective-permute-start.7 = (bf16[144,512]{1,0:T(8,128)(2,1)S(1)}, bf16[144,512]{1,0:T(8,128)(2,1)S(1)}, u32[]{:S(2)}, u32[]{:S(2)}) collective-permute-start(bf16[144,512]{1,0:T(8,128)(2,1)S(1)} %normed.1.refs_0_), channel_id=1, source_target_pairs={{0,2},{1,3},{2,0},{3,1},{4,6},{5,7},{6,4},{7,5},{8,10},{9,11},{10,... | collective-permute-start | bytes 442376 | tf_op jit(solution)/shard_map/ppermute | solution.py:55
  30.9 0.0 collective-permute-start.6
  30.9 0.1 pad_add_fusion.info
  31.0 3.5 %collective-permute-done.8.refs_3_ = bf16[144,512]{1,0:T(8,128)(2,1)S(1)} collective-permute-done((bf16[144,512]{1,0:T(8,128)(2,1)S(1)}, bf16[144,512]{1,0:T(8,128)(2,1)S(1)}, u32[]{:S(2)}, u32[]{:S(2)}) %collective-permute-start.8) | collective-permute-done | bytes 147488 | tf_op jit(solution)/shard_map/ppermute | solution.py:55
  34.5 1.4 %collective-permute-done.7.refs_2_ = bf16[144,512]{1,0:T(8,128)(2,1)S(1)} collective-permute-done((bf16[144,512]{1,0:T(8,128)(2,1)S(1)}, bf16[144,512]{1,0:T(8,128)(2,1)S(1)}, u32[]{:S(2)}, u32[]{:S(2)}) %collective-permute-start.7) | collective-permute-done | bytes 147488 | tf_op jit(solution)/shard_map/ppermute | solution.py:55
  35.9 3.2 %collective-permute-done.6.refs_1_ = bf16[144,512]{1,0:T(8,128)(2,1)S(1)} collective-permute-done((bf16[144,512]{1,0:T(8,128)(2,1)S(1)}, bf16[144,512]{1,0:T(8,128)(2,1)S(1)}, u32[]{:S(2)}, u32[]{:S(2)}) %collective-permute-start.6) | collective-permute-done | bytes 147488 | tf_op jit(solution)/shard_map/ppermute | solution.py:55
  39.2 0.0 collective-permute-done.5.arrived
  39.2 0.6 window.1
  39.8 0.4 collective-permute-start.14
  40.2 2.1 %collective-permute-start.13 = (bf16[256,512]{1,0:T(8,128)(2,1)S(1)}, bf16[256,512]{1,0:T(8,128)(2,1)S(1)}, u32[]{:S(2)}, u32[]{:S(2)}) collective-permute-start(bf16[256,512]{1,0:T(8,128)(2,1)S(1)} %get-tuple-element.71.refs_4_), channel_id=1, source_target_pairs={{0,2},{1,3},{2,0},{3,1},{4,6},{5,7},{6,4},{7,5},{8,10},{9,11},{10,... | collective-permute-start | bytes 786440 | tf_op jit(solution)/shard_map/ppermute | solution.py:55
  42.2 0.1 collective-permute-start.12
  42.3 1.3 %collective-permute-start.9 = (f32[2,1024]{1,0:T(2,128)S(1)}, f32[2,1024]{1,0:T(2,128)S(1)}, u32[]{:S(2)}, u32[]{:S(2)}) collective-permute-start(f32[2,1024]{1,0:T(2,128)S(1)} %get-tuple-element.57.mine), channel_id=1, source_target_pairs={{0,4},{4,0},{1,5},{5,1},{2,6},{6,2},{3,7},{7,3},{8,12},{12,8},{9,1... | collective-permute-start | bytes 24584 | tf_op jit(solution)/shard_map/ppermute | solution.py:59
  43.6 0.8 %collective-permute-done.9.theirs = f32[2,1024]{1,0:T(2,128)S(1)} collective-permute-done((f32[2,1024]{1,0:T(2,128)S(1)}, f32[2,1024]{1,0:T(2,128)S(1)}, u32[]{:S(2)}, u32[]{:S(2)}) %collective-permute-start.9) | collective-permute-done | bytes 8224 | tf_op jit(solution)/shard_map/ppermute | solution.py:59
  44.5 0.6 merged.2
  45.0 5.8 %collective-permute-start.11 = (f32[2,1024]{1,0:T(2,128)S(1)}, f32[2,1024]{1,0:T(2,128)S(1)}, u32[]{:S(2)}, u32[]{:S(2)}) collective-permute-start(f32[2,1024]{1,0:T(2,128)S(1)} %get-tuple-element.59.inclusive), channel_id=1, source_target_pairs={{0,72},{8,80},{16,88},{24,96},{32,104},{40,112},{48,120},{56,128},... | collective-permute-start | bytes 24584 | tf_op jit(solution)/shard_map/ppermute | solution.py:51
  50.8 6.1 %collective-permute-start.10 = (f32[2,1024]{1,0:T(2,128)S(1)}, f32[2,1024]{1,0:T(2,128)S(1)}, u32[]{:S(2)}, u32[]{:S(2)}) collective-permute-start(f32[2,1024]{1,0:T(2,128)S(1)} %get-tuple-element.59.inclusive), channel_id=1, source_target_pairs={{0,24},{8,32},{16,40},{24,48},{32,56},{40,64},{48,72},{56,80},{64,... | collective-permute-start | bytes 24584 | tf_op jit(solution)/shard_map/ppermute | solution.py:51
  57.0 0.8 collective-permute-done.10
  57.8 0.0 collective-permute-done.14.refs_7_
  57.8 0.1 collective-permute-start.18
  57.9 0.5 collective-permute-start.19
  58.4 0.2 collective-permute-start.15
  58.6 0.4 collective-permute-start.21
  59.0 0.3 collective-permute-start.22
  59.3 0.4 collective-permute-done.15.theirs
  59.7 0.2 collective-permute-start.23
  59.8 0.3 collective-permute-start.24
  60.2 0.2 collective-permute-start.20
  60.3 0.6 merged.3
  60.9 0.9 %collective-permute-done.20.refs_11_ = bf16[144,512]{1,0:T(8,128)(2,1)S(1)} collective-permute-done((bf16[144,512]{1,0:T(8,128)(2,1)S(1)}, bf16[144,512]{1,0:T(8,128)(2,1)S(1)}, u32[]{:S(2)}, u32[]{:S(2)}) %collective-permute-start.20) | collective-permute-done | bytes 147488 | tf_op jit(solution)/shard_map/ppermute | solution.py:59
  61.8 3.6 %collective-permute-start.17 = (f32[2,1024]{1,0:T(2,128)S(1)}, f32[2,1024]{1,0:T(2,128)S(1)}, u32[]{:S(2)}, u32[]{:S(2)}) collective-permute-start(f32[2,1024]{1,0:T(2,128)S(1)} %get-tuple-element.67), channel_id=1, source_target_pairs={{0,240},{4,244},{8,248},{12,252},{1,241},{5,245},{9,249},{13,253},... | collective-permute-start | bytes 24584 | tf_op jit(solution)/shard_map/ppermute | solution.py:44
  65.4 6.1 %collective-permute-start.16 = (f32[2,1024]{1,0:T(2,128)S(1)}, f32[2,1024]{1,0:T(2,128)S(1)}, u32[]{:S(2)}, u32[]{:S(2)}) collective-permute-start(f32[2,1024]{1,0:T(2,128)S(1)} %get-tuple-element.67), channel_id=1, source_target_pairs={{0,120},{4,124},{8,128},{12,132},{16,136},{20,140},{24,144},{28,14... | collective-permute-start | bytes 24584 | tf_op jit(solution)/shard_map/ppermute | solution.py:44
  71.6 9.2 %attend.1 = bf16[512,1024]{1,0:T(8,128)(2,1)} custom-call(s32[3]{0:T(128)S(1)} %pad_add_fusion.info, bf16[512,1024]{1,0:T(8,128)(2,1)S(1)} %copy-done.2, bf16[144,512]{1,0:T(8,128)(2,1)S(1)} %normed.1.refs_0_, bf16[144,512]{1,0:T(8,128)(2,1)S(1)} %collective-permute-done.6.refs_1_, bf16[144,512]{1,0:T(8,128)(2,1)S(1)} %collective-permute-done.7.refs_2_, ...), custom_call_target="tpu_custom_call" | custom-call | flops 4294967296 | bytes 4194304 | tf_op jit(solution)/shard_map/attend/pallas_call | solution.py:386
  80.8 1.5 %add_convert_fusion = bf16[512,1024]{1,0:T(8,128)(2,1)} fusion(f32[512,1024]{1,0:T(8,128)S(1)} %copy-done.3, f32[512,1024]{1,0:T(8,128)S(1)} %copy-done.4, f32[1024]{0:T(1024)S(1)} %bitcast.9), kind=kLoop, calls=%fused_computation | loop fusion | flops 1572864 | bytes 5246976 | tf_op jit(solution)/shard_map/convert_element_type | solution.py:457
  (27 shorter events, 0.1 us)
Async XLA Ops:
  1.4 6.7 %collective-permute-start = (bf16[3,1024]{1,0:T(4,128)(2,1)S(1)}, bf16[3,1024]{1,0:T(4,128)(2,1)S(1)}, u32[]{:S(2)}, u32[]{:S(2)}) collective-permute-start(bf16[3,1024]{1,0:T(4,128)(2,1)S(1)} %slice.18), channel_id=1, source_target_pairs={{0,4},{4,8},{8,12},{12,16},{16,20},{20,24},{24,28},{28,32},{32,36}... | collective-permute-start | bytes 18440 | tf_op jit(solution)/shard_map/ppermute | solution.py:44
  8.1 5.1 %copy-start.5 = (bf16[3,1024]{1,0:T(4,128)(2,1)}, bf16[3,1024]{1,0:T(4,128)(2,1)S(1)}, u32[]{:S(2)}) copy-start(bf16[3,1024]{1,0:T(4,128)(2,1)S(1)} %collective-permute-done.edge) | copy-start | bytes 18436
  8.1 14.0 %collective-permute-start.1 = (bf16[144,512]{1,0:T(8,128)(2,1)}, bf16[144,512]{1,0:T(8,128)(2,1)S(1)}, u32[]{:S(2)}, u32[]{:S(2)}) collective-permute-start(bf16[144,512]{1,0:T(8,128)(2,1)} %get-tuple-element.50), channel_id=1, source_target_pairs={{0,1},{1,2},{2,3},{3,0},{4,5},{5,6},{6,7},{7,4},{8,9},{9,10},{10,1... | collective-permute-start | bytes 442376 | tf_op jit(solution)/shard_map/ppermute | solution.py:55
  9.5 12.7 %collective-permute-start.2 = (bf16[144,512]{1,0:T(8,128)(2,1)}, bf16[144,512]{1,0:T(8,128)(2,1)S(1)}, u32[]{:S(2)}, u32[]{:S(2)}) collective-permute-start(bf16[144,512]{1,0:T(8,128)(2,1)} %get-tuple-element.51), channel_id=1, source_target_pairs={{0,2},{1,3},{2,0},{3,1},{4,6},{5,7},{6,4},{7,5},{8,10},{9,11},{10,... | collective-permute-start | bytes 442376 | tf_op jit(solution)/shard_map/ppermute | solution.py:55
  12.1 10.1 %collective-permute-start.3 = (bf16[144,512]{1,0:T(8,128)(2,1)}, bf16[144,512]{1,0:T(8,128)(2,1)S(1)}, u32[]{:S(2)}, u32[]{:S(2)}) collective-permute-start(bf16[144,512]{1,0:T(8,128)(2,1)} %get-tuple-element.52), channel_id=1, source_target_pairs={{0,3},{1,0},{2,1},{3,2},{4,7},{5,4},{6,5},{7,6},{8,11},{9,8},{10,9... | collective-permute-start | bytes 442376 | tf_op jit(solution)/shard_map/ppermute | solution.py:55
  13.2 9.0 %copy-start = (f32[144,512]{1,0:T(8,128)S(1)}, f32[144,512]{1,0:T(8,128)}, u32[]{:S(2)}) copy-start(f32[144,512]{1,0:T(8,128)} %get-tuple-element.49.a) | copy-start | bytes 884740
  13.2 58.4 %copy-start.2 = (bf16[512,1024]{1,0:T(8,128)(2,1)S(1)}, bf16[512,1024]{1,0:T(8,128)(2,1)}, u32[]{:S(2)}) copy-start(bf16[512,1024]{1,0:T(8,128)(2,1)} %q_ref.1) | copy-start | bytes 3145732
  22.2 0.7 copy-start.1
  23.1 1.5 %collective-permute-start.4 = (bf16[144,512]{1,0:T(8,128)(2,1)S(1)}, bf16[144,512]{1,0:T(8,128)(2,1)S(1)}, u32[]{:S(2)}, u32[]{:S(2)}) collective-permute-start(bf16[144,512]{1,0:T(8,128)(2,1)S(1)} %normed.1.refs_0_), channel_id=1, source_target_pairs={{0,4},{4,0},{1,5},{5,1},{2,6},{6,2},{3,7},{7,3},{8,12},{12,8},{9,1... | collective-permute-start | bytes 442376 | tf_op jit(solution)/shard_map/ppermute | solution.py:59
  24.5 14.6 %collective-permute-start.5 = (bf16[288,512]{1,0:T(8,128)(2,1)S(1)}, bf16[288,512]{1,0:T(8,128)(2,1)S(1)}, u32[]{:S(2)}, u32[]{:S(2)}) collective-permute-start(bf16[288,512]{1,0:T(8,128)(2,1)S(1)} %pad_maximum_fusion.pair), channel_id=1, source_target_pairs={{0,8},{8,16},{16,24},{24,32},{32,40},{40,48},{48,56},{56,64},{64,7... | collective-permute-start | bytes 884744 | tf_op jit(solution)/shard_map/ppermute | solution.py:51
  28.7 5.9 %collective-permute-start.8 = (bf16[144,512]{1,0:T(8,128)(2,1)S(1)}, bf16[144,512]{1,0:T(8,128)(2,1)S(1)}, u32[]{:S(2)}, u32[]{:S(2)}) collective-permute-start(bf16[144,512]{1,0:T(8,128)(2,1)S(1)} %normed.1.refs_0_), channel_id=1, source_target_pairs={{0,3},{1,0},{2,1},{3,2},{4,7},{5,4},{6,5},{7,6},{8,11},{9,8},{10,9... | collective-permute-start | bytes 442376 | tf_op jit(solution)/shard_map/ppermute | solution.py:55
  28.8 7.2 %collective-permute-start.7 = (bf16[144,512]{1,0:T(8,128)(2,1)S(1)}, bf16[144,512]{1,0:T(8,128)(2,1)S(1)}, u32[]{:S(2)}, u32[]{:S(2)}) collective-permute-start(bf16[144,512]{1,0:T(8,128)(2,1)S(1)} %normed.1.refs_0_), channel_id=1, source_target_pairs={{0,2},{1,3},{2,0},{3,1},{4,6},{5,7},{6,4},{7,5},{8,10},{9,11},{10,... | collective-permute-start | bytes 442376 | tf_op jit(solution)/shard_map/ppermute | solution.py:55
  30.9 8.2 %collective-permute-start.6 = (bf16[144,512]{1,0:T(8,128)(2,1)S(1)}, bf16[144,512]{1,0:T(8,128)(2,1)S(1)}, u32[]{:S(2)}, u32[]{:S(2)}) collective-permute-start(bf16[144,512]{1,0:T(8,128)(2,1)S(1)} %normed.1.refs_0_), channel_id=1, source_target_pairs={{0,1},{1,2},{2,3},{3,0},{4,5},{5,6},{6,7},{7,4},{8,9},{9,10},{10,1... | collective-permute-start | bytes 442376 | tf_op jit(solution)/shard_map/ppermute | solution.py:55
  39.8 18.0 %collective-permute-start.14 = (bf16[256,512]{1,0:T(8,128)(2,1)S(1)}, bf16[256,512]{1,0:T(8,128)(2,1)S(1)}, u32[]{:S(2)}, u32[]{:S(2)}) collective-permute-start(bf16[256,512]{1,0:T(8,128)(2,1)S(1)} %get-tuple-element.71.refs_4_), channel_id=1, source_target_pairs={{0,3},{1,0},{2,1},{3,2},{4,7},{5,4},{6,5},{7,6},{8,11},{9,8},{10,9... | collective-permute-start | bytes 786440 | tf_op jit(solution)/shard_map/ppermute | solution.py:55
  40.2 17.6 %collective-permute-start.13 = (bf16[256,512]{1,0:T(8,128)(2,1)S(1)}, bf16[256,512]{1,0:T(8,128)(2,1)S(1)}, u32[]{:S(2)}, u32[]{:S(2)}) collective-permute-start(bf16[256,512]{1,0:T(8,128)(2,1)S(1)} %get-tuple-element.71.refs_4_), channel_id=1, source_target_pairs={{0,2},{1,3},{2,0},{3,1},{4,6},{5,7},{6,4},{7,5},{8,10},{9,11},{10,... | collective-permute-start | bytes 786440 | tf_op jit(solution)/shard_map/ppermute | solution.py:55
  42.2 15.5 %collective-permute-start.12 = (bf16[256,512]{1,0:T(8,128)(2,1)S(1)}, bf16[256,512]{1,0:T(8,128)(2,1)S(1)}, u32[]{:S(2)}, u32[]{:S(2)}) collective-permute-start(bf16[256,512]{1,0:T(8,128)(2,1)S(1)} %get-tuple-element.71.refs_4_), channel_id=1, source_target_pairs={{0,1},{1,2},{2,3},{3,0},{4,5},{5,6},{6,7},{7,4},{8,9},{9,10},{10,1... | collective-permute-start | bytes 786440 | tf_op jit(solution)/shard_map/ppermute | solution.py:55
  42.3 2.1 %collective-permute-start.9 = (f32[2,1024]{1,0:T(2,128)S(1)}, f32[2,1024]{1,0:T(2,128)S(1)}, u32[]{:S(2)}, u32[]{:S(2)}) collective-permute-start(f32[2,1024]{1,0:T(2,128)S(1)} %get-tuple-element.57.mine), channel_id=1, source_target_pairs={{0,4},{4,0},{1,5},{5,1},{2,6},{6,2},{3,7},{7,3},{8,12},{12,8},{9,1... | collective-permute-start | bytes 24584 | tf_op jit(solution)/shard_map/ppermute | solution.py:59
  45.0 12.0 %collective-permute-start.11 = (f32[2,1024]{1,0:T(2,128)S(1)}, f32[2,1024]{1,0:T(2,128)S(1)}, u32[]{:S(2)}, u32[]{:S(2)}) collective-permute-start(f32[2,1024]{1,0:T(2,128)S(1)} %get-tuple-element.59.inclusive), channel_id=1, source_target_pairs={{0,72},{8,80},{16,88},{24,96},{32,104},{40,112},{48,120},{56,128},... | collective-permute-start | bytes 24584 | tf_op jit(solution)/shard_map/ppermute | solution.py:51
  50.8 6.9 %collective-permute-start.10 = (f32[2,1024]{1,0:T(2,128)S(1)}, f32[2,1024]{1,0:T(2,128)S(1)}, u32[]{:S(2)}, u32[]{:S(2)}) collective-permute-start(f32[2,1024]{1,0:T(2,128)S(1)} %get-tuple-element.59.inclusive), channel_id=1, source_target_pairs={{0,24},{8,32},{16,40},{24,48},{32,56},{40,64},{48,72},{56,80},{64,... | collective-permute-start | bytes 24584 | tf_op jit(solution)/shard_map/ppermute | solution.py:51
  57.8 2.1 %collective-permute-start.18 = (bf16[144,512]{1,0:T(8,128)(2,1)S(1)}, bf16[144,512]{1,0:T(8,128)(2,1)S(1)}, u32[]{:S(2)}, u32[]{:S(2)}) collective-permute-start(bf16[144,512]{1,0:T(8,128)(2,1)S(1)} %collective-permute-done.6.refs_1_), channel_id=1, source_target_pairs={{0,4},{4,0},{1,5},{5,1},{2,6},{6,2},{3,7},{7,3},{8,12},{12,8},{9,1... | collective-permute-start | bytes 442376 | tf_op jit(solution)/shard_map/ppermute | solution.py:59
  57.9 2.3 %collective-permute-start.19 = (bf16[144,512]{1,0:T(8,128)(2,1)S(1)}, bf16[144,512]{1,0:T(8,128)(2,1)S(1)}, u32[]{:S(2)}, u32[]{:S(2)}) collective-permute-start(bf16[144,512]{1,0:T(8,128)(2,1)S(1)} %collective-permute-done.7.refs_2_), channel_id=1, source_target_pairs={{0,4},{4,0},{1,5},{5,1},{2,6},{6,2},{3,7},{7,3},{8,12},{12,8},{9,1... | collective-permute-start | bytes 442376 | tf_op jit(solution)/shard_map/ppermute | solution.py:59
  58.4 1.3 %collective-permute-start.15 = (f32[4,1024]{1,0:T(4,128)S(1)}, f32[4,1024]{1,0:T(4,128)S(1)}, u32[]{:S(2)}, u32[]{:S(2)}) collective-permute-start(f32[4,1024]{1,0:T(4,128)S(1)} %pad_maximum_fusion.1.mine), channel_id=1, source_target_pairs={{0,4},{4,0},{1,5},{5,1},{2,6},{6,2},{3,7},{7,3},{8,12},{12,8},{9,1... | collective-permute-start | bytes 49160 | tf_op jit(solution)/shard_map/ppermute | solution.py:59
  58.6 6.8 %collective-permute-start.21 = (bf16[256,512]{1,0:T(8,128)(2,1)S(1)}, bf16[256,512]{1,0:T(8,128)(2,1)S(1)}, u32[]{:S(2)}, u32[]{:S(2)}) collective-permute-start(bf16[256,512]{1,0:T(8,128)(2,1)S(1)} %get-tuple-element.71.refs_4_), channel_id=1, source_target_pairs={{0,4},{4,0},{1,5},{5,1},{2,6},{6,2},{3,7},{7,3},{8,12},{12,8},{9,1... | collective-permute-start | bytes 786440 | tf_op jit(solution)/shard_map/ppermute | solution.py:59
  59.0 12.5 %collective-permute-start.22 = (bf16[256,512]{1,0:T(8,128)(2,1)S(1)}, bf16[256,512]{1,0:T(8,128)(2,1)S(1)}, u32[]{:S(2)}, u32[]{:S(2)}) collective-permute-start(bf16[256,512]{1,0:T(8,128)(2,1)S(1)} %collective-permute-done.12.refs_5_), channel_id=1, source_target_pairs={{0,4},{4,0},{1,5},{5,1},{2,6},{6,2},{3,7},{7,3},{8,12},{12,8},{9,1... | collective-permute-start | bytes 786440 | tf_op jit(solution)/shard_map/ppermute | solution.py:59
  59.7 11.9 %collective-permute-start.23 = (bf16[256,512]{1,0:T(8,128)(2,1)S(1)}, bf16[256,512]{1,0:T(8,128)(2,1)S(1)}, u32[]{:S(2)}, u32[]{:S(2)}) collective-permute-start(bf16[256,512]{1,0:T(8,128)(2,1)S(1)} %collective-permute-done.13.refs_6_), channel_id=1, source_target_pairs={{0,4},{4,0},{1,5},{5,1},{2,6},{6,2},{3,7},{7,3},{8,12},{12,8},{9,1... | collective-permute-start | bytes 786440 | tf_op jit(solution)/shard_map/ppermute | solution.py:59
  59.8 11.7 %collective-permute-start.24 = (bf16[256,512]{1,0:T(8,128)(2,1)S(1)}, bf16[256,512]{1,0:T(8,128)(2,1)S(1)}, u32[]{:S(2)}, u32[]{:S(2)}) collective-permute-start(bf16[256,512]{1,0:T(8,128)(2,1)S(1)} %collective-permute-done.14.refs_7_), channel_id=1, source_target_pairs={{0,4},{4,0},{1,5},{5,1},{2,6},{6,2},{3,7},{7,3},{8,12},{12,8},{9,1... | collective-permute-start | bytes 786440 | tf_op jit(solution)/shard_map/ppermute | solution.py:59
  60.2 1.6 %collective-permute-start.20 = (bf16[144,512]{1,0:T(8,128)(2,1)S(1)}, bf16[144,512]{1,0:T(8,128)(2,1)S(1)}, u32[]{:S(2)}, u32[]{:S(2)}) collective-permute-start(bf16[144,512]{1,0:T(8,128)(2,1)S(1)} %collective-permute-done.8.refs_3_), channel_id=1, source_target_pairs={{0,4},{4,0},{1,5},{5,1},{2,6},{6,2},{3,7},{7,3},{8,12},{12,8},{9,1... | collective-permute-start | bytes 442376 | tf_op jit(solution)/shard_map/ppermute | solution.py:59
  61.8 19.0 %copy-start.3 = (f32[512,1024]{1,0:T(8,128)S(1)}, f32[512,1024]{1,0:T(8,128)}, u32[]{:S(2)}) copy-start(f32[512,1024]{1,0:T(8,128)} %get-tuple-element.45) | copy-start | bytes 6291460
  61.8 19.0 %copy-start.4 = (f32[512,1024]{1,0:T(8,128)S(1)}, f32[512,1024]{1,0:T(8,128)}, u32[]{:S(2)}) copy-start(f32[512,1024]{1,0:T(8,128)} %get-tuple-element.46) | copy-start | bytes 6291460
  61.8 19.0 %collective-permute-start.17 = (f32[2,1024]{1,0:T(2,128)S(1)}, f32[2,1024]{1,0:T(2,128)S(1)}, u32[]{:S(2)}, u32[]{:S(2)}) collective-permute-start(f32[2,1024]{1,0:T(2,128)S(1)} %get-tuple-element.67), channel_id=1, source_target_pairs={{0,240},{4,244},{8,248},{12,252},{1,241},{5,245},{9,249},{13,253},... | collective-permute-start | bytes 24584 | tf_op jit(solution)/shard_map/ppermute | solution.py:44
  65.4 15.4 %collective-permute-start.16 = (f32[2,1024]{1,0:T(2,128)S(1)}, f32[2,1024]{1,0:T(2,128)S(1)}, u32[]{:S(2)}, u32[]{:S(2)}) collective-permute-start(f32[2,1024]{1,0:T(2,128)S(1)} %get-tuple-element.67), channel_id=1, source_target_pairs={{0,120},{4,124},{8,128},{12,132},{16,136},{20,140},{24,144},{28,14... | collective-permute-start | bytes 24584 | tf_op jit(solution)/shard_map/ppermute | solution.py:44
